TPU v7x, 32 devices: a whole 2x2x4 slice. The times are simulated.
32 devices in a mesh: seq: 4 (over y, core), head: 8 (over z, x).
Axes of the slice: x: 2, y: 2, z: 4, core: 2. Of those that a mesh axis runs over, the one named last changes fastest.
Arguments:
- inputs: bfloat16 [4096, 3, 2048], P(('seq', 'head')), may hold values from -6 to 6
- attn_gain: float32 [2048], replicated, may hold values from 0.25 to 1.75
- w_query: bfloat16 [2048, 256], P(None, 'head'), may hold values from -0.125 to 0.125
- w_key: bfloat16 [2048, 256], P(None, 'head'), may hold values from -0.125 to 0.125
- w_value: bfloat16 [2048, 2048], P(None, 'head'), may hold values from -0.125 to 0.125
- w_out: bfloat16 [2048, 2048], P('head'), may hold values from -1.5 to 1.5
- out_bias: float32 [2048], replicated, may hold values from -1.5 to 1.5
- mlp_gain: float32 [2048], replicated, may hold values from 0.25 to 1.75
- gate_weight: bfloat16 [2048, 5504], P(None, 'head'), may hold values from -0.125 to 0.125
- up_weight: bfloat16 [2048, 5504], P(None, 'head'), may hold values from -0.125 to 0.125
- down_weight: bfloat16 [5504, 2048], P('head'), may hold values from -0.078125 to 0.078125
- cotangent: bfloat16 [4096, 3, 2048], P(('seq', 'head')), may hold values from -6 to 6
- doc_lengths: int32 [3, 8], replicated, may hold values from 1 to 1536, 4096 in all within a row
Outputs:
- output: bfloat16 [4096, 3, 2048], P(('seq', 'head'))
- input_grad: bfloat16 [4096, 3, 2048], P(('seq', 'head'))
- attn_gain_grad: float32 [2048], P(('seq', 'head'))
- w_query_grad: float32 [2048, 256], P('seq', 'head')
- w_key_grad: float32 [2048, 256], P('seq', 'head')
- w_value_grad: float32 [2048, 2048], P('seq', 'head')
- w_out_grad: float32 [2048, 2048], P('head', 'seq')
- out_bias_grad: float32 [2048], P(('seq', 'head'))
- mlp_gain_grad: float32 [2048], P(('seq', 'head'))
- w_gate_grad: float32 [2048, 5504], P('seq', 'head')
- w_up_grad: float32 [2048, 5504], P('seq', 'head')
- w_down_grad: float32 [5504, 2048], P('head', 'seq')
Inputs may be any that keep to these rules, and one draw needn't show every extreme that they name: `doc_lengths`: in each row the 8 lengths sum to 4096 and the longest is exactly 1536.
All inputs are finite; a program needn't handle non-finite values.
Results may differ from a plain program's by a relative error of at most 0.02.
Values may be sent and summed in bfloat16 or wider, within the bound.
A program may use at most 320 MiB of HBM per device.

v0:
```python
import jax
import jax.numpy as jnp
from jax import lax
from jax.sharding import PartitionSpec as P

FEAT = 16


epsilon = 1e-05
root_half = 0.7071067811865476
exact_precision_flag = lax.Precision.HIGHEST


def entering(array, axis, join, neutral, backward):
    count = lax.axis_size(axis)
    place = lax.axis_index(axis)
    ahead = count - 1 - place if backward else place
    gathered = jax.tree.map(
        lambda a, kind: lax.all_gather(a.astype(kind), axis),
        array,
        (jnp.bfloat16, jnp.bfloat16, jnp.bfloat16),
    )
    state = jax.tree.map(lambda a, e: jnp.zeros_like(a) + jnp.asarray(e, a.dtype), array, neutral)

    def one(step, state):
        source = count - 1 - step if backward else step
        return join(
            state,
            jax.tree.map(
                lambda a, own: lax.dynamic_index_in_dim(a, source, 0, False).astype(own.dtype),
                gathered,
                array,
            ),
        )

    return lax.fori_loop(0, ahead, one, state)


def features(inputs):
    halved = inputs * 0.5
    size_in = inputs.shape[-1]
    squares = (halved[..., :, None] * halved[..., None, :]).reshape(
        inputs.shape[:-1] + (size_in * size_in,)
    ) * root_half
    return jnp.concatenate(
        [jnp.ones(inputs.shape[:-1] + (1,), inputs.dtype), halved, squares], axis=-1
    )


def doc_layout(doc_lengths, group_begin, group_len):
    doc_ends = jnp.cumsum(doc_lengths, axis=-1)
    positions = group_begin + jnp.arange(group_len, dtype=jnp.int32)
    passed = (doc_ends[..., :, None] <= positions).astype(jnp.int32)
    doc_index = jnp.sum(passed, axis=-2)
    doc_begin = jnp.sum(passed * doc_lengths[..., :, None], axis=-2)
    return (doc_index, doc_begin)


def chain_join(earlier, later):
    keep_prev = 1.0 - later[2]
    return (
        later[0] + keep_prev[:, None, None, None] * earlier[0],
        later[1] + keep_prev[:, None, None] * earlier[1],
        jnp.maximum(earlier[2], later[2]),
    )


def rms_scale(values_in):
    return lax.rsqrt(jnp.mean(values_in * values_in, axis=-1, keepdims=True) + epsilon)


def on_device(
    inputs,
    attn_gain,
    w_query,
    w_key,
    w_value,
    w_out,
    out_bias,
    mlp_gain,
    gate_weight,
    up_weight,
    down_weight,
    cotangent,
    doc_lengths,
):
    shard_len = inputs.shape[0]
    batch_rows = inputs.shape[1]
    head_local = w_query.shape[1] // FEAT
    value_dim = w_value.shape[1] // head_local
    group_len = shard_len * lax.axis_size("head")
    group_begin = lax.axis_index("seq") * group_len
    x_float = inputs.astype(jnp.float32)
    scale_one = rms_scale(x_float)
    normed_one = x_float * scale_one
    normed_low = (normed_one * attn_gain).astype(jnp.bfloat16)
    normed_full = lax.all_gather(normed_low, "head", axis=0, tiled=True)
    query_low = (
        jnp.einsum("trd,dc->trc", normed_full, w_query, preferred_element_type=jnp.float32)
        .astype(jnp.bfloat16)
        .reshape(group_len, batch_rows, head_local, FEAT)
    )
    key_low = (
        jnp.einsum("trd,dc->trc", normed_full, w_key, preferred_element_type=jnp.float32)
        .astype(jnp.bfloat16)
        .reshape(group_len, batch_rows, head_local, FEAT)
    )
    value_low = (
        jnp.einsum("trd,dc->trc", normed_full, w_value, preferred_element_type=jnp.float32)
        .astype(jnp.bfloat16)
        .reshape(group_len, batch_rows, head_local, value_dim)
    )
    doc_index, doc_begin = doc_layout(doc_lengths, group_begin, group_len)
    carried = (doc_begin < group_begin).astype(jnp.float32).T
    trailing = (doc_index == doc_index[:, -1:]).astype(jnp.float32).T
    restart = (doc_begin[:, -1] >= group_begin).astype(jnp.float32)
    positions = jnp.arange(group_len, dtype=jnp.int32)
    visible = (
        (positions[None, :] <= positions[:, None])[None]
        & (doc_index[:, :, None] == doc_index[:, None, :])
    )[:, None]
    scores = (
        jnp.einsum("trhf,urhf->rhtu", query_low, key_low, preferred_element_type=jnp.float32) * 0.25
    )
    weights_low = jnp.where(visible, 1.0 + scores + 0.5 * scores * scores, 0.0).astype(jnp.bfloat16)
    query_float = query_low.astype(jnp.float32)
    key_float = key_low.astype(jnp.float32)
    query_feat = features(query_float).astype(jnp.bfloat16)
    key_feat = features(key_float).astype(jnp.bfloat16)
    trail_low = trailing.astype(jnp.bfloat16)[:, :, None, None]
    local_state = jnp.einsum(
        "trhf,trhv->rhfv", key_feat, value_low * trail_low, preferred_element_type=jnp.float32
    )
    local_sum = jnp.sum(key_feat.astype(jnp.float32) * trailing[:, :, None, None], axis=0)
    empty_chain = (jnp.zeros_like(local_state), jnp.zeros_like(local_sum), jnp.zeros_like(restart))
    state_in, sum_in, _ = entering(
        (local_state, local_sum, restart), "seq", chain_join, empty_chain, False
    )
    state_low = state_in.astype(jnp.bfloat16)
    numerator = jnp.einsum(
        "rhtu,urhv->trhv", weights_low, value_low, preferred_element_type=jnp.float32
    )
    numerator = numerator + carried[:, :, None, None] * jnp.einsum(
        "trhf,rhfv->trhv", query_feat, state_low, preferred_element_type=jnp.float32
    )
    query_feat_float = query_feat.astype(jnp.float32)
    denominator = jnp.transpose(jnp.sum(weights_low, axis=-1, dtype=jnp.float32), (2, 0, 1))
    denominator = denominator + carried[:, :, None] * jnp.einsum(
        "trhf,rhf->trh", query_feat_float, sum_in, precision=exact_precision_flag
    )
    attended = (
        (numerator / denominator[..., None])
        .astype(jnp.bfloat16)
        .reshape(group_len, batch_rows, head_local * value_dim)
    )
    row_segment = attended
    attn_branch = lax.psum_scatter(
        jnp.einsum("trc,cd->trd", row_segment, w_out, preferred_element_type=jnp.float32),
        "head",
        scatter_dimension=0,
        tiled=True,
    )
    middle = x_float + attn_branch + out_bias
    scale_two = rms_scale(middle)
    second_normed = middle * scale_two
    normed_two_low = (second_normed * mlp_gain).astype(jnp.bfloat16)

    def projections(row_segment):
        gate_segment = jnp.einsum(
            "czm,my->czy", row_segment, gate_weight, preferred_element_type=jnp.float32
        )
        up_segment = jnp.einsum(
            "czm,my->czy", row_segment, up_weight, preferred_element_type=jnp.float32
        )
        return (gate_segment, up_segment)

    gate_segment, up_segment = projections(
        lax.all_gather(normed_two_low, "head", axis=0, tiled=True)
    )
    hidden_activation = (jax.nn.silu(gate_segment) * up_segment).astype(jnp.bfloat16)
    row_segment = hidden_activation
    perceptron_branch = lax.psum_scatter(
        jnp.einsum(
            "nzh,hi->nzi", row_segment, down_weight, preferred_element_type=jnp.float32
        ).astype(jnp.bfloat16),
        "head",
        scatter_dimension=0,
        tiled=True,
    ).astype(jnp.float32)
    output = (middle + perceptron_branch).astype(jnp.bfloat16)
    second_normed_complete, gradient_complete = (
        lax.all_gather(normed_two_low, "head", axis=0, tiled=True),
        lax.all_gather(cotangent, "head", axis=0, tiled=True),
    )
    gate_projected, up_projected = projections(second_normed_complete)
    down_weight_gradient = jnp.einsum(
        "ebn,eby->ny", hidden_activation, gradient_complete, preferred_element_type=jnp.float32
    )
    hidden_gradient = jnp.einsum(
        "bje,ke->bjk", gradient_complete, down_weight, preferred_element_type=jnp.float32
    )
    sigmoid_gate = jax.nn.sigmoid(gate_projected)
    gate_gradient = (
        hidden_gradient
        * up_projected
        * sigmoid_gate
        * (1.0 + gate_projected * (1.0 - sigmoid_gate))
    ).astype(jnp.bfloat16)
    up_gradient = (hidden_gradient * gate_projected * sigmoid_gate).astype(jnp.bfloat16)
    grad_w_gate = jnp.einsum(
        "ego,egv->ov", second_normed_complete, gate_gradient, preferred_element_type=jnp.float32
    )
    grad_w_up = jnp.einsum(
        "ego,egv->ov", second_normed_complete, up_gradient, preferred_element_type=jnp.float32
    )
    grad_normed_two = lax.psum_scatter(
        (
            jnp.einsum(
                "szq,hq->szh", gate_gradient, gate_weight, preferred_element_type=jnp.float32
            )
            + jnp.einsum("szq,hq->szh", up_gradient, up_weight, preferred_element_type=jnp.float32)
        ).astype(jnp.bfloat16),
        "head",
        scatter_dimension=0,
        tiled=True,
    ).astype(jnp.float32)
    gain_two_part = jnp.sum(grad_normed_two * second_normed, axis=(0, 1))
    grad_scaled_two = grad_normed_two * mlp_gain
    grad_middle = cotangent.astype(jnp.float32) + scale_two * (
        grad_scaled_two
        - second_normed * jnp.mean(grad_scaled_two * second_normed, axis=-1, keepdims=True)
    )
    bias_part = jnp.sum(grad_middle, axis=(0, 1))
    grad_branch = lax.all_gather(grad_middle.astype(jnp.bfloat16), "head", axis=0, tiled=True)
    grad_w_out = jnp.einsum(
        "trc,trd->cd", attended, grad_branch, preferred_element_type=jnp.float32
    )
    grad_attended = jnp.einsum(
        "trd,cd->trc", grad_branch, w_out, preferred_element_type=jnp.float32
    ).reshape(group_len, batch_rows, head_local, value_dim)
    grad_numer = (grad_attended / denominator[..., None]).astype(jnp.bfloat16)
    grad_denom = -jnp.sum(grad_attended * numerator, axis=-1) / (denominator * denominator)
    grad_weights = (
        jnp.einsum("trhv,urhv->rhtu", grad_numer, value_low, preferred_element_type=jnp.float32)
        + jnp.transpose(grad_denom, (1, 2, 0))[..., None]
    )
    grad_scores = jnp.where(visible, grad_weights * (1.0 + scores), 0.0).astype(jnp.bfloat16)
    grad_query = (
        jnp.einsum("rhtu,urhf->trhf", grad_scores, key_low, preferred_element_type=jnp.float32)
        * 0.25
    )
    grad_key = (
        jnp.einsum("rhtu,trhf->urhf", grad_scores, query_low, preferred_element_type=jnp.float32)
        * 0.25
    )
    grad_value = jnp.einsum(
        "rhtu,trhv->urhv", weights_low, grad_numer, preferred_element_type=jnp.float32
    )
    carry_low = carried.astype(jnp.bfloat16)[:, :, None, None]
    grad_state_in = jnp.einsum(
        "trhf,trhv->rhfv", query_feat, grad_numer * carry_low, preferred_element_type=jnp.float32
    )
    grad_sum_in = jnp.einsum(
        "trhf,trh->rhf",
        query_feat_float,
        carried[:, :, None] * grad_denom,
        precision=exact_precision_flag,
    )
    grad_query_feat = carried[:, :, None, None] * (
        jnp.einsum("trhv,rhfv->trhf", grad_numer, state_low, preferred_element_type=jnp.float32)
        + grad_denom[..., None] * sum_in[None]
    )
    empty_grads = (
        jnp.zeros_like(grad_state_in),
        jnp.zeros_like(grad_sum_in),
        jnp.zeros_like(restart),
    )
    grad_state_out, grad_sum_out, _ = entering(
        (grad_state_in, grad_sum_in, restart), "seq", chain_join, empty_grads, True
    )
    grad_state_low = grad_state_out.astype(jnp.bfloat16)
    grad_key_feat = trailing[:, :, None, None] * (
        jnp.einsum("trhv,rhfv->trhf", value_low, grad_state_low, preferred_element_type=jnp.float32)
        + grad_sum_out[None]
    )
    grad_value = grad_value + trailing[:, :, None, None] * jnp.einsum(
        "trhf,rhfv->trhv", key_feat, grad_state_low, preferred_element_type=jnp.float32
    )
    _, query_map_back = jax.vjp(features, query_float)
    _, key_map_back = jax.vjp(features, key_float)
    grad_query = grad_query + query_map_back(grad_query_feat)[0]
    grad_key = grad_key + key_map_back(grad_key_feat)[0]
    grad_query_low = grad_query.astype(jnp.bfloat16).reshape(
        group_len, batch_rows, head_local * FEAT
    )
    grad_key_low = grad_key.astype(jnp.bfloat16).reshape(group_len, batch_rows, head_local * FEAT)
    grad_value_low = grad_value.astype(jnp.bfloat16).reshape(
        group_len, batch_rows, head_local * value_dim
    )
    grad_w_query = jnp.einsum(
        "trd,trc->dc", normed_full, grad_query_low, preferred_element_type=jnp.float32
    )
    grad_w_key = jnp.einsum(
        "trd,trc->dc", normed_full, grad_key_low, preferred_element_type=jnp.float32
    )
    grad_w_value = jnp.einsum(
        "trd,trc->dc", normed_full, grad_value_low, preferred_element_type=jnp.float32
    )
    summed = jnp.einsum("trc,dc->trd", grad_query_low, w_query, preferred_element_type=jnp.float32)
    summed = summed + jnp.einsum(
        "trc,dc->trd", grad_key_low, w_key, preferred_element_type=jnp.float32
    )
    grad_normed_one = lax.psum_scatter(
        (
            summed
            + jnp.einsum("trc,dc->trd", grad_value_low, w_value, preferred_element_type=jnp.float32)
        ).astype(jnp.bfloat16),
        "head",
        scatter_dimension=0,
        tiled=True,
    ).astype(jnp.float32)
    gain_one_part = jnp.sum(grad_normed_one * normed_one, axis=(0, 1))
    grad_scaled_one = grad_normed_one * attn_gain
    input_grad = (
        grad_middle
        + scale_one
        * (
            grad_scaled_one
            - normed_one * jnp.mean(grad_scaled_one * normed_one, axis=-1, keepdims=True)
        )
    ).astype(jnp.bfloat16)
    gain_one, bias_grad, gain_two = (
        lax.psum_scatter(gain_one_part, ("seq", "head"), scatter_dimension=0, tiled=True),
        lax.psum_scatter(bias_part, ("seq", "head"), scatter_dimension=0, tiled=True),
        lax.psum_scatter(gain_two_part, ("seq", "head"), scatter_dimension=0, tiled=True),
    )
    summed_query, summed_key, summed_value, summed_out, summed_gate, summed_up, summed_down = (
        lax.psum_scatter(
            grad_w_query.astype(jnp.bfloat16), "seq", scatter_dimension=0, tiled=True
        ).astype(jnp.float32),
        lax.psum_scatter(
            grad_w_key.astype(jnp.bfloat16), "seq", scatter_dimension=0, tiled=True
        ).astype(jnp.float32),
        lax.psum_scatter(
            grad_w_value.astype(jnp.bfloat16), "seq", scatter_dimension=0, tiled=True
        ).astype(jnp.float32),
        lax.psum_scatter(
            grad_w_out.astype(jnp.bfloat16), "seq", scatter_dimension=1, tiled=True
        ).astype(jnp.float32),
        lax.psum_scatter(
            grad_w_gate.astype(jnp.bfloat16), "seq", scatter_dimension=0, tiled=True
        ).astype(jnp.float32),
        lax.psum_scatter(
            grad_w_up.astype(jnp.bfloat16), "seq", scatter_dimension=0, tiled=True
        ).astype(jnp.float32),
        lax.psum_scatter(
            down_weight_gradient.astype(jnp.bfloat16), "seq", scatter_dimension=1, tiled=True
        ).astype(jnp.float32),
    )
    return (
        output,
        input_grad,
        gain_one,
        summed_query,
        summed_key,
        summed_value,
        summed_out,
        bias_grad,
        gain_two,
        summed_gate,
        summed_up,
        summed_down,
    )


def solution(mesh):
    placed = (
        P(("seq", "head"), None, None),
        P(),
        P(None, "head"),
        P(None, "head"),
        P(None, "head"),
        P("head", None),
        P(),
        P(),
        P(None, "head"),
        P(None, "head"),
        P("head", None),
        P(("seq", "head"), None, None),
        P(),
    )
    return jax.shard_map(
        on_device,
        mesh=mesh,
        in_specs=placed,
        out_specs=(
            P(("seq", "head"), None, None),
            P(("seq", "head"), None, None),
            P(("seq", "head")),
            P("seq", "head"),
            P("seq", "head"),
            P("seq", "head"),
            P("head", "seq"),
            P(("seq", "head")),
            P(("seq", "head")),
            P("seq", "head"),
            P("seq", "head"),
            P("head", "seq"),
        ),
        check_vma=False,
    )
```

profile of v0, /device:TPU:0, one launch (start us, length us, event | category | flops | bytes accessed | tf_op | source)
XLA Modules:
  0.0 2234.3 jit_solution(17653696838373602096)
XLA Ops:
  14.8 8.3 all-reduce
  28.0 164.0 %all-gather.12.cloned.1.call-done = bf16[1024,3,2048]{2,0,1:T(8,128)(2,1)} async-done(((bf16[128,3,2048]{2,0,1:T(8,128)(2,1)}), bf16[1024,3,2048]{2,0,1:T(8,128)(2,1)}) %all-gather.12.cloned.1.call-update) | async-done | bytes 12582928 | tf_op jit(solution)/shard_map/all_gather | solution.py:97
  192.1 8.6 convolution_convert_fusion.3
  206.8 14.2 convolution_convert_fusion.1
  241.7 15.4 convert_reduce_fusion
  277.5 10.1 fusion.61
  287.7 412.3 %reduce-scatter.12.cloned.1.call-done = f32[128,3,2048]{2,0,1:T(8,128)} async-done(((f32[1024,3,2048]{2,0,1:T(8,128)}), f32[128,3,2048]{2,0,1:T(8,128)}) %reduce-scatter.12.cloned.1.call-update) | async-done | bytes 3145744 | tf_op jit(solution)/shard_map/reduce_scatter | solution.py:157
  707.0 174.9 %all-gather.14.cloned.1.call-done = bf16[1024,3,2048]{2,0,1:T(8,128)(2,1)} async-done(((bf16[128,3,2048]{2,0,1:T(8,128)(2,1)}), bf16[1024,3,2048]{2,0,1:T(8,128)(2,1)}) %all-gather.14.cloned.1.call-update) | async-done | bytes 12582928 | tf_op jit(solution)/shard_map/all_gather | solution.py:178
  881.9 15.0 fusion.33
  896.8 11.2 fusion.37
  908.1 150.5 %all-gather.16.cloned.1.call-done = bf16[1024,3,2048]{2,0,1:T(8,128)(2,1)} async-done(((bf16[128,3,2048]{2,0,1:T(8,128)(2,1)}), bf16[1024,3,2048]{2,0,1:T(8,128)(2,1)}) %all-gather.16.cloned.1.call-update) | async-done | bytes 12582928 | tf_op jit(solution)/shard_map/all_gather | solution.py:193
  1058.5 22.0 multiply_convert_fusion
  1080.6 17.3 fusion.35
  1097.9 18.9 add_convert_fusion.1
  1116.9 15.2 convolution_convert_fusion
  1132.2 190.8 %reduce-scatter.16.cloned.1.call-done = bf16[128,3,2048]{2,0,1:T(8,128)(2,1)} async-done(((bf16[1024,3,2048]{2,0,1:T(8,128)(2,1)}), bf16[128,3,2048]{2,0,1:T(8,128)(2,1)}) %reduce-scatter.16.cloned.1.call-update) | async-done | bytes 1572880 | tf_op jit(solution)/shard_map/reduce_scatter | solution.py:216
  1327.0 206.5 %reduce-scatter.14.cloned.1.call-done = bf16[128,3,2048]{2,0,1:T(8,128)(2,1)} async-done(((bf16[1024,3,2048]{2,0,1:T(8,128)(2,1)}), bf16[128,3,2048]{2,0,1:T(8,128)(2,1)}) %reduce-scatter.14.cloned.1.call-update) | async-done | bytes 1572880 | tf_op jit(solution)/shard_map/reduce_scatter | solution.py:182
  1542.5 175.6 %all-gather.18.cloned.1.call-done = bf16[1024,3,2048]{2,0,1:T(8,128)(2,1)} async-done(((bf16[128,3,2048]{2,0,1:T(8,128)(2,1)}), bf16[1024,3,2048]{2,0,1:T(8,128)(2,1)}) %all-gather.18.cloned.1.call-update) | async-done | bytes 12582928 | tf_op jit(solution)/shard_map/all_gather | solution.py:234
  1718.2 9.0 multiply_reduce_fusion.5
  1732.1 14.5 bitcast_convert_fusion
  1746.7 14.4 bitcast_convert_fusion.1
  1761.1 14.6 bitcast_convert_fusion.2
  1783.6 17.5 select_convert_fusion
  1810.6 10.3 fusion.78
  1820.9 10.6 fusion.98
  1831.7 9.9 fusion.40
  1870.5 8.2 fusion.58
  1881.7 10.4 fusion.63
  1900.1 22.1 add_convert_fusion
  1939.7 26.5 %reduce-scatter.24.cloned.1.call-done = bf16[512,256]{1,0:T(8,128)(2,1)} async-done(((bf16[2048,256]{1,0:T(8,128)(2,1)}), bf16[512,256]{1,0:T(8,128)(2,1)}) %reduce-scatter.24.cloned.1.call-update) | async-done | bytes 262160 | tf_op jit(solution)/shard_map/reduce_scatter | solution.py:344
  1968.0 209.8 %reduce-scatter.18.cloned.1.call-done = bf16[128,3,2048]{2,0,1:T(8,128)(2,1)} async-done(((bf16[1024,3,2048]{2,0,1:T(8,128)(2,1)}), bf16[128,3,2048]{2,0,1:T(8,128)(2,1)}) %reduce-scatter.18.cloned.1.call-update) | async-done | bytes 1572880 | tf_op jit(solution)/shard_map/reduce_scatter | solution.py:313
  2181.0 39.7 %all-reduce.4 = (f32[2048]{0:T(1024)S(1)}, f32[2048]{0:T(1024)S(1)}, f32[2048]{0:T(1024)S(1)}) all-reduce(f32[2048]{0:T(1024)S(1)} %get-tuple-element.232, f32[2048]{0:T(1024)S(1)} %copy-done.57, f32[2048]{0:T(1024)S(1)} %copy-done.56), channel_id=11, replica_groups=mesh['seq'=4,'head'=8] {'seq','head'}, use_global_device_ids=true, to_apply=%region_23.24.clone | all-reduce | flops 6144 | bytes 49152
  (284 shorter events, 174.9 us)
Async XLA Ops:
  7.2 1051.4 %copy-start = (bf16[688,2048]{1,0:T(8,128)(2,1)S(1)}, bf16[688,2048]{1,0:T(8,128)(2,1)}, u32[]{:S(2)}) copy-start(bf16[688,2048]{1,0:T(8,128)(2,1)} %param.27) | copy-start | bytes 8454148
  7.2 184.8 %all-gather.12.cloned.1.call-start = ((), (), s32[]{:S(2)}) async-start(), calls=%async_computation.11 | async-start | bytes 14155776 | tf_op jit(solution)/shard_map/all_gather | solution.py:97
  12.7 179.3 %copy-start.38 = (bf16[2048,32]{0,1:T(8,128)(2,1)S(1)}, bf16[2048,32]{0,1:T(8,128)(2,1)}, u32[]{:S(2)}) copy-start(bf16[2048,32]{0,1:T(8,128)(2,1)} %param.19) | copy-start | bytes 393220
  12.8 252.4 %all-gather.20.cloned.1.call-start = ((), (), s32[]{:S(2)}) async-start(), calls=%async_computation.26 | async-start | bytes 2096640 | tf_op jit(solution)/shard_map/all_gather | solution.py:19
  23.3 248.3 %copy-start.63 = (bf16[273]{0:T(512)(128)(2,1)}, bf16[273]{0:T(512)(128)(2,1)S(1)}, u32[]{:S(2)}) copy-start(bf16[273]{0:T(512)(128)(2,1)S(1)} %pad.3.clone) | copy-start | bytes 1642
  24.4 247.2 %copy-start.35 = (f32[3,1024]{1,0:T(4,128)}, f32[3,1024]{1,0:T(4,128)S(1)}, u32[]{:S(2)}) copy-start(f32[3,1024]{1,0:T(4,128)S(1)} %get-tuple-element.276) | copy-start | bytes 36868
  24.5 205.6 %copy-start.44 = (f32[1024,3]{0,1:T(4,128)}, f32[1024,3]{0,1:T(4,128)S(1)}, u32[]{:S(2)}) copy-start(f32[1024,3]{0,1:T(4,128)S(1)} %get-tuple-element.282) | copy-start | bytes 36868
  28.0 173.5 %copy-start.40 = (bf16[2048,32]{0,1:T(8,128)(2,1)S(1)}, bf16[2048,32]{0,1:T(8,128)(2,1)}, u32[]{:S(2)}) copy-start(bf16[2048,32]{0,1:T(8,128)(2,1)} %param.20) | copy-start | bytes 393220
  230.0 470.0 %reduce-scatter.12.cloned.1.call-start = ((), (), s32[]{:S(2)}) async-start(), calls=%async_computation.12 | async-start | bytes 28311552 | tf_op jit(solution)/shard_map/reduce_scatter | solution.py:157
  287.6 412.4 %copy-start.60 = (f32[2048]{0:T(1024)S(1)}, f32[2048]{0:T(1024)}, u32[]{:S(2)}) copy-start(f32[2048]{0:T(1024)} %param.23) | copy-start | bytes 24580
  287.6 417.1 %copy-start.54 = (f32[2048]{0:T(1024)S(1)}, f32[2048]{0:T(1024)}, u32[]{:S(2)}) copy-start(f32[2048]{0:T(1024)} %param.24) | copy-start | bytes 24580
  287.6 594.2 %all-gather.14.cloned.1.call-start = ((), (), s32[]{:S(2)}) async-start(), calls=%async_computation.13 | async-start | bytes 14155776 | tf_op jit(solution)/shard_map/all_gather | solution.py:178
  706.1 352.4 %all-gather.16.cloned.1.call-start = ((), (), s32[]{:S(2)}) async-start(), calls=%async_computation.15 | async-start | bytes 14155776 | tf_op jit(solution)/shard_map/all_gather | solution.py:193
  706.7 616.2 %reduce-scatter.16.cloned.1.call-start = ((), (), s32[]{:S(2)}) async-start(), calls=%async_computation.16 | async-start | bytes 14155776 | tf_op jit(solution)/shard_map/reduce_scatter | solution.py:216
  1116.8 416.6 %reduce-scatter.14.cloned.1.call-start = ((), (), s32[]{:S(2)}) async-start(), calls=%async_computation.14 | async-start | bytes 14155776 | tf_op jit(solution)/shard_map/reduce_scatter | solution.py:182
  1132.1 401.3 %copy-start.20 = (bf16[128,3,2048]{2,0,1:T(8,128)(2,1)S(1)}, bf16[128,3,2048]{2,0,1:T(8,128)(2,1)}, u32[]{:S(2)}) copy-start(bf16[128,3,2048]{2,0,1:T(8,128)(2,1)} %param.28) | copy-start | bytes 4718596
  1132.1 586.0 %all-gather.18.cloned.1.call-start = ((), (), s32[]{:S(2)}) async-start(), calls=%async_computation.17 | async-start | bytes 14155776 | tf_op jit(solution)/shard_map/all_gather | solution.py:234
  1539.4 178.7 %copy-start.32 = (bf16[256,2048]{1,0:T(8,128)(2,1)S(1)}, bf16[256,2048]{1,0:T(8,128)(2,1)}, u32[]{:S(2)}) copy-start(bf16[256,2048]{1,0:T(8,128)(2,1)} %param.22) | copy-start | bytes 3145732
  1542.5 309.3 %all-gather.22.cloned.1.call-start = ((), (), s32[]{:S(2)}) async-start(), calls=%async_computation.27 | async-start | bytes 2096640 | tf_op jit(solution)/shard_map/all_gather | solution.py:19
  1732.1 190.3 %reduce-scatter.32.cloned.1.call-start = ((), (), s32[]{:S(2)}) async-start(), calls=%async_computation.25 | async-start | bytes 3522560 | tf_op jit(solution)/shard_map/reduce_scatter | solution.py:356
  1746.6 178.1 %reduce-scatter.30.cloned.1.call-start = ((), (), s32[]{:S(2)}) async-start(), calls=%async_computation.24 | async-start | bytes 3522560 | tf_op jit(solution)/shard_map/reduce_scatter | solution.py:353
  1761.0 166.1 %reduce-scatter.28.cloned.1.call-start = ((), (), s32[]{:S(2)}) async-start(), calls=%async_computation.23 | async-start | bytes 3522560 | tf_op jit(solution)/shard_map/reduce_scatter | solution.py:350
  1775.8 153.7 %reduce-scatter.20.cloned.1.call-start = ((), (), s32[]{:S(2)}) async-start(), calls=%async_computation.19 | async-start | bytes 163840 | tf_op jit(solution)/shard_map/reduce_scatter | solution.py:338
  1831.5 99.5 %reduce-scatter.26.cloned.1.call-start = ((), (), s32[]{:S(2)}) async-start(), calls=%async_computation.22 | async-start | bytes 1310720 | tf_op jit(solution)/shard_map/reduce_scatter | solution.py:347
  1851.7 86.6 %reduce-scatter.22.cloned.1.call-start = ((), (), s32[]{:S(2)}) async-start(), calls=%async_computation.20 | async-start | bytes 163840 | tf_op jit(solution)/shard_map/reduce_scatter | solution.py:341
  1892.1 74.1 %reduce-scatter.24.cloned.1.call-start = ((), (), s32[]{:S(2)}) async-start(), calls=%async_computation.21 | async-start | bytes 1310720 | tf_op jit(solution)/shard_map/reduce_scatter | solution.py:344
  1900.1 277.7 %reduce-scatter.18.cloned.1.call-start = ((), (), s32[]{:S(2)}) async-start(), calls=%async_computation.18 | async-start | bytes 14155776 | tf_op jit(solution)/shard_map/reduce_scatter | solution.py:313
  1922.3 255.5 %copy-start.55 = (f32[2048]{0:T(1024)S(1)}, f32[2048]{0:T(1024)}, u32[]{:S(2)}) copy-start(f32[2048]{0:T(1024)} %param.18) | copy-start | bytes 24580
  1922.3 255.5 %copy-start.59 = (f32[128,3]{0,1:T(4,128)S(1)}, f32[128,3]{0,1:T(4,128)}, u32[]{:S(2)}) copy-start(f32[128,3]{0,1:T(4,128)} %copy-done.58) | copy-start | bytes 4612
  1924.7 256.2 %copy-start.56 = (f32[2048]{0:T(1024)S(1)}, f32[2048]{0:T(1024)}, u32[]{:S(2)}) copy-start(f32[2048]{0:T(1024)} %get-tuple-element.230) | copy-start | bytes 24580
  1924.7 256.2 %copy-start.57 = (f32[2048]{0:T(1024)S(1)}, f32[2048]{0:T(1024)}, u32[]{:S(2)}) copy-start(f32[2048]{0:T(1024)} %get-tuple-element.271) | copy-start | bytes 24580
  2177.8 49.5 %copy-start.1 = (bf16[688,2048]{1,0:T(8,128)(2,1)S(1)}, bf16[688,2048]{1,0:T(8,128)(2,1)}, u32[]{:S(2)}) copy-start(bf16[688,2048]{1,0:T(8,128)(2,1)} %param.27) | copy-start | bytes 8454148
  (61 other events, 569.3 us)
Sparse Core Ops, SparseCore 0:
  12.9 179.1 all-gather.11
  230.1 18.4 all-gather.19
  287.7 412.2 reduce-scatter.11
  706.3 175.5 all-gather.13
  883.9 174.6 all-gather.15
  1116.9 205.9 reduce-scatter.15
  1326.6 206.8 reduce-scatter.13
  1542.6 175.5 all-gather.17
  1732.2 18.4 all-gather.21
  1753.1 35.9 reduce-scatter.31
  1791.8 35.9 reduce-scatter.29
  1830.2 36.0 reduce-scatter.27
  1869.4 19.5 reduce-scatter.19
  1891.4 24.8 reduce-scatter.25
  1918.7 19.5 reduce-scatter.21
  1941.3 24.8 reduce-scatter.23
  1970.1 207.6 reduce-scatter.17
where the time goes:
time: 2240 us; the launch traced here: 2230 us
  waiting for transfers between devices  1720 us (77%)
  matrix products  349 us (16%)
  other arithmetic  66.9 us (3%)
  blocking collectives  58.4 us (3%)
  local copies, waits for them, and re-layouts  25.8 us (1%)
    reduce_scatter x1, waiting for transfers between devices, on_device(): lax.psum_scatter(jnp.einsum('trc,cd->trd', row_segment, w_out, preferred_...  412 us
    reduce_scatter x1, waiting for transfers between devices, on_device(): lax.psum_scatter((summed + jnp.einsum('trc,dc->trd', grad_value_low, w_va...  210 us
    reduce_scatter x1, waiting for transfers between devices, on_device(): lax.psum_scatter(jnp.einsum('nzh,hi->nzi', row_segment, down_weight, pref...  206 us
    reduce_scatter x1, waiting for transfers between devices, on_device(): lax.psum_scatter((jnp.einsum('szq,hq->szh', gate_gradient, gate_weight, p...  191 us
    all_gather x1, waiting for transfers between devices, on_device(): lax.all_gather(grad_middle.astype(jnp.bfloat16), 'head', axis=0, tiled=True)  176 us
    all_gather x1, waiting for transfers between devices, on_device(): lax.all_gather(normed_two_low, 'head', axis=0, tiled=True)  175 us
    all_gather x1, waiting for transfers between devices, on_device(): normed_full = lax.all_gather(normed_low, 'head', axis=0, tiled=True)  164 us
    all_gather x1, waiting for transfers between devices, on_device(): lax.all_gather(cotangent, 'head', axis=0, tiled=True)  150 us
  transfers between devices with their start and end apart: 17, of which 10 were waited for; matrix products, arithmetic and copies ran while one was open for 12% of the time, Pallas kernels for 0%

commit v1 on v0

v1 whole, which is shorter than its diff:
```python
import functools

import jax
import jax.numpy as jnp
import numpy as np
from jax import lax
from jax.experimental import pallas as pl
from jax.experimental.pallas import tpu as pltpu
from jax.sharding import Mesh
from jax.sharding import PartitionSpec as P

FEAT = 16
EPS = 1e-05
ROOT_HALF = 0.7071067811865476
TILE = 256
AUX = 136
BF = jnp.bfloat16
F32 = jnp.float32
MESH_ID = pl.DeviceIdType.MESH
NT = (((1,), (1,)), ((), ()))
TN = (((0,), (0,)), ((), ()))


def dot(a, b, dims=(((1,), (0,)), ((), ()))):
    return lax.dot_general(a, b, dims, preferred_element_type=F32)


def feature_tables(nh):
    cols = [(None, None)] + [(i, None) for i in range(FEAT)]
    cols += [(i, j) for i in range(FEAT) for j in range(i, FEAT)]
    pick_a = np.zeros((2 * nh, 128, TILE), np.float32)
    pick_b = np.zeros((2 * nh, 128, TILE), np.float32)
    rows = np.zeros((8, TILE), np.float32)
    for c, (i, j) in enumerate(cols):
        scale = 1.0 if i is None else 0.5 if j is None else 0.25 * ROOT_HALF
        rows[0, c] = 1.0 if i is None else 0.0
        rows[1, c] = 1.0 if j is None else 0.0
        rows[2, c] = scale * (2.0 if j is not None and i != j else 1.0)
        rows[3, c] = scale
        for n in range(2 * nh):
            if i is not None:
                pick_a[n, FEAT * n + i, c] = 1.0
            if j is not None:
                pick_b[n, FEAT * n + j, c] = 1.0
    align = np.zeros((4 * nh, 128, 128), np.float32)
    for h in range(nh):
        for f in range(FEAT):
            q, k = FEAT * h + f, FEAT * (nh + h) + f
            align[4 * h, q, f] = 0.25
            align[4 * h + 1, k, f] = 1.0
            align[4 * h + 2, k, q] = 0.25
            align[4 * h + 3, q, k] = 0.25
    to_low = lambda a: jnp.asarray(a, BF)
    return to_low(pick_a), to_low(pick_b), jnp.asarray(rows), to_low(align)


def begin_at(lens, row, docs, position, start_block):
    start = -start_block
    found = start + position * 0
    for j in range(docs):
        if j:
            start = start + lens[row, j - 1]
            found = jnp.where(start <= position, start, found)
    return found


def chain_weights(lens, row, docs, block, blocks, length, backward):
    out, alive = [], None
    for k in range(1, blocks):
        source = block + k if backward else block - k
        inside = (source < blocks) if backward else (source >= 0)
        here = inside if alive is None else jnp.logical_and(alive, inside)
        out.append(jnp.where(here, 1.0, 0.0).astype(F32))
        first = begin_at(lens, row, docs, length - 1, source * length)
        passes = first < 0
        alive = passes if alive is None else jnp.logical_and(alive, passes)
    return out


def lane_iota(shape):
    return lax.broadcasted_iota(jnp.int32, shape, len(shape) - 1)


def row_iota(shape):
    return lax.broadcasted_iota(jnp.int32, shape, len(shape) - 2)


def with_ones(v, lanes=(0, 1)):
    side = lane_iota(v.shape)
    ones = jnp.where((side >= lanes[0]) & (side <= lanes[1]), 1.0, 0.0).astype(BF)
    return jnp.concatenate([v, ones], axis=1)


def split_sum(state, total, third):
    rows = row_iota(state.shape)
    high = total.astype(BF).astype(F32)
    low = total - high
    out = jnp.where(rows < 128, state, 0.0)
    out = jnp.where(rows == 128, high, out)
    if third:
        out = jnp.where(rows == 129, high, out)
        out = jnp.where(rows == 130, low, out)
    else:
        out = jnp.where(rows == 129, low, out)
    return out.astype(BF)


def flat(ref):
    x = ref[...]
    return x.reshape(x.shape[0] * x.shape[2], x.shape[3])


def picks(qk, pa, pb, rows, n):
    a = dot(qk, pa[n]) + rows[0:1, :]
    b = dot(qk, pb[n]) + rows[1:2, :]
    return a, b


def state_kernel(nh, vd, docs, lens, meta, x_ref, pa, pb, rows, out):
    row = pl.program_id(0)
    x = flat(x_ref)
    length = x.shape[0]
    qk = x[:, nh * vd :]
    last = begin_at(lens, row, docs, length - 1, meta[0] * length)
    trail = row_iota((length, 2 * 128)) >= last
    for h in range(nh):
        a, b = picks(qk, pa, pb, rows, nh + h)
        kf = (a * b * rows[3:4, :]).astype(BF)
        va = jnp.where(trail, with_ones(x[:, h * vd : (h + 1) * vd]).astype(F32), 0.0).astype(BF)
        st = dot(va, kf, TN)[:AUX]
        out[0, h] = split_sum(st, st[128:129], False)


def intra_kernel(nh, vd, docs, lens, meta, x_ref, align, num_out, den_out):
    row = pl.program_id(0)
    x = flat(x_ref)
    length = x.shape[0]
    qk = x[:, nh * vd :]
    one16 = jnp.where(lane_iota((1, 128)) == FEAT, 1.0, 0.0)
    tile = min(TILE, length)
    dens = [jnp.zeros((tile, 128), F32) for _ in range(length // tile)]
    for h in range(nh):
        qa = (dot(qk, align[4 * h]) + one16).astype(BF)
        ka = (dot(qk, align[4 * h + 1]) + one16).astype(BF)
        va = with_ones(x[:, h * vd : (h + 1) * vd])
        for t in range(length // tile):
            lo, hi = t * tile, (t + 1) * tile
            s1 = dot(qa[lo:hi], ka[:hi], NT)
            w = 0.5 * (s1 * s1) + 0.5
            pos = lo + row_iota((tile, 1))
            beg = begin_at(lens, row, docs, pos, meta[0] * length)
            kpos = lane_iota(w.shape)
            w = jnp.where((kpos >= beg) & (kpos <= pos), w, 0.0).astype(BF)
            acc = dot(w, va[:hi])
            num_out[0, lo:hi, h * vd : (h + 1) * vd] = acc[:, :vd]
            lane = lane_iota((tile, 128))
            dens[t] = jnp.where(lane == h, acc[:, vd : vd + 1], dens[t])
    for t in range(length // tile):
        den_out[0, t * tile : (t + 1) * tile, :] = dens[t]


def gather_states(sts, weights, h):
    total = None
    for st, w in zip(sts, weights):
        part = st[0, h].astype(F32) * w
        total = part if total is None else total + part
    return total


def attend_kernel(nh, vd, docs, blocks, lens, meta, x_ref, num, den, pa, pb, rows, *rest):
    sts, (att_out, den_out, st_out) = rest[: blocks - 1], rest[blocks - 1 :]
    row = pl.program_id(0)
    x = flat(x_ref)
    length = x.shape[0]
    qk = x[:, nh * vd :]
    weights = chain_weights(lens, row, docs, meta[0], blocks, length, False)
    pos = row_iota((length, 1))
    carried = begin_at(lens, row, docs, pos, meta[0] * length) < 0
    lane = lane_iota((length, 128))
    dens = den[0]
    for h in range(nh):
        st = gather_states(sts, weights, h)
        st = split_sum(st, st[128:129] + st[129:130], True)
        st_out[0, h] = st
        a, b = picks(qk, pa, pb, rows, h)
        qf = (a * b * rows[2:3, :]).astype(BF)
        inter = dot(qf, st, NT)
        more = jnp.where(carried, inter[:, :vd], 0.0)
        more_den = jnp.where(carried, inter[:, 128:129] + inter[:, 130:131], 0.0)
        total = dens[:, h : h + 1] + more_den
        value = (num[0, :, h * vd : (h + 1) * vd] + more) / total
        att_out[:, 0, :, h * vd : (h + 1) * vd] = value.astype(BF).reshape(
            att_out.shape[0], att_out.shape[2], vd
        )
        dens = jnp.where(lane == h, total, dens)
    den_out[0] = dens


def back_state_kernel(nh, vd, docs, lens, meta, x_ref, ga_ref, att_ref, den, pa, pb, rows, gn_out, out):
    row = pl.program_id(0)
    x, ga, att = flat(x_ref), flat(ga_ref), flat(att_ref)
    length = x.shape[0]
    qk = x[:, nh * vd :]
    pos = row_iota((length, 1))
    carried = begin_at(lens, row, docs, pos, meta[0] * length) < 0
    side = lane_iota((length, 128))
    for h in range(nh):
        cut = slice(h * vd, (h + 1) * vd)
        inv = 1.0 / den[0, :, h : h + 1]
        gah = ga[:, cut].astype(F32) * inv
        gd = -jnp.sum(gah * att[:, cut].astype(F32), axis=1, keepdims=True)
        high = gd.astype(BF).astype(F32)
        aux = jnp.where((side == 0) | (side == 2), high, jnp.where(side == 1, gd - high, 0.0))
        gn = jnp.concatenate([gah, aux], axis=1)
        gn_out[0, :, h * 256 : (h + 1) * 256] = gn.astype(BF)
        a, b = picks(qk, pa, pb, rows, h)
        qf = (a * b * rows[2:3, :]).astype(BF)
        st = dot(jnp.where(carried, gn, 0.0).astype(BF), qf, TN)[:AUX]
        out[0, h] = split_sum(st, st[128:129] + st[129:130], False)


def back_intra_kernel(
    nh, vd, docs, lens, meta, x_ref, gn_ref, st_ref, pa, pb, rows, align, gqk_out, gv_out
):
    row = pl.program_id(0)
    x = flat(x_ref)
    length = x.shape[0]
    qk = x[:, nh * vd :]
    one16 = jnp.where(lane_iota((1, 128)) == FEAT, 1.0, 0.0)
    tile = min(TILE, length)
    pos = row_iota((length, 1))
    carried = begin_at(lens, row, docs, pos, meta[0] * length) < 0
    gqk = None
    for h in range(nh):
        qa = (dot(qk, align[4 * h]) + one16).astype(BF)
        ka = (dot(qk, align[4 * h + 1]) + one16).astype(BF)
        k_at_q = dot(qk, align[4 * h + 2]).astype(BF)
        q_at_k = dot(qk, align[4 * h + 3]).astype(BF)
        va = with_ones(x[:, h * vd : (h + 1) * vd])
        gn = gn_ref[0, :, h * 256 : (h + 1) * 256]
        st = st_ref[0, h]
        gqf = jnp.where(carried, dot(gn[:, :AUX], st), 0.0) * rows[2:3, :]
        a, b = picks(qk, pa, pb, rows, h)
        part = dot((gqf * b).astype(BF), pa[h], NT) + dot((gqf * a).astype(BF), pb[h], NT)
        gqk = part if gqk is None else gqk + part
        gk_parts = []
        gq_parts = [None] * (length // tile)
        for t in range(length // tile):
            lo, hi = t * tile, (t + 1) * tile
            s1 = dot(ka[lo:hi], qa[lo:], NT)
            w = 0.5 * (s1 * s1) + 0.5
            kpos = lo + row_iota((tile, 1))
            qpos = lo + lane_iota((1, length - lo))
            beg = begin_at(lens, row, docs, qpos, meta[0] * length)
            see = (kpos >= beg) & (kpos <= qpos)
            gw = dot(va[lo:hi], gn[lo:], NT)
            gs = jnp.where(see, gw * s1, 0.0).astype(BF)
            w = jnp.where(see, w, 0.0).astype(BF)
            gv_out[0, lo:hi, h * vd : (h + 1) * vd] = dot(w, gn[lo:, :vd])
            gk_parts.append(dot(gs, q_at_k[lo:]))
            gq = dot(gs, k_at_q[lo:hi], TN)
            for u in range(t, length // tile):
                piece = gq[(u - t) * tile : (u - t + 1) * tile]
                gq_parts[u] = piece if gq_parts[u] is None else gq_parts[u] + piece
        gqk = gqk + jnp.concatenate(gk_parts, axis=0) + jnp.concatenate(gq_parts, axis=0)
    gqk_out[0] = gqk


def back_key_kernel(nh, vd, docs, blocks, lens, meta, x_ref, gqk_ref, gv_ref, pa, pb, rows, *rest):
    sts, (out,) = rest[: blocks - 1], rest[blocks - 1 :]
    row = pl.program_id(0)
    x = flat(x_ref)
    length = x.shape[0]
    qk = x[:, nh * vd :]
    weights = chain_weights(lens, row, docs, meta[0], blocks, length, True)
    last = begin_at(lens, row, docs, length - 1, meta[0] * length)
    trail = row_iota((length, 1)) >= last
    gqk = gqk_ref[0]
    shape = (out.shape[0], out.shape[2])
    for h in range(nh):
        st = gather_states(sts, weights, h)
        st = split_sum(st, st[128:129] + st[129:130], False)
        va = with_ones(x[:, h * vd : (h + 1) * vd])
        gkf = jnp.where(trail, dot(va[:, :AUX], st), 0.0) * rows[3:4, :]
        a, b = picks(qk, pa, pb, rows, nh + h)
        gqk = gqk + dot((gkf * b).astype(BF), pa[nh + h], NT)
        gqk = gqk + dot((gkf * a).astype(BF), pb[nh + h], NT)
        kf = (a * b * rows[3:4, :]).astype(BF)
        more = jnp.where(trail, dot(kf, st[:vd], NT), 0.0)
        gv = gv_ref[0, :, h * vd : (h + 1) * vd] + more
        out[:, 0, :, h * vd : (h + 1) * vd] = gv.astype(BF).reshape(shape + (vd,))
    out[:, 0, :, nh * vd :] = gqk.astype(BF).reshape(shape + (128,))


def row_call(kernel, rows_n, scalars, ins, outs, flops):
    def spec(shape, dim):
        if dim is None:
            return pl.BlockSpec(shape, lambda r, *_: (0,) * len(shape))
        block = tuple(1 if d == dim else n for d, n in enumerate(shape))
        return pl.BlockSpec(block, lambda r, *_: tuple(r if d == dim else 0 for d in range(len(shape))))

    moved = sum(a.size * a.dtype.itemsize for a, _ in ins)
    moved += sum(int(np.prod(s)) * np.dtype(t).itemsize for s, t, _ in outs)
    return pl.pallas_call(
        kernel,
        out_shape=tuple(jax.ShapeDtypeStruct(s, t) for s, t, _ in outs),
        grid_spec=pltpu.PrefetchScalarGridSpec(
            num_scalar_prefetch=len(scalars),
            grid=(rows_n,),
            in_specs=[spec(a.shape, d) for a, d in ins],
            out_specs=[spec(s, d) for s, t, d in outs],
        ),
        compiler_params=pltpu.CompilerParams(vmem_limit_bytes=56 * 1024 * 1024),
        cost_estimate=pl.CostEstimate(flops=int(flops), bytes_accessed=int(moved), transcendentals=0),
    )(*scalars, *[a for a, _ in ins])


def exchange_kernel(to_blocks, width, src, dst, ssem, rsem, lsem):
    s, a, b = lax.axis_index("seq"), lax.axis_index("ha"), lax.axis_index("hb")
    size_a, size_b = lax.axis_size("ha"), lax.axis_size("hb")
    count = size_a * size_b
    bar = pltpu.get_barrier_semaphore()
    same = s == a

    def copy(k):
        base = a if to_blocks else s
        pa = lax.rem(base + k // size_b, size_a)
        pb = lax.rem(b + k % size_b, size_b)
        piece = pa * size_b + pb
        if to_blocks:
            source = src.at[:, pl.ds(pl.multiple_of(piece * width, 128), width)]
            place = dst.at[a * size_b + b]
            target, sender = (pa, s, pb), (a, pa, pb)
        else:
            source = src.at[piece]
            place = dst.at[:, pl.ds(pl.multiple_of((s * size_b + b) * width, 128), width)]
            target, sender = (a, pa, pb), (pa, s, pb)
        remote = functools.partial(
            pltpu.make_async_remote_copy,
            src_ref=source,
            dst_ref=place,
            send_sem=ssem.at[k],
            recv_sem=rsem.at[k],
            device_id=target,
            device_id_type=MESH_ID,
        )
        return sender, remote, functools.partial(pltpu.make_async_copy, source, place, lsem)

    def either(k, remote, local):
        if k:
            remote()
        else:
            pl.when(jnp.logical_not(same))(remote)
            pl.when(same)(local)

    for k in range(count):
        sender = copy(k)[0]
        signal = functools.partial(pl.semaphore_signal, bar, 1, device_id=sender, device_id_type=MESH_ID)
        either(k, signal, lambda: None)
    pl.semaphore_wait(bar, jnp.where(same, count - 1, count))
    for k in range(count):
        _, remote, local = copy(k)
        either(k, lambda: remote().start(), lambda: local().start())
    for k in range(count):
        _, remote, local = copy(k)
        either(k, lambda: remote().wait(), lambda: local().wait())


def exchange(x, to_blocks, width, collective):
    count = lax.axis_size("ha") * lax.axis_size("hb")
    tokens = x.shape[0] if to_blocks else x.shape[1]
    shape = (count, tokens, width) if to_blocks else (tokens, count * width)
    return pl.pallas_call(
        functools.partial(exchange_kernel, to_blocks, width),
        out_shape=jax.ShapeDtypeStruct(shape, x.dtype),
        in_specs=[pl.BlockSpec(memory_space=pl.ANY)],
        out_specs=pl.BlockSpec(memory_space=pl.ANY),
        scratch_shapes=[
            pltpu.SemaphoreType.DMA((count,)),
            pltpu.SemaphoreType.DMA((count,)),
            pltpu.SemaphoreType.DMA,
        ],
        compiler_params=pltpu.CompilerParams(collective_id=collective, has_side_effects=True),
        cost_estimate=pl.CostEstimate(flops=0, bytes_accessed=x.size * 2, transcendentals=0),
    )(x)


def transpose_perm(size):
    return [(s * size + z, z * size + s) for s in range(size) for z in range(size)]


def swap_home(x):
    return lax.ppermute(x, ("seq", "ha"), transpose_perm(lax.axis_size("seq")))


def chain_pieces(x, backward):
    size = lax.axis_size("ha")
    out = []
    for k in range(1, size):
        if backward:
            perm = [(i, i - k) for i in range(k, size)]
        else:
            perm = [(i, i + k) for i in range(size - k)]
        out.append(lax.ppermute(x, "ha", perm))
    return out


def sum_home(x):
    size = lax.axis_size("ha")
    a = lax.axis_index("ha")
    total = None
    for k in range(size):
        block = lax.dynamic_index_in_dim(x, lax.rem(a + k, size), 0, False)
        perm = [(s * size + z, ((z + k) % size) * size + s) for s in range(size) for z in range(size)]
        got = lax.ppermute(block, ("seq", "ha"), perm).astype(F32)
        total = got if total is None else total + got
    return total


def rms_scale(x):
    return lax.rsqrt(jnp.mean(x * x, axis=-1, keepdims=True) + EPS)


def on_device(
    inputs,
    attn_gain,
    w_query,
    w_key,
    w_value,
    w_out,
    out_bias,
    mlp_gain,
    gate_weight,
    up_weight,
    down_weight,
    cotangent,
    doc_lengths,
):
    blocks = lax.axis_size("seq")
    group = ("seq", "hb")
    count = blocks * lax.axis_size("hb")
    sub_len, rows_n, width = inputs.shape
    docs = doc_lengths.shape[1]
    nh = w_query.shape[1] // FEAT
    vd = w_value.shape[1] // nh
    vw = nh * vd
    xw = vw + 128
    length = sub_len * count
    tokens = rows_n * sub_len
    meta = lax.axis_index("ha").astype(jnp.int32).reshape(1)
    pa, pb, frows, align = feature_tables(nh)
    scalars = (doc_lengths, meta)

    x = jnp.transpose(inputs, (1, 0, 2)).astype(F32)
    cot = jnp.transpose(cotangent, (1, 0, 2))
    scale_one = rms_scale(x)
    normed_one = x * scale_one
    normed_low = (normed_one * attn_gain).astype(BF)
    normed_full = lax.all_gather(swap_home(normed_low), group, axis=0)
    pad = jnp.zeros((128 - 2 * nh * FEAT, width), BF)
    w_in = swap_home(jnp.concatenate([w_value.T, w_query.T, w_key.T, pad], axis=0))
    w_out_home = swap_home(w_out)
    gate_t, up_t, down = swap_home(gate_weight.T), swap_home(up_weight.T), swap_home(down_weight)
    w_out_full = lax.all_gather(w_out_home, group, axis=0, tiled=True)
    w_in_full = lax.all_gather(w_in, group, axis=0, tiled=True)

    qkv = jnp.einsum("grtd,cd->grtc", normed_full, w_in, preferred_element_type=F32).astype(BF)
    pair = nh * rows_n * length * length
    (states,) = row_call(
        functools.partial(state_kernel, nh, vd, docs),
        rows_n,
        scalars,
        [(qkv, 1), (pa, None), (pb, None), (frows, None)],
        [((rows_n, nh, AUX, TILE), BF, 0)],
        nh * rows_n * length * 256 * 256 * 4,
    )
    earlier = chain_pieces(states, False)
    num, den = row_call(
        functools.partial(intra_kernel, nh, vd, docs),
        rows_n,
        scalars,
        [(qkv, 1), (align, None)],
        [((rows_n, length, vw), F32, 0), ((rows_n, length, 128), F32, 0)],
        pair * 256 * 4,
    )
    att, den, state_in = row_call(
        functools.partial(attend_kernel, nh, vd, docs, blocks),
        rows_n,
        scalars,
        [(qkv, 1), (num, 0), (den, 0), (pa, None), (pb, None), (frows, None)]
        + [(e, 0) for e in earlier],
        [
            ((count, rows_n, sub_len, vw), BF, 1),
            ((rows_n, length, 128), F32, 0),
            ((rows_n, nh, AUX, TILE), BF, 0),
        ],
        nh * rows_n * length * 256 * 256 * 6,
    )
    attended = exchange(att.reshape(count, tokens, vw), False, vw, 0)
    attn_branch = dot(attended, w_out_full).reshape(rows_n, sub_len, width)
    middle = x + attn_branch + out_bias
    scale_two = rms_scale(middle)
    normed_two = middle * scale_two
    normed_two_low = (normed_two * mlp_gain).astype(BF)

    n2f = lax.all_gather(normed_two_low, group, axis=0).reshape(count * tokens, width)
    cotf = lax.all_gather(cot, group, axis=0).reshape(count * tokens, width)
    gate = dot(n2f, gate_t, NT)
    up = dot(n2f, up_t, NT)
    sig = jax.nn.sigmoid(gate)
    hidden = (gate * sig * up).astype(BF)
    grad_hidden = dot(cotf, down, NT)
    grad_gate = (grad_hidden * up * sig * (1.0 + gate * (1.0 - sig))).astype(BF)
    grad_up = (grad_hidden * gate * sig).astype(BF)
    grad_two = (dot(grad_gate, gate_t) + dot(grad_up, up_t)).astype(BF)
    grad_two = (
        lax.psum_scatter(grad_two, group, scatter_dimension=0, tiled=True)
        .astype(F32)
        .reshape(rows_n, sub_len, width)
    )
    branch = dot(hidden, down).astype(BF)
    branch = (
        lax.psum_scatter(branch, group, scatter_dimension=0, tiled=True)
        .astype(F32)
        .reshape(rows_n, sub_len, width)
    )
    output = (middle + branch).astype(BF)

    gain_two_part = jnp.sum(grad_two * normed_two, axis=(0, 1))
    scaled = grad_two * mlp_gain
    grad_middle = cot.astype(F32) + scale_two * (
        scaled - normed_two * jnp.mean(scaled * normed_two, axis=-1, keepdims=True)
    )
    bias_part = jnp.sum(grad_middle, axis=(0, 1))
    grad_branch = grad_middle.astype(BF)

    grad_att = dot(grad_branch.reshape(tokens, width), w_out_full, NT).astype(BF)
    grad_att = exchange(grad_att, True, vw, 1).reshape(count, rows_n, sub_len, vw)
    gn, grad_states = row_call(
        functools.partial(back_state_kernel, nh, vd, docs),
        rows_n,
        scalars,
        [(qkv, 1), (grad_att, 1), (att, 1), (den, 0), (pa, None), (pb, None), (frows, None)],
        [((rows_n, length, nh * 256), BF, 0), ((rows_n, nh, AUX, TILE), BF, 0)],
        nh * rows_n * length * 256 * 256 * 4,
    )
    later = chain_pieces(grad_states, True)
    gqk, gv = row_call(
        functools.partial(back_intra_kernel, nh, vd, docs),
        rows_n,
        scalars,
        [(qkv, 1), (gn, 0), (state_in, 0), (pa, None), (pb, None), (frows, None), (align, None)],
        [((rows_n, length, 128), F32, 0), ((rows_n, length, vw), F32, 0)],
        pair * 256 * 8,
    )
    (gqkv,) = row_call(
        functools.partial(back_key_kernel, nh, vd, docs, blocks),
        rows_n,
        scalars,
        [(qkv, 1), (gqk, 0), (gv, 0), (pa, None), (pb, None), (frows, None)] + [(e, 0) for e in later],
        [((count, rows_n, sub_len, xw), BF, 1)],
        nh * rows_n * length * 256 * 256 * 6,
    )
    grad_in = exchange(gqkv.reshape(count, tokens, xw), False, xw, 2)
    grad_one = dot(grad_in, w_in_full).reshape(rows_n, sub_len, width)
    gain_one_part = jnp.sum(grad_one * normed_one, axis=(0, 1))
    scaled = grad_one * attn_gain
    input_grad = (
        grad_middle
        + scale_one * (scaled - normed_one * jnp.mean(scaled * normed_one, axis=-1, keepdims=True))
    ).astype(BF)

    flat_tokens = count * tokens
    grad_w_in = dot(gqkv.reshape(flat_tokens, xw), normed_full.reshape(flat_tokens, width), TN)
    grad_w_in = sum_home(
        jnp.transpose(grad_w_in.astype(BF).reshape(xw, blocks, width // blocks), (1, 0, 2))
    )
    branch_full = lax.all_gather(swap_home(grad_branch), group, axis=0).reshape(flat_tokens, width)
    grad_w_out = dot(att.reshape(flat_tokens, vw), branch_full, TN)
    grad_w_out = sum_home(
        jnp.transpose(grad_w_out.astype(BF).reshape(vw, blocks, width // blocks), (1, 0, 2))
    )

    def ff_grad(a, b):
        part = dot(a, b, TN).astype(BF)
        part = lax.psum_scatter(part, "ha", scatter_dimension=1, tiled=True)
        return swap_home(part).astype(F32)

    grad_gate_w = ff_grad(grad_gate, n2f)
    grad_up_w = ff_grad(grad_up, n2f)
    grad_down_w = ff_grad(hidden, cotf)
    vectors = jnp.stack([gain_one_part, bias_part, gain_two_part])
    vectors = lax.psum_scatter(vectors, ("seq", "ha", "hb"), scatter_dimension=1, tiled=True)
    qk_cut = vw + nh * FEAT
    return (
        jnp.transpose(output, (1, 0, 2)),
        jnp.transpose(input_grad, (1, 0, 2)),
        vectors[0],
        grad_w_in[vw:qk_cut].T,
        grad_w_in[qk_cut : qk_cut + nh * FEAT].T,
        grad_w_in[:vw].T,
        grad_w_out,
        vectors[1],
        vectors[2],
        grad_gate_w.T,
        grad_up_w.T,
        grad_down_w,
    )


def solution(mesh):
    seq, head = mesh.shape["seq"], mesh.shape["head"]
    inner = Mesh(mesh.devices.reshape(seq, seq, head // seq), ("seq", "ha", "hb"))
    every, heads = ("seq", "ha", "hb"), ("ha", "hb")
    placed = (
        P(every, None, None),
        P(),
        P(None, heads),
        P(None, heads),
        P(None, heads),
        P(heads, None),
        P(),
        P(),
        P(None, heads),
        P(None, heads),
        P(heads, None),
        P(every, None, None),
        P(),
    )
    return jax.shard_map(
        on_device,
        mesh=inner,
        in_specs=placed,
        out_specs=(
            P(every, None, None),
            P(every, None, None),
            P(every),
            P("seq", heads),
            P("seq", heads),
            P("seq", heads),
            P(heads, "seq"),
            P(every),
            P(every),
            P("seq", heads),
            P("seq", heads),
            P(heads, "seq"),
        ),
        check_vma=False,
    )
```

time: 2240 us -> 1700 us (0.76)
  waiting for transfers between devices: 1720 us -> 931 us
  Pallas kernels: 0 us -> 312 us
  starting transfers between devices: 1.26 us -> 161 us
  matrix products: 349 us -> 198 us
  blocking collectives: 58.4 us -> 0 us
  other arithmetic: 66.9 us -> 29.3 us
    reduce_scatter x11 -> x5, waiting for transfers between devices: 1050 us -> 392 us  [the longest x1 194 us: on_device(): lax.psum_scatter(grad_two, group, scatter_dimension=0, tiled=True)]
    pallas_call x0 -> x9, Pallas kernels: none -> 312 us  [the longest x3 245 us: exchange(): pl.pallas_call(functools.partial(exchange_kernel, to_blocks, width), out_...]
    all_gather x6, waiting for transfers between devices: 665 us -> 401 us  [the longest x1 194 us: on_device(): normed_full = lax.all_gather(swap_home(normed_low), group, axis=0)]
    ppermute x0 -> x24, starting transfers between devices: none -> 161 us  [the longest x8 67.2 us: sum_home(): got = lax.ppermute(block, ('seq', 'ha'), perm).astype(F32)]
    dot_general x35 -> x15, matrix products: 349 us -> 198 us  [the longest x14 188 us: dot(): return lax.dot_general(a, b, dims, preferred_element_type=F32)]
    ppermute x0 -> x24, waiting for transfers between devices: none -> 77.3 us  [the longest x6 40.8 us: chain_pieces(): out.append(lax.ppermute(x, 'ha', perm))]
    unnamed x17 -> x13, waiting for transfers between devices: 0.79 us -> 61 us
    unnamed x2 -> x0, blocking collectives: 48 us -> none
  transfers between devices with their start and end apart: 17 -> 36, of which waited for: 10 -> 14; matrix products, arithmetic and copies ran while one was open for 12% -> 11% of each run, Pallas kernels for 0% -> 19%
where the time goes in v1:
time: 1700 us; the launch traced here: 1690 us
  waiting for transfers between devices  931 us (55%)
  Pallas kernels  312 us (18%)
  matrix products  198 us (12%)
  starting transfers between devices  161 us (9%)
  local copies, waits for them, and re-layouts  38.6 us (2%)
  other arithmetic  29.3 us (2%)
    pallas_call x3, Pallas kernels, exchange(): pl.pallas_call(functools.partial(exchange_kernel, to_blocks, width), out_...  245 us
    all_gather x1, waiting for transfers between devices, on_device(): normed_full = lax.all_gather(swap_home(normed_low), group, axis=0)  194 us
    reduce_scatter x1, waiting for transfers between devices, on_device(): lax.psum_scatter(grad_two, group, scatter_dimension=0, tiled=True)  194 us
    dot_general x14, matrix products, dot(): return lax.dot_general(a, b, dims, preferred_element_type=F32)  188 us
    all_gather x1, waiting for transfers between devices, on_device(): lax.all_gather(normed_two_low, group, axis=0).reshape(count * tokens, width)  105 us
    reduce_scatter x3, waiting for transfers between devices, ff_grad(): part = lax.psum_scatter(part, 'ha', scatter_dimension=1, tiled=True)  105 us
    reduce_scatter x1, waiting for transfers between devices, on_device(): lax.psum_scatter(branch, group, scatter_dimension=0, tiled=True).astype(F32)  93.3 us
    all_gather x1, waiting for transfers between devices, on_device(): lax.all_gather(swap_home(grad_branch), group, axis=0)  74.5 us
  transfers between devices with their start and end apart: 36, of which 14 were waited for; matrix products, arithmetic and copies ran while one was open for 11% of the time, Pallas kernels for 19%

profile of v1, /device:TPU:0, one launch (start us, length us, event | category | flops | bytes accessed | tf_op | source)
XLA Modules:
  0.0 1686.0 jit_solution(1304539961873053315)
XLA Ops:
  20.9 194.4 %all-gather.15.cloned.1.call-done = bf16[24,128,2048]{2,1,0:T(8,128)(2,1)} async-done(((bf16[3,128,2048]{2,1,0:T(8,128)(2,1)}), bf16[24,128,2048]{2,1,0:T(8,128)(2,1)}) %all-gather.15.cloned.1.call-update) | async-done | bytes 12582928 | tf_op jit(solution)/shard_map/all_gather | solution.py:459
  215.3 10.8 convolution_convert_fusion.5.x_ref
  241.9 13.8 collective-permute-start.3
  257.0 10.8 shard_map.256
  284.2 37.2 %shard_map.259 = bf16[384,2048]{1,0:T(8,128)(2,1)} custom-call(bf16[8,384,256]{2,1,0:T(8,128)(2,1)} %bitcast.138), custom_call_target="tpu_custom_call" | custom-call | bytes 1572864 | tf_op jit(solution)/shard_map/pallas_call | solution.py:373
  335.0 22.8 %collective-permute-start.7 = (bf16[688,2048]{1,0:T(8,128)(2,1)}, bf16[688,2048]{1,0:T(8,128)(2,1)}, u32[]{:S(2)}, u32[]{:S(2)}) collective-permute-start(bf16[688,2048]{1,0:T(8,128)(2,1)} %bitcast.174), channel_id=1, source_target_pairs={{0,0},{2,8},{4,16},{6,24},{8,2},{10,10},{12,18},{14,26},{16,4},{18... | collective-permute-start | bytes 8454152 | tf_op jit(solution)/shard_map/ppermute | solution.py:393
  357.8 22.8 %collective-permute-start.6 = (bf16[688,2048]{1,0:T(8,128)(2,1)}, bf16[688,2048]{1,0:T(8,128)(2,1)}, u32[]{:S(2)}, u32[]{:S(2)}) collective-permute-start(bf16[688,2048]{1,0:T(8,128)(2,1)} %bitcast.175), channel_id=1, source_target_pairs={{0,0},{2,8},{4,16},{6,24},{8,2},{10,10},{12,18},{14,26},{16,4},{18... | collective-permute-start | bytes 8454152 | tf_op jit(solution)/shard_map/ppermute | solution.py:393
  380.5 27.2 %all-gather.19.cloned.1.call-done = bf16[24,128,2048]{2,1,0:T(8,128)(2,1)} async-done(((bf16[3,128,2048]{2,1,0:T(8,128)(2,1)}), bf16[24,128,2048]{2,1,0:T(8,128)(2,1)}) %all-gather.19.cloned.1.call-update) | async-done | bytes 12582928 | tf_op jit(solution)/shard_map/all_gather | solution.py:507
  407.7 14.9 fusion.30
  422.6 104.6 %all-gather.17.cloned.1.call-done = bf16[24,128,2048]{2,1,0:T(8,128)(2,1)} async-done(((bf16[3,128,2048]{2,1,0:T(8,128)(2,1)}), bf16[24,128,2048]{2,1,0:T(8,128)(2,1)}) %all-gather.17.cloned.1.call-update) | async-done | bytes 12582928 | tf_op jit(solution)/shard_map/all_gather | solution.py:506
  527.2 14.9 fusion.29
  542.1 22.1 %multiply_convert_fusion.1 = (bf16[3072,688]{0,1:T(8,128)(2,1)}, bf16[3072,688]{0,1:T(8,128)(2,1)}, bf16[3072,688]{0,1:T(8,128)(2,1)S(1)}) fusion(f32[3072,688]{0,1:T(8,128)} %fusion.30, f32[3072,688]{0,1:T(8,128)} %fusion.29, bf16[3072,2048]{1,0:T(8,128)(2,1)} %bitcast.171, bf16[688,2048]{1,0:T(8,128)(2,1)} %collective-permute-done.6), kind=kOutput, calls=%fused_computation.3 | convolution fusion | flops 8690860032 | bytes 44990464 | tf_op jit(solution)/shard_map/dot_general | solution.py:25
  564.2 16.8 fusion.31
  581.0 19.3 %add_convert_fusion = bf16[3072,2048]{1,0:T(8,128)(2,1)} fusion(f32[3072,2048]{1,0:T(8,128)} %fusion.31, bf16[3072,688]{0,1:T(8,128)(2,1)} %get-tuple-element.74, bf16[688,2048]{1,0:T(8,128)(2,1)} %collective-permute-done.6), kind=kOutput, calls=%fused_computation | convolution fusion | flops 8669626368 | bytes 44793856 | tf_op jit(solution)/shard_map/dot_general | solution.py:25
  600.4 15.4 convolution_convert_fusion
  616.6 14.2 convolution_convert_fusion.1
  630.9 14.3 convolution_convert_fusion.3
  645.2 14.5 convolution_convert_fusion.2
  659.8 194.4 %reduce-scatter.11.cloned.1.call-done = bf16[384,2048]{1,0:T(8,128)(2,1)} async-done(((bf16[3072,2048]{1,0:T(8,128)(2,1)}), bf16[384,2048]{1,0:T(8,128)(2,1)}) %reduce-scatter.11.cloned.1.call-update) | async-done | bytes 1572880 | tf_op jit(solution)/shard_map/reduce_scatter | solution.py:517
  856.6 93.3 %reduce-scatter.9.cloned.1.call-done = bf16[384,2048]{1,0:T(8,128)(2,1)} async-done(((bf16[3072,2048]{1,0:T(8,128)(2,1)}), bf16[384,2048]{1,0:T(8,128)(2,1)}) %reduce-scatter.9.cloned.1.call-update) | async-done | bytes 1572880 | tf_op jit(solution)/shard_map/reduce_scatter | solution.py:523
  958.0 9.9 convolution_convert_fusion.4.src
  967.9 65.4 %shard_map.260 = bf16[8,384,256]{2,1,0:T(8,128)(2,1)} custom-call(bf16[384,2048]{1,0:T(8,128)(2,1)} %convolution_convert_fusion.4.src), custom_call_target="tpu_custom_call" | custom-call | bytes 1572864 | tf_op jit(solution)/shard_map/pallas_call | solution.py:373
  1048.8 22.5 %shard_map.262 = (f32[3,1024,128]{2,1,0:T(8,128)}, f32[3,1024,256]{2,1,0:T(8,128)}) custom-call(s32[3,8]{1,0:T(4,128)} %lens.11, s32[1]{0:T(128)} %bitcast.1.meta, bf16[8,3,128,384]{3,2,1,0:T(8,128)(2,1)} %convolution_convert_fusion.5.x_ref, bf16[3,1024,512]{2,1,0:T(8,128)(2,1)} %get-tuple-element.25.gn_ref, ...), custom_call_target="tpu_custom_call" | custom-call | flops 12884901888 | bytes 11436032 | tf_op jit(solution)/shard_map/pallas_call | solution.py:304
  1071.2 34.4 %collective-permute-done.10.rest_1_ = bf16[3,2,136,256]{3,2,1,0:T(8,128)(2,1)S(1)} collective-permute-done((bf16[3,2,136,256]{3,2,1,0:T(8,128)(2,1)}, bf16[3,2,136,256]{3,2,1,0:T(8,128)(2,1)S(1)}, u32[]{:S(2)}, u32[]{:S(2)}) %collective-permute-start.10) | collective-permute-done | bytes 417824 | tf_op jit(solution)/shard_map/ppermute | solution.py:404
  1116.1 141.9 %shard_map.264 = bf16[384,3072]{1,0:T(8,128)(2,1)} custom-call(bf16[8,384,384]{2,1,0:T(8,128)(2,1)} %bitcast.142), custom_call_target="tpu_custom_call" | custom-call | bytes 2359296 | tf_op jit(solution)/shard_map/pallas_call | solution.py:373
  1274.0 29.7 %reduce-scatter.13.cloned.1.call-done = bf16[688,512]{1,0:T(8,128)(2,1)} async-done(((bf16[688,2048]{1,0:T(8,128)(2,1)}), bf16[688,512]{1,0:T(8,128)(2,1)}) %reduce-scatter.13.cloned.1.call-update) | async-done | bytes 704528 | tf_op jit(solution)/shard_map/reduce_scatter | solution.py:586
  1305.6 74.9 %reduce-scatter.15.cloned.1.call-done = bf16[688,512]{1,0:T(8,128)(2,1)} async-done(((bf16[688,2048]{1,0:T(8,128)(2,1)}), bf16[688,512]{1,0:T(8,128)(2,1)}) %reduce-scatter.15.cloned.1.call-update) | async-done | bytes 704528 | tf_op jit(solution)/shard_map/reduce_scatter | solution.py:586
  1419.4 23.5 %collective-permute-start.13 = (bf16[384,512]{0,1:T(8,128)(2,1)}, bf16[384,512]{0,1:T(8,128)(2,1)S(1)}, u32[]{:S(2)}, u32[]{:S(2)}) collective-permute-start(bf16[384,512]{0,1:T(8,128)(2,1)} %bitcast.31), channel_id=1, source_target_pairs={{0,8},{2,16},{4,24},{6,0},{8,10},{10,18},{12,26},{14,2},{16,12},{1... | collective-permute-start | bytes 1179656 | tf_op jit(solution)/shard_map/ppermute | solution.py:415
  1442.9 33.7 %collective-permute-start.14 = (bf16[384,512]{0,1:T(8,128)(2,1)}, bf16[384,512]{0,1:T(8,128)(2,1)S(1)}, u32[]{:S(2)}, u32[]{:S(2)}) collective-permute-start(bf16[384,512]{0,1:T(8,128)(2,1)} %bitcast.32), channel_id=1, source_target_pairs={{0,16},{2,24},{4,0},{6,8},{8,18},{10,26},{12,2},{14,10},{16,20},{1... | collective-permute-start | bytes 1179656 | tf_op jit(solution)/shard_map/ppermute | solution.py:415
  1486.7 59.4 %reduce-scatter.19.cloned.1.call-done = f32[64,3]{1,0:T(8,128)} async-done(((f32[2048,3]{1,0:T(8,128)}), f32[64,3]{1,0:T(8,128)}) %reduce-scatter.19.cloned.1.call-update) | async-done | bytes 784
  1550.1 74.5 %all-gather.21.cloned.1.call-done = bf16[24,128,2048]{2,1,0:T(8,128)(2,1)} async-done(((bf16[3,128,2048]{2,1,0:T(8,128)(2,1)}), bf16[24,128,2048]{2,1,0:T(8,128)(2,1)}) %all-gather.21.cloned.1.call-update) | async-done | bytes 12582928 | tf_op jit(solution)/shard_map/all_gather | solution.py:578
  1651.4 26.6 %collective-permute-done.19 = bf16[256,512]{1,0:T(8,128)(2,1)S(1)} collective-permute-done((bf16[256,512]{1,0:T(8,128)(2,1)S(1)}, bf16[256,512]{1,0:T(8,128)(2,1)S(1)}, u32[]{:S(2)}, u32[]{:S(2)}) %collective-permute-start.19) | collective-permute-done | bytes 262176 | tf_op jit(solution)/shard_map/ppermute | solution.py:415
  (184 shorter events, 196.3 us)
Async XLA Ops:
  7.2 208.2 %all-gather.15.cloned.1.call-start = ((), (), s32[]{:S(2)}) async-start(), calls=%async_computation.13 | async-start | bytes 14155776 | tf_op jit(solution)/shard_map/all_gather | solution.py:459
  12.9 308.5 %all-gather.11.cloned.1.call-start = ((), (), s32[]{:S(2)}) async-start(), calls=%async_computation.6 | async-start | bytes 9437184 | tf_op jit(solution)/shard_map/all_gather | solution.py:464
  15.9 391.8 %all-gather.19.cloned.1.call-start = ((), (), s32[]{:S(2)}) async-start(), calls=%async_computation.15 | async-start | bytes 14155776 | tf_op jit(solution)/shard_map/all_gather | solution.py:507
  16.6 510.6 %all-gather.17.cloned.1.call-start = ((), (), s32[]{:S(2)}) async-start(), calls=%async_computation.14 | async-start | bytes 14155776 | tf_op jit(solution)/shard_map/all_gather | solution.py:506
  232.3 35.5 %collective-permute-start.4 = (bf16[3,2,136,256]{3,2,1,0:T(8,128)(2,1)}, bf16[3,2,136,256]{3,2,1,0:T(8,128)(2,1)S(1)}, u32[]{:S(2)}, u32[]{:S(2)}) collective-permute-start(bf16[3,2,136,256]{3,2,1,0:T(8,128)(2,1)} %shard_map.257), channel_id=1, source_target_pairs={{0,6},{1,7},{8,14},{9,15},{16,22},{17,23},{24,30},{25,31}} | collective-permute-start | bytes 1253384 | tf_op jit(solution)/shard_map/ppermute | solution.py:404
  241.9 26.0 %collective-permute-start.3 = (bf16[3,2,136,256]{3,2,1,0:T(8,128)(2,1)}, bf16[3,2,136,256]{3,2,1,0:T(8,128)(2,1)S(1)}, u32[]{:S(2)}, u32[]{:S(2)}) collective-permute-start(bf16[3,2,136,256]{3,2,1,0:T(8,128)(2,1)} %shard_map.257), channel_id=1, source_target_pairs={{0,4},{2,6},{1,5},{3,7},{8,12},{10,14},{9,13},{11,15},{16,20},{18,... | collective-permute-start | bytes 1253384 | tf_op jit(solution)/shard_map/ppermute | solution.py:404
  255.7 18.6 %collective-permute-start.2 = (bf16[3,2,136,256]{3,2,1,0:T(8,128)(2,1)}, bf16[3,2,136,256]{3,2,1,0:T(8,128)(2,1)S(1)}, u32[]{:S(2)}, u32[]{:S(2)}) collective-permute-start(bf16[3,2,136,256]{3,2,1,0:T(8,128)(2,1)} %shard_map.257), channel_id=1, source_target_pairs={{0,2},{2,4},{4,6},{1,3},{3,5},{5,7},{8,10},{10,12},{12,14},{9,11},... | collective-permute-start | bytes 1253384 | tf_op jit(solution)/shard_map/ppermute | solution.py:404
  331.9 522.3 %reduce-scatter.11.cloned.1.call-start = ((), (), s32[]{:S(2)}) async-start(), calls=%async_computation.8 | async-start | bytes 14155776 | tf_op jit(solution)/shard_map/reduce_scatter | solution.py:517
  332.8 47.8 %collective-permute-start.8 = (bf16[688,2048]{1,0:T(8,128)(2,1)S(1)}, bf16[688,2048]{1,0:T(8,128)(2,1)}, u32[]{:S(2)}, u32[]{:S(2)}) collective-permute-start(bf16[688,2048]{1,0:T(8,128)(2,1)S(1)} %copy-done.27), channel_id=1, source_target_pairs={{0,0},{2,8},{4,16},{6,24},{8,2},{10,10},{12,18},{14,26},{16,4},{18... | collective-permute-start | bytes 8454152 | tf_op jit(solution)/shard_map/ppermute | solution.py:393
  335.0 87.6 %collective-permute-start.7 = (bf16[688,2048]{1,0:T(8,128)(2,1)}, bf16[688,2048]{1,0:T(8,128)(2,1)}, u32[]{:S(2)}, u32[]{:S(2)}) collective-permute-start(bf16[688,2048]{1,0:T(8,128)(2,1)} %bitcast.174), channel_id=1, source_target_pairs={{0,0},{2,8},{4,16},{6,24},{8,2},{10,10},{12,18},{14,26},{16,4},{18... | collective-permute-start | bytes 8454152 | tf_op jit(solution)/shard_map/ppermute | solution.py:393
  357.8 184.3 %collective-permute-start.6 = (bf16[688,2048]{1,0:T(8,128)(2,1)}, bf16[688,2048]{1,0:T(8,128)(2,1)}, u32[]{:S(2)}, u32[]{:S(2)}) collective-permute-start(bf16[688,2048]{1,0:T(8,128)(2,1)} %bitcast.175), channel_id=1, source_target_pairs={{0,0},{2,8},{4,16},{6,24},{8,2},{10,10},{12,18},{14,26},{16,4},{18... | collective-permute-start | bytes 8454152 | tf_op jit(solution)/shard_map/ppermute | solution.py:393
  600.3 349.6 %reduce-scatter.9.cloned.1.call-start = ((), (), s32[]{:S(2)}) async-start(), calls=%async_computation.7 | async-start | bytes 14155776 | tf_op jit(solution)/shard_map/reduce_scatter | solution.py:523
  615.8 642.3 %all-gather.13.cloned.1.call-start = ((), (), s32[]{:S(2)}) async-start(), calls=%async_computation.9 | async-start | bytes 14155776 | tf_op jit(solution)/shard_map/all_gather | solution.py:465
  616.5 655.7 %reduce-scatter.17.cloned.1.call-start = ((), (), s32[]{:S(2)}) async-start(), calls=%async_computation.12 | async-start | bytes 3522560 | tf_op jit(solution)/shard_map/reduce_scatter | solution.py:586
  630.8 672.9 %reduce-scatter.13.cloned.1.call-start = ((), (), s32[]{:S(2)}) async-start(), calls=%async_computation.10 | async-start | bytes 3522560 | tf_op jit(solution)/shard_map/reduce_scatter | solution.py:586
  645.2 735.3 %reduce-scatter.15.cloned.1.call-start = ((), (), s32[]{:S(2)}) async-start(), calls=%async_computation.11 | async-start | bytes 3522560 | tf_op jit(solution)/shard_map/reduce_scatter | solution.py:586
  659.8 886.4 %reduce-scatter.19.cloned.1.call-start = ((), (), s32[]{:S(2)}) async-start(), calls=%async_computation.17 | async-start | bytes 1081344
  1042.8 28.4 %collective-permute-start.11 = (bf16[3,2,136,256]{3,2,1,0:T(8,128)(2,1)}, bf16[3,2,136,256]{3,2,1,0:T(8,128)(2,1)S(1)}, u32[]{:S(2)}, u32[]{:S(2)}) collective-permute-start(bf16[3,2,136,256]{3,2,1,0:T(8,128)(2,1)} %get-tuple-element.29), channel_id=1, source_target_pairs={{6,0},{7,1},{14,8},{15,9},{22,16},{23,17},{30,24},{31,25}} | collective-permute-start | bytes 1253384 | tf_op jit(solution)/shard_map/ppermute | solution.py:404
  1044.1 61.5 %collective-permute-start.10 = (bf16[3,2,136,256]{3,2,1,0:T(8,128)(2,1)}, bf16[3,2,136,256]{3,2,1,0:T(8,128)(2,1)S(1)}, u32[]{:S(2)}, u32[]{:S(2)}) collective-permute-start(bf16[3,2,136,256]{3,2,1,0:T(8,128)(2,1)} %get-tuple-element.29), channel_id=1, source_target_pairs={{4,0},{6,2},{5,1},{7,3},{12,8},{14,10},{13,9},{15,11},{20,16},{22,... | collective-permute-start | bytes 1253384 | tf_op jit(solution)/shard_map/ppermute | solution.py:404
  1045.4 60.2 %collective-permute-start.9 = (bf16[3,2,136,256]{3,2,1,0:T(8,128)(2,1)}, bf16[3,2,136,256]{3,2,1,0:T(8,128)(2,1)S(1)}, u32[]{:S(2)}, u32[]{:S(2)}) collective-permute-start(bf16[3,2,136,256]{3,2,1,0:T(8,128)(2,1)} %get-tuple-element.29), channel_id=1, source_target_pairs={{2,0},{4,2},{6,4},{3,1},{5,3},{7,5},{10,8},{12,10},{14,12},{11,9},... | collective-permute-start | bytes 1253384 | tf_op jit(solution)/shard_map/ppermute | solution.py:404
  1046.7 224.4 %collective-permute-start.16 = (bf16[3,128,2048]{2,1,0:T(8,128)(2,1)}, bf16[3,128,2048]{2,1,0:T(8,128)(2,1)S(1)}, u32[]{:S(2)}, u32[]{:S(2)}) collective-permute-start(bf16[3,128,2048]{2,1,0:T(8,128)(2,1)} %convert_element_type.103), channel_id=1, source_target_pairs={{0,0},{2,8},{4,16},{6,24},{8,2},{10,10},{12,18},{14,26},{16,4},{18... | collective-permute-start | bytes 4718600 | tf_op jit(solution)/shard_map/ppermute | solution.py:393
  1271.0 353.6 %all-gather.21.cloned.1.call-start = ((), (), s32[]{:S(2)}) async-start(), calls=%async_computation.16 | async-start | bytes 14155776 | tf_op jit(solution)/shard_map/all_gather | solution.py:578
  1272.3 115.0 %collective-permute-start.23 = (bf16[688,512]{1,0:T(8,128)(2,1)}, bf16[688,512]{1,0:T(8,128)(2,1)S(1)}, u32[]{:S(2)}, u32[]{:S(2)}) collective-permute-start(bf16[688,512]{1,0:T(8,128)(2,1)} %reduce-scatter.17.cloned.1.call-done), channel_id=1, source_target_pairs={{0,0},{2,8},{4,16},{6,24},{8,2},{10,10},{12,18},{14,26},{16,4},{18... | collective-permute-start | bytes 2113544 | tf_op jit(solution)/shard_map/ppermute | solution.py:393
  1303.7 84.9 %collective-permute-start.21 = (bf16[688,512]{1,0:T(8,128)(2,1)}, bf16[688,512]{1,0:T(8,128)(2,1)S(1)}, u32[]{:S(2)}, u32[]{:S(2)}) collective-permute-start(bf16[688,512]{1,0:T(8,128)(2,1)} %reduce-scatter.13.cloned.1.call-done), channel_id=1, source_target_pairs={{0,0},{2,8},{4,16},{6,24},{8,2},{10,10},{12,18},{14,26},{16,4},{18... | collective-permute-start | bytes 2113544 | tf_op jit(solution)/shard_map/ppermute | solution.py:393
  1380.5 9.4 collective-permute-start.22
  1419.4 129.5 %collective-permute-start.13 = (bf16[384,512]{0,1:T(8,128)(2,1)}, bf16[384,512]{0,1:T(8,128)(2,1)S(1)}, u32[]{:S(2)}, u32[]{:S(2)}) collective-permute-start(bf16[384,512]{0,1:T(8,128)(2,1)} %bitcast.31), channel_id=1, source_target_pairs={{0,8},{2,16},{4,24},{6,0},{8,10},{10,18},{12,26},{14,2},{16,12},{1... | collective-permute-start | bytes 1179656 | tf_op jit(solution)/shard_map/ppermute | solution.py:415
  1442.9 106.0 %collective-permute-start.14 = (bf16[384,512]{0,1:T(8,128)(2,1)}, bf16[384,512]{0,1:T(8,128)(2,1)S(1)}, u32[]{:S(2)}, u32[]{:S(2)}) collective-permute-start(bf16[384,512]{0,1:T(8,128)(2,1)} %bitcast.32), channel_id=1, source_target_pairs={{0,16},{2,24},{4,0},{6,8},{8,18},{10,26},{12,2},{14,10},{16,20},{1... | collective-permute-start | bytes 1179656 | tf_op jit(solution)/shard_map/ppermute | solution.py:415
  1476.7 72.2 %collective-permute-start.15 = (bf16[384,512]{0,1:T(8,128)(2,1)}, bf16[384,512]{0,1:T(8,128)(2,1)S(1)}, u32[]{:S(2)}, u32[]{:S(2)}) collective-permute-start(bf16[384,512]{0,1:T(8,128)(2,1)} %bitcast.152), channel_id=1, source_target_pairs={{0,24},{2,0},{4,8},{6,16},{8,26},{10,2},{12,10},{14,18},{16,28},{1... | collective-permute-start | bytes 1179656 | tf_op jit(solution)/shard_map/ppermute | solution.py:415
  1477.4 71.5 %collective-permute-start.12 = (bf16[384,512]{0,1:T(8,128)(2,1)}, bf16[384,512]{0,1:T(8,128)(2,1)}, u32[]{:S(2)}, u32[]{:S(2)}) collective-permute-start(bf16[384,512]{0,1:T(8,128)(2,1)} %bitcast.151), channel_id=1, source_target_pairs={{0,0},{2,8},{4,16},{6,24},{8,2},{10,10},{12,18},{14,26},{16,4},{18... | collective-permute-start | bytes 1179656 | tf_op jit(solution)/shard_map/ppermute | solution.py:415
  1635.2 16.2 collective-permute-start.18
  1636.3 41.8 %collective-permute-start.19 = (bf16[256,512]{1,0:T(8,128)(2,1)S(1)}, bf16[256,512]{1,0:T(8,128)(2,1)S(1)}, u32[]{:S(2)}, u32[]{:S(2)}) collective-permute-start(bf16[256,512]{1,0:T(8,128)(2,1)S(1)} %bitcast.155), channel_id=1, source_target_pairs={{0,16},{2,24},{4,0},{6,8},{8,18},{10,26},{12,2},{14,10},{16,20},{1... | collective-permute-start | bytes 786440 | tf_op jit(solution)/shard_map/ppermute | solution.py:415
  1638.4 39.6 %collective-permute-start.17 = (bf16[256,512]{1,0:T(8,128)(2,1)S(1)}, bf16[256,512]{1,0:T(8,128)(2,1)S(1)}, u32[]{:S(2)}, u32[]{:S(2)}) collective-permute-start(bf16[256,512]{1,0:T(8,128)(2,1)S(1)} %bitcast.154), channel_id=1, source_target_pairs={{0,0},{2,8},{4,16},{6,24},{8,2},{10,10},{12,18},{14,26},{16,4},{18... | collective-permute-start | bytes 786440 | tf_op jit(solution)/shard_map/ppermute | solution.py:415
  (36 other events, 1144.0 us)
Sparse Core Ops, SparseCore 0:
  13.1 202.2 all-gather.14
  217.8 71.8 all-gather.10
  291.6 116.0 all-gather.18
  410.0 117.1 all-gather.16
  600.4 253.6 reduce-scatter.10
  857.5 92.3 reduce-scatter.8
  951.8 104.7 all-gather.12
  1059.0 104.2 reduce-scatter.16
  1165.7 137.9 reduce-scatter.12
  1305.9 74.5 reduce-scatter.14
  1382.8 163.2 reduce-scatter.18
  1547.9 76.5 all-gather.20

commit v2 on v1

--- a/solution.py
+++ b/solution.py
@@ -315,55 +315,61 @@
     )(*scalars, *[a for a, _ in ins])
 
 
+SEQ = ("sy", "sc")
+HEAD = ("ha", "hb")
+
+
+def here():
+    return tuple(lax.axis_index(n) for n in ("sy", "sc", "ha", "hb"))
+
+
+def remote(src, dst, ssem, rsem, k, device):
+    return pltpu.make_async_remote_copy(
+        src_ref=src,
+        dst_ref=dst,
+        send_sem=ssem.at[k],
+        recv_sem=rsem.at[k],
+        device_id=device,
+        device_id_type=MESH_ID,
+    )
+
+
+def greet(devices):
+    bar = pltpu.get_barrier_semaphore()
+    for device in devices:
+        pl.semaphore_signal(bar, 1, device_id=device, device_id_type=MESH_ID)
+    pl.semaphore_wait(bar, len(devices))
+
+
 def exchange_kernel(to_blocks, width, src, dst, ssem, rsem, lsem):
-    s, a, b = lax.axis_index("seq"), lax.axis_index("ha"), lax.axis_index("hb")
+    sy, sc, a, b = here()
     size_a, size_b = lax.axis_size("ha"), lax.axis_size("hb")
     count = size_a * size_b
-    bar = pltpu.get_barrier_semaphore()
-    same = s == a
-
-    def copy(k):
-        base = a if to_blocks else s
-        pa = lax.rem(base + k // size_b, size_a)
-        pb = lax.rem(b + k % size_b, size_b)
+    me = a * size_b + b
+
+    def peer(k):
+        return lax.rem(a + k // size_b, size_a), lax.rem(b + k % size_b, size_b)
+
+    def ends(k):
+        pa, pb = peer(k)
         piece = pa * size_b + pb
         if to_blocks:
-            source = src.at[:, pl.ds(pl.multiple_of(piece * width, 128), width)]
-            place = dst.at[a * size_b + b]
-            target, sender = (pa, s, pb), (a, pa, pb)
-        else:
-            source = src.at[piece]
-            place = dst.at[:, pl.ds(pl.multiple_of((s * size_b + b) * width, 128), width)]
-            target, sender = (a, pa, pb), (pa, s, pb)
-        remote = functools.partial(
-            pltpu.make_async_remote_copy,
-            src_ref=source,
-            dst_ref=place,
-            send_sem=ssem.at[k],
-            recv_sem=rsem.at[k],
-            device_id=target,
-            device_id_type=MESH_ID,
-        )
-        return sender, remote, functools.partial(pltpu.make_async_copy, source, place, lsem)
-
-    def either(k, remote, local):
-        if k:
-            remote()
-        else:
-            pl.when(jnp.logical_not(same))(remote)
-            pl.when(same)(local)
-
-    for k in range(count):
-        sender = copy(k)[0]
-        signal = functools.partial(pl.semaphore_signal, bar, 1, device_id=sender, device_id_type=MESH_ID)
-        either(k, signal, lambda: None)
-    pl.semaphore_wait(bar, jnp.where(same, count - 1, count))
-    for k in range(count):
-        _, remote, local = copy(k)
-        either(k, lambda: remote().start(), lambda: local().start())
-    for k in range(count):
-        _, remote, local = copy(k)
-        either(k, lambda: remote().wait(), lambda: local().wait())
+            return src.at[:, pl.ds(pl.multiple_of(piece * width, 128), width)], dst.at[me]
+        return src.at[piece], dst.at[:, pl.ds(pl.multiple_of(me * width, 128), width)]
+
+    def at(k):
+        pa, pb = peer(k)
+        return sy, sc, pa, pb
+
+    greet([at(k) for k in range(1, count)])
+    copies = [remote(*ends(k), ssem, rsem, k - 1, at(k)) for k in range(1, count)]
+    for copy in copies:
+        copy.start()
+    local = pltpu.make_async_copy(*ends(0), lsem)
+    local.start()
+    local.wait()
+    for copy in copies:
+        copy.wait()
 
 
 def exchange(x, to_blocks, width, collective):
@@ -376,45 +382,325 @@
         in_specs=[pl.BlockSpec(memory_space=pl.ANY)],
         out_specs=pl.BlockSpec(memory_space=pl.ANY),
         scratch_shapes=[
-            pltpu.SemaphoreType.DMA((count,)),
-            pltpu.SemaphoreType.DMA((count,)),
+            pltpu.SemaphoreType.DMA((count - 1,)),
+            pltpu.SemaphoreType.DMA((count - 1,)),
             pltpu.SemaphoreType.DMA,
         ],
         compiler_params=pltpu.CompilerParams(collective_id=collective, has_side_effects=True),
-        cost_estimate=pl.CostEstimate(flops=0, bytes_accessed=x.size * 2, transcendentals=0),
+        cost_estimate=pl.CostEstimate(flops=0, bytes_accessed=x.size * 500, transcendentals=0),
     )(x)
 
 
-def transpose_perm(size):
-    return [(s * size + z, z * size + s) for s in range(size) for z in range(size)]
-
-
-def swap_home(x):
-    return lax.ppermute(x, ("seq", "ha"), transpose_perm(lax.axis_size("seq")))
+def gather_kernel(arrays, *refs):
+    srcs, dsts, (ssem, rsem, lsem) = refs[:arrays], refs[arrays : 2 * arrays], refs[2 * arrays :]
+    sy, sc, a, b = here()
+    size = lax.axis_size("ha")
+    to_up, to_down, to_side = (sy, sc, a + 1, b), (sy, sc, a - 1, b), (sy, sc, a, 1 - b)
+    has_up, has_down = a < size - 1, a > 0
+    bar = pltpu.get_barrier_semaphore()
+
+    def signal(device):
+        pl.semaphore_signal(bar, 1, device_id=device, device_id_type=MESH_ID)
+
+    def send(n, k, pa, device):
+        ref = dsts[n].at[pa * 2 + b]
+        return remote(ref, ref, ssem, rsem, 3 * size * n + k, device)
+
+    local = [pltpu.make_async_copy(s, d.at[a * 2 + b], lsem.at[n]) for n, (s, d) in enumerate(zip(srcs, dsts))]
+    for copy in local:
+        copy.start()
+    pl.when(has_up)(lambda: signal(to_up))
+    pl.when(has_down)(lambda: signal(to_down))
+    signal(to_side)
+    pl.semaphore_wait(bar, 1 + has_up.astype(jnp.int32) + has_down.astype(jnp.int32))
+    for copy in local:
+        copy.wait()
+
+    def spread(n, k, pa, up, down):
+        if up:
+            pl.when(has_up)(lambda: send(n, k, pa, to_up).start())
+        if down:
+            pl.when(has_down)(lambda: send(n, size + k, pa, to_down).start())
+        send(n, 2 * size + pa, pa, to_side).start()
+
+    for n in range(arrays):
+        spread(n, 0, a, True, True)
+    for k in range(1, size):
+        for n in range(arrays):
+
+            @pl.when(a - k >= 0)
+            def _():
+                send(n, k - 1, a - k, to_side).wait_recv()
+                spread(n, k, a - k, True, False)
+
+            @pl.when(a + k < size)
+            def _():
+                send(n, size + k - 1, a + k, to_side).wait_recv()
+                spread(n, k, a + k, False, True)
+
+    for n in range(arrays):
+        for k in range(size):
+            ref = dsts[n].at[k * 2 + 1 - b]
+            remote(ref, ref, ssem, rsem, 3 * size * n + 2 * size + k, to_side).wait_recv()
+        for k in range(size):
+            send(n, 2 * size + k, k, to_side).wait_send()
+            pl.when(jnp.logical_and(has_up, a - k >= 0))(lambda: send(n, k, a - k, to_side).wait_send())
+            pl.when(jnp.logical_and(has_down, a + k < size))(
+                lambda: send(n, size + k, a + k, to_side).wait_send()
+            )
+
+
+def gather_block(xs, collective):
+    if (lax.axis_size("ha"), lax.axis_size("hb")) != (4, 2):
+        return [lax.all_gather(x, HEAD, axis=0) for x in xs]
+    n = len(xs)
+    return pl.pallas_call(
+        functools.partial(gather_kernel, n),
+        out_shape=[jax.ShapeDtypeStruct((8,) + x.shape, x.dtype) for x in xs],
+        in_specs=[pl.BlockSpec(memory_space=pl.ANY)] * n,
+        out_specs=[pl.BlockSpec(memory_space=pl.ANY)] * n,
+        scratch_shapes=[
+            pltpu.SemaphoreType.DMA((12 * n,)),
+            pltpu.SemaphoreType.DMA((12 * n,)),
+            pltpu.SemaphoreType.DMA((n,)),
+        ],
+        compiler_params=pltpu.CompilerParams(collective_id=collective, has_side_effects=True),
+        cost_estimate=pl.CostEstimate(flops=0, bytes_accessed=xs[0].size * 600, transcendentals=0),
+    )(*xs)
+
+
+def swap(x, axis):
+    return lax.ppermute(x, axis, [(0, 1), (1, 0)])
 
 
 def chain_pieces(x, backward):
-    size = lax.axis_size("ha")
+    size = lax.axis_size("sy") * 2
     out = []
     for k in range(1, size):
         if backward:
             perm = [(i, i - k) for i in range(k, size)]
         else:
             perm = [(i, i + k) for i in range(size - k)]
-        out.append(lax.ppermute(x, "ha", perm))
+        out.append(lax.ppermute(x, SEQ, perm))
     return out
 
 
-def sum_home(x):
-    size = lax.axis_size("ha")
-    a = lax.axis_index("ha")
+def tie(x, *after):
+    return lax.optimization_barrier((x, *jax.tree.leaves(after)))[0]
+
+
+def my_columns(x):
+    size = x.shape[1] // (lax.axis_size("sy") * 2)
+    place = lax.axis_index("sy") * 2 + lax.axis_index("sc")
+    return lax.dynamic_slice_in_dim(x, place * size, size, 1)
+
+
+def seq_pieces(x):
+    if lax.axis_size("sy") != 2:
+        return list(lax.all_gather(x, SEQ, axis=0))
+    along_y = swap(x, "sy")
+    other, other_y = swap(x, "sc"), swap(along_y, "sc")
+    return [x, along_y, other, other_y]
+
+
+def piece_places(count):
+    if lax.axis_size("sy") != 2:
+        return list(range(count))
+    y, c = lax.axis_index("sy"), lax.axis_index("sc")
+    return [y * 2 + c, (1 - y) * 2 + c, y * 2 + 1 - c, (1 - y) * 2 + 1 - c]
+
+
+def by_columns(a, pieces):
+    parts = [dot(a, p) for p in pieces]
+    if lax.axis_size("sy") == 2:
+        y, c = lax.axis_index("sy") == 0, lax.axis_index("sc") == 0
+        rows = [(jnp.where(y, parts[k], parts[k + 1]), jnp.where(y, parts[k + 1], parts[k])) for k in (0, 2)]
+        parts = []
+        for own, other in zip(*rows):
+            parts += [jnp.where(c, own, other), jnp.where(c, other, own)]
+    return jnp.concatenate(parts, axis=1)
+
+
+def by_columns_back(a, pieces):
+    size = pieces[0].shape[1]
     total = None
-    for k in range(size):
-        block = lax.dynamic_index_in_dim(x, lax.rem(a + k, size), 0, False)
-        perm = [(s * size + z, ((z + k) % size) * size + s) for s in range(size) for z in range(size)]
-        got = lax.ppermute(block, ("seq", "ha"), perm).astype(F32)
-        total = got if total is None else total + got
+    for p, place in zip(pieces, piece_places(len(pieces))):
+        part = dot(lax.dynamic_slice_in_dim(a, place * size, size, 1), p, NT)
+        total = part if total is None else total + part
     return total
+
+
+def unit_window(x, size):
+    units = x.shape[0]
+    window = -(-units // (size * 16)) * 16
+    place = lax.axis_index("sy") * 2 + lax.axis_index("sc")
+    start = jnp.minimum(place * window, units - window)
+    part = lax.dynamic_slice_in_dim(x, start, window, 0)
+    fresh = start + lax.broadcasted_iota(jnp.int32, part.shape, 0) >= place * window
+    return jnp.where(fresh, part, jnp.zeros_like(part))
+
+
+def windows_joined(parts, units):
+    size, window = parts.shape[0], parts.shape[1]
+    pieces = []
+    for i in range(size):
+        start = min(i * window, units - window)
+        pieces.append(parts[i, max(i * window - start, 0) :])
+    return jnp.concatenate(pieces, axis=0)
+
+
+def ff_kernel(meta, n2, cot, mine, theirs, *rest):
+    gg_out, gu_out, hid_out, n2_out, cot_out, part_out, acc = rest[-7:]
+    shard = pl.program_id(0)
+
+    def work(w, first):
+        x, c = n2[...], cot[...]
+        units, width = w.shape[0] * w.shape[2], w.shape[3]
+        w_gate, w_up, w_down = (w[:, i].reshape(units, width) for i in range(3))
+        gate, up, gh = dot(x, w_gate, NT), dot(x, w_up, NT), dot(c, w_down, NT)
+        sig = jax.nn.sigmoid(gate)
+        act = gate * sig
+        hid_out[0, 0] = (act * up).astype(BF)
+        gg = (gh * up * (sig + act * (1.0 - sig))).astype(BF)
+        gu = (gh * act).astype(BF)
+        gg_out[0, 0] = gg
+        gu_out[0, 0] = gu
+        back = dot(gg, w_gate) + dot(gu, w_up)
+        if first:
+            acc[...] = back
+            n2_out[0] = x
+            cot_out[0] = c
+        else:
+            part_out[...] = (acc[...] + back).astype(BF)
+
+    @pl.when(shard == 0)
+    def _():
+        work(mine, True)
+
+    @pl.when(shard == 1)
+    def _():
+        work(theirs, False)
+
+
+def ff_chunk(n2, cot, mine, theirs, place, chunks, kept):
+    tokens, width = n2.shape
+    units = mine.shape[0] * mine.shape[2]
+    keep = jax.ShapeDtypeStruct((2, chunks, tokens, units), BF)
+    held_shape = jax.ShapeDtypeStruct((chunks, tokens, width), BF)
+    whole = pl.BlockSpec((tokens, width), lambda i, m: (0, 0))
+    weights = pl.BlockSpec(mine.shape, lambda i, m: (0, 0, 0, 0), pipeline_mode=pl.Buffered(1))
+    piece = pl.BlockSpec((1, 1, tokens, units), lambda i, m: (i, m[0], 0, 0))
+    held = pl.BlockSpec((1, tokens, width), lambda i, m: (m[0], 0, 0))
+    old = [] if kept is None else list(kept)
+    return pl.pallas_call(
+        ff_kernel,
+        out_shape=(keep, keep, keep, held_shape, held_shape, jax.ShapeDtypeStruct((tokens, width), BF)),
+        grid_spec=pltpu.PrefetchScalarGridSpec(
+            num_scalar_prefetch=1,
+            grid=(2,),
+            in_specs=[whole, whole, weights, weights] + [pl.BlockSpec(memory_space=pl.ANY)] * len(old),
+            out_specs=[piece, piece, piece, held, held, whole],
+            scratch_shapes=[pltpu.VMEM((tokens, width), F32)],
+        ),
+        input_output_aliases={5 + i: i for i in range(len(old))},
+        compiler_params=pltpu.CompilerParams(vmem_limit_bytes=58 * 1024 * 1024),
+        cost_estimate=pl.CostEstimate(
+            flops=tokens * width * units * 20,
+            bytes_accessed=12 * units * width + 8 * tokens * width,
+            transcendentals=0,
+        ),
+    )(place, n2, cot, mine, theirs, *old)
+
+
+def branch_kernel(hidden, mine, theirs, out):
+    width = out.shape[1]
+    part = dot(hidden[0, 0], mine[:, 0].reshape(-1, width)) + dot(hidden[1, 0], theirs[:, 0].reshape(-1, width))
+    out[...] = part.astype(BF)
+
+
+def branch_product(hidden, mine, theirs):
+    _, chunks, tokens, units = hidden.shape
+    width = mine.shape[3]
+    weights = pl.BlockSpec(
+        (mine.shape[0], 1) + mine.shape[2:], lambda i: (0, 2, 0, 0), pipeline_mode=pl.Buffered(1)
+    )
+    return pl.pallas_call(
+        branch_kernel,
+        out_shape=jax.ShapeDtypeStruct((chunks * tokens, width), BF),
+        grid=(chunks,),
+        in_specs=[pl.BlockSpec((2, 1, tokens, units), lambda i: (0, i, 0, 0)), weights, weights],
+        out_specs=pl.BlockSpec((tokens, width), lambda i: (i, 0)),
+        compiler_params=pltpu.CompilerParams(vmem_limit_bytes=40 * 1024 * 1024),
+        cost_estimate=pl.CostEstimate(
+            flops=chunks * tokens * units * width * 4, bytes_accessed=12 * units * width, transcendentals=0
+        ),
+    )(hidden, mine, theirs)
+
+
+QUAD = ("sy", "hb")
+
+
+def ring_gather(x):
+    half = x.shape[0] // 2
+    from_x, from_y = swap(x, "hb"), swap(x, "sy")
+    across = jnp.concatenate([swap(from_y[:half], "hb"), swap(from_x[half:], "sy")], axis=0)
+    return x, from_x, from_y, across
+
+
+def add_low(a, b):
+    return (a.astype(F32) + b.astype(F32)).astype(BF)
+
+
+def ring_sum(parts, meanwhile=lambda stage: ()):
+    own, to_x, to_y, across = parts
+    half = own.shape[0] // 2
+    via_x, via_y = swap(across[:half], "hb"), swap(across[half:], "sy")
+    x_low, y_high = swap(to_x[:half], "hb"), swap(to_y[half:], "sy")
+    work = meanwhile(0)
+    via_x, via_y = tie(via_x, *work), tie(via_y, *work)
+    y_low = swap(add_low(to_y[:half], via_x), "sy")
+    x_high = swap(add_low(to_x[half:], via_y), "hb")
+    work = meanwhile(1)
+    y_low, x_high = tie(y_low, *work), tie(x_high, *work)
+    low = own[:half].astype(F32) + x_low.astype(F32) + y_low.astype(F32)
+    high = own[half:].astype(F32) + x_high.astype(F32) + y_high.astype(F32)
+    return jnp.concatenate([low, high], axis=0)
+
+
+def quad_gather(x):
+    if (lax.axis_size("sy"), lax.axis_size("hb")) == (2, 2):
+        return ring_gather(x)
+    return (lax.all_gather(x, QUAD, axis=0, tiled=True),)
+
+
+def quad_sum(parts, meanwhile=lambda stage: ()):
+    if len(parts) == 4:
+        return ring_sum(parts, meanwhile)
+    for stage in (0, 1):
+        meanwhile(stage)
+    return lax.psum_scatter(parts[0], QUAD, scatter_dimension=0, tiled=True).astype(F32)
+
+
+def ff_group(n2, cots, mine, theirs):
+    kept, parts = None, []
+    for i, (chunk, cot) in enumerate(zip(quad_gather(n2), cots)):
+        place = jnp.full((1,), i, jnp.int32)
+        *kept, part = ff_chunk(chunk, cot, mine, theirs, place, len(cots), kept)
+        parts.append(part)
+    grads, branch = [], []
+    flat = [k.reshape((2, -1, k.shape[-1]) if k.ndim == 4 else (-1, k.shape[-1])) for k in kept]
+    pairs = [(flat[0], flat[3]), (flat[1], flat[3]), (flat[2], flat[4])]
+
+    def meanwhile(stage):
+        if stage == 0:
+            grads.extend(swap(dot(a[1], b, TN).astype(BF), "sc") for a, b in pairs)
+            return grads
+        for i, (a, b) in enumerate(pairs):
+            grads[i] = (dot(a[0], b, TN) + grads[i].astype(F32)).astype(BF)
+        branch.append(branch_product(kept[2], mine, theirs))
+        return grads + branch
+
+    return quad_sum(parts, meanwhile), grads, branch[0]
 
 
 def rms_scale(x):
@@ -436,9 +722,10 @@
     cotangent,
     doc_lengths,
 ):
-    blocks = lax.axis_size("seq")
-    group = ("seq", "hb")
-    count = blocks * lax.axis_size("hb")
+    every = ("sy", "sc", "ha", "hb")
+    blocks = lax.axis_size("sy") * 2
+    size_a, size_b = lax.axis_size("ha"), lax.axis_size("hb")
+    count = size_a * size_b
     sub_len, rows_n, width = inputs.shape
     docs = doc_lengths.shape[1]
     nh = w_query.shape[1] // FEAT
@@ -447,7 +734,7 @@
     xw = vw + 128
     length = sub_len * count
     tokens = rows_n * sub_len
-    meta = lax.axis_index("ha").astype(jnp.int32).reshape(1)
+    meta = (lax.axis_index("sy") * 2 + lax.axis_index("sc")).astype(jnp.int32).reshape(1)
     pa, pb, frows, align = feature_tables(nh)
     scalars = (doc_lengths, meta)
 
@@ -455,14 +742,17 @@
     cot = jnp.transpose(cotangent, (1, 0, 2))
     scale_one = rms_scale(x)
     normed_one = x * scale_one
-    normed_low = (normed_one * attn_gain).astype(BF)
-    normed_full = lax.all_gather(swap_home(normed_low), group, axis=0)
     pad = jnp.zeros((128 - 2 * nh * FEAT, width), BF)
-    w_in = swap_home(jnp.concatenate([w_value.T, w_query.T, w_key.T, pad], axis=0))
-    w_out_home = swap_home(w_out)
-    gate_t, up_t, down = swap_home(gate_weight.T), swap_home(up_weight.T), swap_home(down_weight)
-    w_out_full = lax.all_gather(w_out_home, group, axis=0, tiled=True)
-    w_in_full = lax.all_gather(w_in, group, axis=0, tiled=True)
+    w_in = jnp.concatenate([w_value.T, w_query.T, w_key.T, pad], axis=0)
+    units = down_weight.shape[0]
+    windows = [unit_window(w, blocks) for w in (gate_weight.T, up_weight.T, down_weight)]
+    w_in_piece = my_columns(w_in)
+    to_fetch = jnp.concatenate(windows + [w_in_piece.reshape(-1, width)], axis=0)
+    normed_full, w_out_piece = gather_block([(normed_one * attn_gain).astype(BF), my_columns(w_out)], 3)
+    fetched = lax.all_gather(tie(to_fetch, normed_full), "ha", axis=0)
+    w_out_pieces = seq_pieces(w_out_piece.reshape(-1, w_out_piece.shape[-1]))
+    window = windows[0].shape[0]
+    mine = fetched[:, : 3 * window].reshape(size_a, 3, window, width)
 
     qkv = jnp.einsum("grtd,cd->grtc", normed_full, w_in, preferred_element_type=F32).astype(BF)
     pair = nh * rows_n * length * length
@@ -487,7 +777,7 @@
         functools.partial(attend_kernel, nh, vd, docs, blocks),
         rows_n,
         scalars,
-        [(qkv, 1), (num, 0), (den, 0), (pa, None), (pb, None), (frows, None)]
+        [(qkv, 1), (tie(num, w_out_pieces), 0), (den, 0), (pa, None), (pb, None), (frows, None)]
         + [(e, 0) for e in earlier],
         [
             ((count, rows_n, sub_len, vw), BF, 1),
@@ -496,36 +786,19 @@
         ],
         nh * rows_n * length * 256 * 256 * 6,
     )
-    attended = exchange(att.reshape(count, tokens, vw), False, vw, 0)
-    attn_branch = dot(attended, w_out_full).reshape(rows_n, sub_len, width)
+    flat_cot = tie(cot.reshape(tokens, width), earlier)
+    cots = quad_gather(flat_cot)
+    attended = exchange(tie(att, cots).reshape(count, tokens, vw), False, vw, 0)
+    attn_branch = by_columns(attended, w_out_pieces).reshape(rows_n, sub_len, width)
     middle = x + attn_branch + out_bias
     scale_two = rms_scale(middle)
     normed_two = middle * scale_two
     normed_two_low = (normed_two * mlp_gain).astype(BF)
 
-    n2f = lax.all_gather(normed_two_low, group, axis=0).reshape(count * tokens, width)
-    cotf = lax.all_gather(cot, group, axis=0).reshape(count * tokens, width)
-    gate = dot(n2f, gate_t, NT)
-    up = dot(n2f, up_t, NT)
-    sig = jax.nn.sigmoid(gate)
-    hidden = (gate * sig * up).astype(BF)
-    grad_hidden = dot(cotf, down, NT)
-    grad_gate = (grad_hidden * up * sig * (1.0 + gate * (1.0 - sig))).astype(BF)
-    grad_up = (grad_hidden * gate * sig).astype(BF)
-    grad_two = (dot(grad_gate, gate_t) + dot(grad_up, up_t)).astype(BF)
-    grad_two = (
-        lax.psum_scatter(grad_two, group, scatter_dimension=0, tiled=True)
-        .astype(F32)
-        .reshape(rows_n, sub_len, width)
-    )
-    branch = dot(hidden, down).astype(BF)
-    branch = (
-        lax.psum_scatter(branch, group, scatter_dimension=0, tiled=True)
-        .astype(F32)
-        .reshape(rows_n, sub_len, width)
-    )
-    output = (middle + branch).astype(BF)
-
+    theirs = swap(tie(mine, attended), "sc")
+    n2 = normed_two_low.reshape(tokens, width)
+    grad_two, ff_grads, branch = ff_group(n2, cots, mine, theirs)
+    grad_two = grad_two.reshape(rows_n, sub_len, width)
     gain_two_part = jnp.sum(grad_two * normed_two, axis=(0, 1))
     scaled = grad_two * mlp_gain
     grad_middle = cot.astype(F32) + scale_two * (
@@ -534,8 +807,18 @@
     bias_part = jnp.sum(grad_middle, axis=(0, 1))
     grad_branch = grad_middle.astype(BF)
 
-    grad_att = dot(grad_branch.reshape(tokens, width), w_out_full, NT).astype(BF)
+    flat_branch = grad_branch.reshape(tokens, width)
+    grad_att = by_columns_back(flat_branch, w_out_pieces).astype(BF)
+    step = branch.shape[0] // len(cots)
+    branch = tie(branch, grad_att)
+    branch = quad_sum([branch[i * step : (i + 1) * step] for i in range(len(cots))])
+    output = (middle + branch.reshape(rows_n, sub_len, width)).astype(BF)
     grad_att = exchange(grad_att, True, vw, 1).reshape(count, rows_n, sub_len, vw)
+    near = tie(fetched[:, 3 * window :].reshape((size_a,) + w_in_piece.shape), grad_att)
+    side = lax.axis_index("hb") == 0
+    aside = swap(near, "hb")
+    w_in_piece = jnp.stack([jnp.where(side, near, aside), jnp.where(side, aside, near)], axis=1)
+    w_in_pieces = seq_pieces(w_in_piece.reshape(-1, w_in_piece.shape[-1]))
     gn, grad_states = row_call(
         functools.partial(back_state_kernel, nh, vd, docs),
         rows_n,
@@ -562,7 +845,7 @@
         nh * rows_n * length * 256 * 256 * 6,
     )
     grad_in = exchange(gqkv.reshape(count, tokens, xw), False, xw, 2)
-    grad_one = dot(grad_in, w_in_full).reshape(rows_n, sub_len, width)
+    grad_one = by_columns(grad_in, w_in_pieces).reshape(rows_n, sub_len, width)
     gain_one_part = jnp.sum(grad_one * normed_one, axis=(0, 1))
     scaled = grad_one * attn_gain
     input_grad = (
@@ -570,27 +853,49 @@
         + scale_one * (scaled - normed_one * jnp.mean(scaled * normed_one, axis=-1, keepdims=True))
     ).astype(BF)
 
+    def seq_sum(a, b):
+        part = dot(a, b, TN).astype(BF).reshape(a.shape[1], blocks // 2, 2, width // blocks)
+        core = lax.axis_index("sc")
+        ours, given = (
+            lax.dynamic_index_in_dim(part, i, 2, False).reshape(a.shape[1], -1) for i in (core, 1 - core)
+        )
+        part = add_low(ours, swap(given, "sc"))
+        if lax.axis_size("sy") != 2:
+            return lax.psum_scatter(part, "sy", scatter_dimension=1, tiled=True)
+        y = lax.axis_index("sy")
+        size = width // blocks
+        kept, sent = (lax.dynamic_slice_in_dim(part, i * size, size, 1) for i in (y, 1 - y))
+        return (kept.astype(F32) + swap(sent, "sy").astype(F32)).astype(BF)
+
     flat_tokens = count * tokens
-    grad_w_in = dot(gqkv.reshape(flat_tokens, xw), normed_full.reshape(flat_tokens, width), TN)
-    grad_w_in = sum_home(
-        jnp.transpose(grad_w_in.astype(BF).reshape(xw, blocks, width // blocks), (1, 0, 2))
-    )
-    branch_full = lax.all_gather(swap_home(grad_branch), group, axis=0).reshape(flat_tokens, width)
-    grad_w_out = dot(att.reshape(flat_tokens, vw), branch_full, TN)
-    grad_w_out = sum_home(
-        jnp.transpose(grad_w_out.astype(BF).reshape(vw, blocks, width // blocks), (1, 0, 2))
-    )
-
-    def ff_grad(a, b):
-        part = dot(a, b, TN).astype(BF)
-        part = lax.psum_scatter(part, "ha", scatter_dimension=1, tiled=True)
-        return swap_home(part).astype(F32)
-
-    grad_gate_w = ff_grad(grad_gate, n2f)
-    grad_up_w = ff_grad(grad_up, n2f)
-    grad_down_w = ff_grad(hidden, cotf)
+    grad_w_in = seq_sum(gqkv.reshape(flat_tokens, xw), normed_full.reshape(flat_tokens, width)).astype(F32)
+    grad_w_out = seq_sum(attended, flat_branch)
+
+    def ff_home(part):
+        part = lax.psum_scatter(part, "ha", scatter_dimension=0, tiled=True)
+        part = part.reshape(part.shape[0], blocks, width // blocks)
+        part = lax.all_to_all(jnp.transpose(part, (1, 0, 2)), SEQ, 0, 0, tiled=True)
+        return windows_joined(part.astype(F32), units)
+
+    grad_gate_w, grad_up_w, grad_down_w = (ff_home(g) for g in ff_grads)
+    grad_w_out = tie(grad_w_out, grad_down_w)
+    grad_w_out = lax.psum_scatter(grad_w_out, HEAD, scatter_dimension=0, tiled=True).astype(F32)
     vectors = jnp.stack([gain_one_part, bias_part, gain_two_part])
-    vectors = lax.psum_scatter(vectors, ("seq", "ha", "hb"), scatter_dimension=1, tiled=True)
+    if (lax.axis_size("sy"), size_a, size_b) == (2, 4, 2):
+        vectors = vectors.reshape(3, 2, 2, 4, 2, -1)
+        for axis, where in (("sc", 2), ("sy", 1), ("hb", 4)):
+            i = lax.axis_index(axis)
+            given = swap(lax.dynamic_slice_in_dim(vectors, 1 - i, 1, where), axis)
+            vectors = lax.dynamic_slice_in_dim(vectors, i, 1, where) + given
+        vectors = vectors.reshape(3, 4, -1)
+        i = lax.axis_index("ha")
+        total = lax.dynamic_index_in_dim(vectors, i, 1, False)
+        for k in range(1, 4):
+            piece = lax.dynamic_index_in_dim(vectors, lax.rem(i + k, 4), 1, False)
+            total = total + lax.ppermute(piece, "ha", [(z, (z + k) % 4) for z in range(4)])
+        vectors = total
+    else:
+        vectors = lax.psum_scatter(vectors, every, scatter_dimension=1, tiled=True)
     qk_cut = vw + nh * FEAT
     return (
         jnp.transpose(output, (1, 0, 2)),
@@ -610,8 +915,8 @@
 
 def solution(mesh):
     seq, head = mesh.shape["seq"], mesh.shape["head"]
-    inner = Mesh(mesh.devices.reshape(seq, seq, head // seq), ("seq", "ha", "hb"))
-    every, heads = ("seq", "ha", "hb"), ("ha", "hb")
+    inner = Mesh(mesh.devices.reshape(seq // 2, 2, seq, head // seq), ("sy", "sc", "ha", "hb"))
+    every, heads = ("sy", "sc", "ha", "hb"), ("ha", "hb")
     placed = (
         P(every, None, None),
         P(),
@@ -635,15 +940,15 @@
             P(every, None, None),
             P(every, None, None),
             P(every),
-            P("seq", heads),
-            P("seq", heads),
-            P("seq", heads),
-            P(heads, "seq"),
+            P(SEQ, heads),
+            P(SEQ, heads),
+            P(SEQ, heads),
+            P(heads, SEQ),
             P(every),
             P(every),
-            P("seq", heads),
-            P("seq", heads),
-            P(heads, "seq"),
+            P(SEQ, heads),
+            P(SEQ, heads),
+            P(heads, SEQ),
         ),
         check_vma=False,
     )

time: 1700 us -> 1290 us (0.76)
  waiting for transfers between devices: 931 us -> 350 us
  Pallas kernels: 312 us -> 574 us
  matrix products: 198 us -> 107 us
  starting transfers between devices: 161 us -> 73.3 us
  local copies, waits for them, and re-layouts: 38.6 us -> 91.2 us
  other arithmetic: 29.3 us -> 73.6 us
    all_gather x6 -> x1, waiting for transfers between devices: 401 us -> 32 us  [on_device(): fetched = lax.all_gather(tie(to_fetch, normed_full), 'ha', axis=0)]
    reduce_scatter x5 -> x4, waiting for transfers between devices: 392 us -> 40.4 us  [the longest x1 40.4 us: on_device(): lax.psum_scatter(grad_w_out, HEAD, scatter_dimension=0, tiled=True)]
    pallas_call x0 -> x6, Pallas kernels: none -> 332 us  [the longest x1 218 us: gather_block(): pl.pallas_call(functools.partial(gather_kernel, n), out_shape=[jax.ShapeD...]
    ppermute x24 -> x47, waiting for transfers between devices: 77.3 us -> 191 us  [the longest x38 150 us: swap(): return lax.ppermute(x, axis, [(0, 1), (1, 0)])]
    ppermute x24 -> x47, starting transfers between devices: 161 us -> 61 us  [the longest x38 36.4 us: swap(): return lax.ppermute(x, axis, [(0, 1), (1, 0)])]
    dot_general x14 -> x20, matrix products: 188 us -> 96.3 us  [dot(): return lax.dot_general(a, b, dims, preferred_element_type=F32)]
    all_to_all x0 -> x3, waiting for transfers between devices: none -> 86.5 us  [ff_home(): part = lax.all_to_all(jnp.transpose(part, (1, 0, 2)), SEQ, 0, 0, tiled=True)]
    pallas_call x3, Pallas kernels: 245 us -> 174 us  [exchange(): pl.pallas_call(functools.partial(exchange_kernel, to_blocks, width), out_...]
  transfers between devices with their start and end apart: 36 -> 55, of which waited for: 14 -> 21; matrix products, arithmetic and copies ran while one was open for 11% -> 17% of each run, Pallas kernels for 19% -> 20%
where the time goes in v2:
time: 1290 us; the launch traced here: 1280 us
  Pallas kernels  574 us (44%)
  waiting for transfers between devices  350 us (27%)
  matrix products  107 us (8%)
  local copies, waits for them, and re-layouts  91.2 us (7%)
  other arithmetic  73.6 us (6%)
  starting transfers between devices  73.3 us (6%)
  between operations  15.2 us (1%)
    pallas_call x1, Pallas kernels, gather_block(): pl.pallas_call(functools.partial(gather_kernel, n), out_shape=[jax.ShapeD...  218 us
    pallas_call x3, Pallas kernels, exchange(): pl.pallas_call(functools.partial(exchange_kernel, to_blocks, width), out_...  174 us
    ppermute x38, waiting for transfers between devices, swap(): return lax.ppermute(x, axis, [(0, 1), (1, 0)])  150 us
    pallas_call x4, Pallas kernels, ff_chunk(): pl.pallas_call(ff_kernel, out_shape=(keep, keep, keep, held_shape, held_s...  99.5 us
    dot_general x20, matrix products, dot(): return lax.dot_general(a, b, dims, preferred_element_type=F32)  96.3 us
    all_to_all x3, waiting for transfers between devices, ff_home(): part = lax.all_to_all(jnp.transpose(part, (1, 0, 2)), SEQ, 0, 0, tiled=True)  86.5 us
    pallas_call x6, Pallas kernels, row_call(): pl.pallas_call(kernel, out_shape=tuple((jax.ShapeDtypeStruct(s, t) for s,...  68.4 us
    ppermute x6, waiting for transfers between devices, chain_pieces(): out.append(lax.ppermute(x, SEQ, perm))  40.8 us
  transfers between devices with their start and end apart: 55, of which 21 were waited for; matrix products, arithmetic and copies ran while one was open for 17% of the time, Pallas kernels for 20%

profile of v2, /device:TPU:0, one launch (start us, length us, event | category | flops | bytes accessed | tf_op | source)
XLA Modules:
  0.0 1284.3 jit_solution(4878673374476934781)
XLA Ops:
  18.7 218.4 %shard_map.256 = (bf16[8,3,128,2048]{3,2,1,0:T(8,128)(2,1)}, bf16[8,256,512]{2,1,0:T(8,128)(2,1)}) custom-call(bf16[3,128,2048]{2,1,0:T(8,128)(2,1)} %fusion.4.refs_0_, bf16[256,512]{1,0:T(8,128)(2,1)} %constant_dynamic-slice_fusion.14.refs_1_), custom_call_target="tpu_custom_call" | custom-call | bytes 471859200 | tf_op jit(solution)/shard_map/pallas_call | solution.py:457
  241.6 10.9 convolution_convert_fusion.4.x_ref
  264.2 32.8 %collective-permute-done.5.rest_2_ = bf16[3,2,136,256]{3,2,1,0:T(8,128)(2,1)S(1)} collective-permute-done((bf16[3,2,136,256]{3,2,1,0:T(8,128)(2,1)}, bf16[3,2,136,256]{3,2,1,0:T(8,128)(2,1)S(1)}, u32[]{:S(2)}, u32[]{:S(2)}) %collective-permute-start.5) | collective-permute-done | bytes 417824 | tf_op jit(solution)/shard_map/ppermute | solution.py:484
  308.5 30.4 %collective-permute-done.7.cot = bf16[384,2048]{1,0:T(8,128)(2,1)S(1)} collective-permute-done((bf16[384,2048]{1,0:T(8,128)(2,1)}, bf16[384,2048]{1,0:T(8,128)(2,1)S(1)}, u32[]{:S(2)}, u32[]{:S(2)}) %collective-permute-start.7) | collective-permute-done | bytes 1572896 | tf_op jit(solution)/shard_map/ppermute | solution.py:473
  345.1 10.8 shard_map.257
  357.6 9.7 shard_map.259
  367.3 54.4 %shard_map.260 = bf16[384,2048]{1,0:T(8,128)(2,1)} custom-call(bf16[8,384,256]{2,1,0:T(8,128)(2,1)} %bitcast.238), custom_call_target="tpu_custom_call" | custom-call | bytes 393216000 | tf_op jit(solution)/shard_map/pallas_call | solution.py:379
  421.7 32.0 %all-gather.3.cloned.1.call-done = bf16[2496,2048]{1,0:T(8,128)(2,1)} async-done(((bf16[624,2048]{1,0:T(8,128)(2,1)}), bf16[2496,2048]{1,0:T(8,128)(2,1)}) %all-gather.3.cloned.1.call-update) | async-done | bytes 10223632 | tf_op jit(solution)/shard_map/all_gather | solution.py:752
  453.7 8.5 slice.206
  476.9 33.8 %collective-permute-done.12.n2 = bf16[384,2048]{1,0:T(8,128)(2,1)S(1)} collective-permute-done((bf16[384,2048]{1,0:T(8,128)(2,1)S(1)}, bf16[384,2048]{1,0:T(8,128)(2,1)S(1)}, u32[]{:S(2)}, u32[]{:S(2)}) %collective-permute-start.12) | collective-permute-done | bytes 1572896 | tf_op jit(solution)/shard_map/ppermute | solution.py:473
  513.9 16.0 %collective-permute-done.13 = bf16[192,2048]{1,0:T(8,128)(2,1)S(1)} collective-permute-done((bf16[192,2048]{1,0:T(8,128)(2,1)S(1)}, bf16[192,2048]{1,0:T(8,128)(2,1)S(1)}, u32[]{:S(2)}, u32[]{:S(2)}) %collective-permute-start.13) | collective-permute-done | bytes 786464 | tf_op jit(solution)/shard_map/ppermute | solution.py:473
  532.5 24.8 %shard_map.261 = (bf16[2,4,384,704]{3,2,1,0:T(8,128)(2,1)}, bf16[2,4,384,704]{3,2,1,0:T(8,128)(2,1)}, bf16[2,4,384,704]{3,2,1,0:T(8,128)(2,1)}, bf16[4,384,2048]...) custom-call(s32[1]{0:T(128)} %constant.94.clone.1.meta, bf16[384,2048]{1,0:T(8,128)(2,1)} %bitcast.259, ...), custom_call_target="tpu_custom_call" | custom-call | flops 11072962560 | bytes 23592960 | tf_op jit(solution)/shard_map/pallas_call | solution.py:595
  557.4 25.0 %shard_map.262 = (bf16[2,4,384,704]{3,2,1,0:T(8,128)(2,1)}, bf16[2,4,384,704]{3,2,1,0:T(8,128)(2,1)}, bf16[2,4,384,704]{3,2,1,0:T(8,128)(2,1)}, bf16[4,384,2048]...) custom-call(s32[1]{0:T(128)} %constant.93.clone.1.meta, ...), custom_call_target="tpu_custom_call", output_to_operand_aliasing={{0}: (5, {}), {1}: (6, {}), {2}: (7, {}), {3}: (8, {}), {4}... | custom-call | flops 11072962560 | bytes 23592960 | tf_op jit(solution)/shard_map/pallas_call | solution.py:595
  582.4 24.8 %shard_map.263 = (bf16[2,4,384,704]{3,2,1,0:T(8,128)(2,1)}, bf16[2,4,384,704]{3,2,1,0:T(8,128)(2,1)}, bf16[2,4,384,704]{3,2,1,0:T(8,128)(2,1)}, bf16[4,384,2048]...) custom-call(s32[1]{0:T(128)} %constant.92.clone.1.meta, ...), custom_call_target="tpu_custom_call", output_to_operand_aliasing={{0}: (5, {}), {1}: (6, {}), {2}: (7, {}), {3}: (8, {}), {4}... | custom-call | flops 11072962560 | bytes 23592960 | tf_op jit(solution)/shard_map/pallas_call | solution.py:595
  607.2 24.9 %shard_map.264 = (bf16[2,4,384,704]{3,2,1,0:T(8,128)(2,1)}, bf16[2,4,384,704]{3,2,1,0:T(8,128)(2,1)}, bf16[2,4,384,704]{3,2,1,0:T(8,128)(2,1)}, bf16[4,384,2048]...) custom-call(s32[1]{0:T(128)} %constant.89.clone.1.meta, ...), custom_call_target="tpu_custom_call", output_to_operand_aliasing={{0}: (5, {}), {1}: (6, {}), {2}: (7, {}), {3}: (8, {}), {4}... | custom-call | flops 11072962560 | bytes 23592960 | tf_op jit(solution)/shard_map/pallas_call | solution.py:595
  676.2 9.4 convolution_convert_fusion.1
  698.7 13.6 %shard_map.265 = bf16[1536,2048]{1,0:T(8,128)(2,1)S(1)} custom-call(bf16[2,4,384,704]{3,2,1,0:T(8,128)(2,1)S(1)} %copy-done.2, bf16[4,3,176,2048]{3,2,1,0:T(8,128)(2,1)} %bitcast.218, bf16[4,3,176,2048]{3,2,1,0:T(8,128)(2,1)} %collective-permute-done.14.theirs), custom_call_target="tpu_custom_call" | custom-call | flops 8858370048 | bytes 17301504 | tf_op jit(solution)/shard_map/pallas_call | solution.py:627
  715.0 14.9 %collective-permute-done.21 = bf16[192,2048]{1,0:T(8,128)(2,1)S(1)} collective-permute-done((bf16[192,2048]{1,0:T(8,128)(2,1)S(1)}, bf16[192,2048]{1,0:T(8,128)(2,1)S(1)}, u32[]{:S(2)}, u32[]{:S(2)}) %collective-permute-start.21) | collective-permute-done | bytes 786464 | tf_op jit(solution)/shard_map/ppermute | solution.py:473
  733.3 10.1 add_convert_fusion.1
  770.8 49.7 %shard_map.266 = bf16[8,384,256]{2,1,0:T(8,128)(2,1)} custom-call(bf16[384,2048]{1,0:T(8,128)(2,1)} %add_convert_fusion.6.src), custom_call_target="tpu_custom_call" | custom-call | bytes 393216000 | tf_op jit(solution)/shard_map/pallas_call | solution.py:379
  820.5 9.6 shard_map.267
  847.9 22.1 %shard_map.268 = (f32[3,1024,128]{2,1,0:T(8,128)}, f32[3,1024,256]{2,1,0:T(8,128)}) custom-call(s32[3,8]{1,0:T(4,128)} %lens.11, s32[1]{0:T(128)} %bitcast.1.meta, bf16[8,3,128,384]{3,2,1,0:T(8,128)(2,1)} %convolution_convert_fusion.4.x_ref, bf16[3,1024,512]{2,1,0:T(8,128)(2,1)} %get-tuple-element.99.gn_ref, ...), custom_call_target="tpu_custom_call" | custom-call | flops 12884901888 | bytes 11436032 | tf_op jit(solution)/shard_map/pallas_call | solution.py:304
  870.0 8.5 constant_dynamic-slice_fusion.1
  886.6 9.8 shard_map.269
  896.4 9.6 bitcast_convert_fusion.1
  916.1 9.3 copy.93
  925.4 70.1 %shard_map.270 = bf16[384,3072]{1,0:T(8,128)(2,1)} custom-call(bf16[8,384,384]{2,1,0:T(8,128)(2,1)} %bitcast.236), custom_call_target="tpu_custom_call" | custom-call | bytes 589824000 | tf_op jit(solution)/shard_map/pallas_call | solution.py:379
  1006.1 28.2 %collective-permute-done.26 = bf16[192,2048]{1,0:T(8,128)(2,1)S(1)} collective-permute-done((bf16[192,2048]{1,0:T(8,128)(2,1)S(1)}, bf16[192,2048]{1,0:T(8,128)(2,1)S(1)}, u32[]{:S(2)}, u32[]{:S(2)}) %collective-permute-start.26) | collective-permute-done | bytes 786464 | tf_op jit(solution)/shard_map/ppermute | solution.py:473
  1064.3 50.7 %all-to-all-done.1 = bf16[4,176,512]{2,1,0:T(8,128)(2,1)S(1)} async-done(((bf16[4,176,512]{2,1,0:T(8,128)(2,1)}), bf16[4,176,512]{2,1,0:T(8,128)(2,1)S(1)}, u32[]{:S(2)}, u32[]{:S(2)}) %all-to-all-start.1) | async-done | bytes 720928 | tf_op jit(solution)/shard_map/all_to_all | solution.py:877
  1149.5 35.8 %all-to-all-done = bf16[4,176,512]{2,1,0:T(8,128)(2,1)} async-done(((bf16[4,176,512]{2,1,0:T(8,128)(2,1)}), bf16[4,176,512]{2,1,0:T(8,128)(2,1)}, u32[]{:S(2)}, u32[]{:S(2)}) %all-to-all-start) | async-done | bytes 720928 | tf_op jit(solution)/shard_map/all_to_all | solution.py:877
  1213.2 13.4 %collective-permute-start.40 = (f32[3,64]{1,0:T(4,128)S(1)}, f32[3,64]{1,0:T(4,128)S(1)}, u32[]{:S(2)}, u32[]{:S(2)}) collective-permute-start(f32[3,64]{1,0:T(4,128)S(1)} %get-tuple-element.203), channel_id=1, source_target_pairs={{0,2},{2,4},{4,6},{6,0},{1,3},{3,5},{5,7},{7,1},{8,10},{10,12},{12... | collective-permute-start | bytes 2312 | tf_op jit(solution)/shard_map/ppermute | solution.py:895
  1235.4 40.4 %reduce-scatter.7.cloned.1.call-done = bf16[256,512]{1,0:T(8,128)(2,1)} async-done(((bf16[2048,512]{1,0:T(8,128)(2,1)}), bf16[256,512]{1,0:T(8,128)(2,1)}) %reduce-scatter.7.cloned.1.call-update) | async-done | bytes 262160 | tf_op jit(solution)/shard_map/reduce_scatter | solution.py:882
  (348 shorter events, 306.7 us)
Async XLA Ops:
  7.2 446.5 %all-gather.3.cloned.1.call-start = ((), (), s32[]{:S(2)}) async-start(), calls=%async_computation.11 | async-start | bytes 12779520 | tf_op jit(solution)/shard_map/all_gather | solution.py:752
  240.0 812.6 %reduce-scatter.9.cloned.1.call-start = ((), (), s32[]{:S(2)}) async-start(), calls=%async_computation.9 | async-start | bytes 3604480 | tf_op jit(solution)/shard_map/reduce_scatter | solution.py:875
  240.1 68.0 %collective-permute-start = (bf16[2048,512]{1,0:T(8,128)(2,1)}, bf16[2048,512]{1,0:T(8,128)(2,1)}, u32[]{:S(2)}, u32[]{:S(2)}) collective-permute-start(bf16[2048,512]{1,0:T(8,128)(2,1)} %bitcast.7), channel_id=1, source_target_pairs={{0,16},{16,0},{1,17},{17,1},{2,18},{18,2},{3,19},{19,3},{4,20},{20... | collective-permute-start | bytes 6291464 | tf_op jit(solution)/shard_map/ppermute | solution.py:473
  258.9 38.1 %collective-permute-start.5 = (bf16[3,2,136,256]{3,2,1,0:T(8,128)(2,1)}, bf16[3,2,136,256]{3,2,1,0:T(8,128)(2,1)S(1)}, u32[]{:S(2)}, u32[]{:S(2)}) collective-permute-start(bf16[3,2,136,256]{3,2,1,0:T(8,128)(2,1)} %shard_map.258), channel_id=1, source_target_pairs={{0,24},{1,25},{2,26},{3,27},{4,28},{5,29},{6,30},{7,31}} | collective-permute-start | bytes 1253384 | tf_op jit(solution)/shard_map/ppermute | solution.py:484
  260.7 44.4 %collective-permute-start.4 = (bf16[3,2,136,256]{3,2,1,0:T(8,128)(2,1)}, bf16[3,2,136,256]{3,2,1,0:T(8,128)(2,1)S(1)}, u32[]{:S(2)}, u32[]{:S(2)}) collective-permute-start(bf16[3,2,136,256]{3,2,1,0:T(8,128)(2,1)} %shard_map.258), channel_id=1, source_target_pairs={{0,16},{8,24},{1,17},{9,25},{2,18},{10,26},{3,19},{11,27},{4,20},{... | collective-permute-start | bytes 1253384 | tf_op jit(solution)/shard_map/ppermute | solution.py:484
  262.6 42.5 %collective-permute-start.3 = (bf16[3,2,136,256]{3,2,1,0:T(8,128)(2,1)}, bf16[3,2,136,256]{3,2,1,0:T(8,128)(2,1)S(1)}, u32[]{:S(2)}, u32[]{:S(2)}) collective-permute-start(bf16[3,2,136,256]{3,2,1,0:T(8,128)(2,1)} %shard_map.258), channel_id=1, source_target_pairs={{0,8},{8,16},{16,24},{1,9},{9,17},{17,25},{2,10},{10,18},{18,26},{... | collective-permute-start | bytes 1253384 | tf_op jit(solution)/shard_map/ppermute | solution.py:484
  308.0 49.5 %collective-permute-start.1 = (bf16[2048,512]{1,0:T(8,128)(2,1)}, bf16[2048,512]{1,0:T(8,128)(2,1)}, u32[]{:S(2)}, u32[]{:S(2)}) collective-permute-start(bf16[2048,512]{1,0:T(8,128)(2,1)} %bitcast.7), channel_id=1, source_target_pairs={{0,8},{8,0},{1,9},{9,1},{2,10},{10,2},{3,11},{11,3},{4,12},{12,4},... | collective-permute-start | bytes 6291464 | tf_op jit(solution)/shard_map/ppermute | solution.py:473
  308.0 49.5 %collective-permute-start.2 = (bf16[2048,512]{1,0:T(8,128)(2,1)}, bf16[2048,512]{1,0:T(8,128)(2,1)S(1)}, u32[]{:S(2)}, u32[]{:S(2)}) collective-permute-start(bf16[2048,512]{1,0:T(8,128)(2,1)} %collective-permute-done), channel_id=1, source_target_pairs={{0,8},{8,0},{1,9},{9,1},{2,10},{10,2},{3,11},{11,3},{4,12},{12,4},... | collective-permute-start | bytes 6291464 | tf_op jit(solution)/shard_map/ppermute | solution.py:473
  462.2 70.4 %collective-permute-start.14 = (bf16[4,3,176,2048]{3,2,1,0:T(8,128)(2,1)}, bf16[4,3,176,2048]{3,2,1,0:T(8,128)(2,1)}, u32[]{:S(2)}, u32[]{:S(2)}) collective-permute-start(bf16[4,3,176,2048]{3,2,1,0:T(8,128)(2,1)} %bitcast.213), channel_id=1, source_target_pairs={{0,8},{8,0},{1,9},{9,1},{2,10},{10,2},{3,11},{11,3},{4,12},{12,4},... | collective-permute-start | bytes 25952264 | tf_op jit(solution)/shard_map/ppermute | solution.py:473
  653.2 409.1 %reduce-scatter.11.cloned.1.call-start = ((), (), s32[]{:S(2)}) async-start(), calls=%async_computation.10 | async-start | bytes 3604480 | tf_op jit(solution)/shard_map/reduce_scatter | solution.py:875
  674.5 456.7 %reduce-scatter.5.cloned.1.call-start = ((), (), s32[]{:S(2)}) async-start(), calls=%async_computation.7 | async-start | bytes 3604480 | tf_op jit(solution)/shard_map/reduce_scatter | solution.py:875
  685.6 44.3 %collective-permute-start.19 = (bf16[704,2048]{1,0:T(8,128)(2,1)}, bf16[704,2048]{1,0:T(8,128)(2,1)}, u32[]{:S(2)}, u32[]{:S(2)}) collective-permute-start(bf16[704,2048]{1,0:T(8,128)(2,1)} %convolution_convert_fusion.1), channel_id=1, source_target_pairs={{0,8},{8,0},{1,9},{9,1},{2,10},{10,2},{3,11},{11,3},{4,12},{12,4},... | collective-permute-start | bytes 8650760 | tf_op jit(solution)/shard_map/ppermute | solution.py:473
  692.0 59.4 %collective-permute-start.15 = (bf16[192,2048]{1,0:T(8,128)(2,1)S(1)}, bf16[192,2048]{1,0:T(8,128)(2,1)}, u32[]{:S(2)}, u32[]{:S(2)}) collective-permute-start(bf16[192,2048]{1,0:T(8,128)(2,1)S(1)} %slice.162), channel_id=1, source_target_pairs={{0,1},{1,0},{2,3},{3,2},{4,5},{5,4},{6,7},{7,6},{8,9},{9,8},{10,11... | collective-permute-start | bytes 2359304 | tf_op jit(solution)/shard_map/ppermute | solution.py:473
  693.4 58.0 %collective-permute-start.23 = (bf16[192,2048]{1,0:T(8,128)(2,1)S(1)}, bf16[192,2048]{1,0:T(8,128)(2,1)}, u32[]{:S(2)}, u32[]{:S(2)}) collective-permute-start(bf16[192,2048]{1,0:T(8,128)(2,1)S(1)} %slice.174), channel_id=1, source_target_pairs={{0,16},{16,0},{1,17},{17,1},{2,18},{18,2},{3,19},{19,3},{4,20},{20... | collective-permute-start | bytes 2359304 | tf_op jit(solution)/shard_map/ppermute | solution.py:473
  830.1 54.8 %collective-permute-start.32 = (bf16[3,2,136,256]{3,2,1,0:T(8,128)(2,1)}, bf16[3,2,136,256]{3,2,1,0:T(8,128)(2,1)S(1)}, u32[]{:S(2)}, u32[]{:S(2)}) collective-permute-start(bf16[3,2,136,256]{3,2,1,0:T(8,128)(2,1)} %get-tuple-element.103), channel_id=1, source_target_pairs={{24,0},{25,1},{26,2},{27,3},{28,4},{29,5},{30,6},{31,7}} | collective-permute-start | bytes 1253384 | tf_op jit(solution)/shard_map/ppermute | solution.py:484
  831.7 54.1 %collective-permute-start.31 = (bf16[3,2,136,256]{3,2,1,0:T(8,128)(2,1)}, bf16[3,2,136,256]{3,2,1,0:T(8,128)(2,1)S(1)}, u32[]{:S(2)}, u32[]{:S(2)}) collective-permute-start(bf16[3,2,136,256]{3,2,1,0:T(8,128)(2,1)} %get-tuple-element.103), channel_id=1, source_target_pairs={{16,0},{24,8},{17,1},{25,9},{18,2},{26,10},{19,3},{27,11},{20,4},{... | collective-permute-start | bytes 1253384 | tf_op jit(solution)/shard_map/ppermute | solution.py:484
  833.1 52.6 %collective-permute-start.30 = (bf16[3,2,136,256]{3,2,1,0:T(8,128)(2,1)}, bf16[3,2,136,256]{3,2,1,0:T(8,128)(2,1)S(1)}, u32[]{:S(2)}, u32[]{:S(2)}) collective-permute-start(bf16[3,2,136,256]{3,2,1,0:T(8,128)(2,1)} %get-tuple-element.103), channel_id=1, source_target_pairs={{8,0},{16,8},{24,16},{9,1},{17,9},{25,17},{10,2},{18,10},{26,18},{... | collective-permute-start | bytes 1253384 | tf_op jit(solution)/shard_map/ppermute | solution.py:484
  841.7 160.4 %collective-permute-start.33 = (bf16[4,384,512]{2,1,0:T(8,128)(2,1)}, bf16[4,384,512]{2,1,0:T(8,128)(2,1)}, u32[]{:S(2)}, u32[]{:S(2)}) collective-permute-start(bf16[4,384,512]{2,1,0:T(8,128)(2,1)} %reshape.184), channel_id=1, source_target_pairs={{0,1},{1,0},{2,3},{3,2},{4,5},{5,4},{6,7},{7,6},{8,9},{9,8},{10,11... | collective-permute-start | bytes 4718600 | tf_op jit(solution)/shard_map/ppermute | solution.py:473
  844.6 151.5 %collective-permute-start.27 = (bf16[192,2048]{1,0:T(8,128)(2,1)}, bf16[192,2048]{1,0:T(8,128)(2,1)}, u32[]{:S(2)}, u32[]{:S(2)}) collective-permute-start(bf16[192,2048]{1,0:T(8,128)(2,1)} %get-tuple-element.168), channel_id=1, source_target_pairs={{0,16},{16,0},{1,17},{17,1},{2,18},{18,2},{3,19},{19,3},{4,20},{20... | collective-permute-start | bytes 2359304 | tf_op jit(solution)/shard_map/ppermute | solution.py:473
  884.9 111.8 %collective-permute-start.25 = (bf16[192,2048]{1,0:T(8,128)(2,1)}, bf16[192,2048]{1,0:T(8,128)(2,1)}, u32[]{:S(2)}, u32[]{:S(2)}) collective-permute-start(bf16[192,2048]{1,0:T(8,128)(2,1)} %get-tuple-element.169), channel_id=1, source_target_pairs={{0,1},{1,0},{2,3},{3,2},{4,5},{5,4},{6,7},{7,6},{8,9},{9,8},{10,11... | collective-permute-start | bytes 2359304 | tf_op jit(solution)/shard_map/ppermute | solution.py:473
  885.7 233.7 %collective-permute-start.45 = (bf16[2048,1024]{1,0:T(8,128)(2,1)}, bf16[2048,1024]{1,0:T(8,128)(2,1)}, u32[]{:S(2)}, u32[]{:S(2)}) collective-permute-start(bf16[2048,1024]{1,0:T(8,128)(2,1)} %copy.94), channel_id=1, source_target_pairs={{0,8},{8,0},{1,9},{9,1},{2,10},{10,2},{3,11},{11,3},{4,12},{12,4},... | collective-permute-start | bytes 12582920 | tf_op jit(solution)/shard_map/ppermute | solution.py:473
  909.0 89.4 %collective-permute-start.43 = (bf16[384,1024]{0,1:T(8,128)(2,1)}, bf16[384,1024]{0,1:T(8,128)(2,1)}, u32[]{:S(2)}, u32[]{:S(2)}) collective-permute-start(bf16[384,1024]{0,1:T(8,128)(2,1)} %bitcast.46), channel_id=1, source_target_pairs={{0,8},{8,0},{1,9},{9,1},{2,10},{10,2},{3,11},{11,3},{4,12},{12,4},... | collective-permute-start | bytes 2359304 | tf_op jit(solution)/shard_map/ppermute | solution.py:473
  996.1 38.2 %collective-permute-start.24 = (bf16[192,2048]{1,0:T(8,128)(2,1)}, bf16[192,2048]{1,0:T(8,128)(2,1)S(1)}, u32[]{:S(2)}, u32[]{:S(2)}) collective-permute-start(bf16[192,2048]{1,0:T(8,128)(2,1)} %get-tuple-element.166), channel_id=1, source_target_pairs={{0,1},{1,0},{2,3},{3,2},{4,5},{5,4},{6,7},{7,6},{8,9},{9,8},{10,11... | collective-permute-start | bytes 2359304 | tf_op jit(solution)/shard_map/ppermute | solution.py:473
  996.7 61.4 %collective-permute-start.29 = (bf16[192,2048]{1,0:T(8,128)(2,1)}, bf16[192,2048]{1,0:T(8,128)(2,1)}, u32[]{:S(2)}, u32[]{:S(2)}) collective-permute-start(bf16[192,2048]{1,0:T(8,128)(2,1)} %get-tuple-element.167), channel_id=1, source_target_pairs={{0,16},{16,0},{1,17},{17,1},{2,18},{18,2},{3,19},{19,3},{4,20},{20... | collective-permute-start | bytes 2359304 | tf_op jit(solution)/shard_map/ppermute | solution.py:473
  1002.0 41.7 %collective-permute-start.44 = (bf16[384,512]{0,1:T(8,128)(2,1)S(1)}, bf16[384,512]{0,1:T(8,128)(2,1)S(1)}, u32[]{:S(2)}, u32[]{:S(2)}) collective-permute-start(bf16[384,512]{0,1:T(8,128)(2,1)S(1)} %constant_dynamic-slice_fusion.3), channel_id=1, source_target_pairs={{0,16},{16,0},{1,17},{17,1},{2,18},{18,2},{3,19},{19,3},{4,20},{20... | collective-permute-start | bytes 1179656 | tf_op jit(solution)/shard_map/ppermute | solution.py:473
  1034.3 91.3 %collective-permute-start.34 = (bf16[3072,512]{1,0:T(8,128)(2,1)}, bf16[3072,512]{1,0:T(8,128)(2,1)}, u32[]{:S(2)}, u32[]{:S(2)}) collective-permute-start(bf16[3072,512]{1,0:T(8,128)(2,1)} %bitcast.34), channel_id=1, source_target_pairs={{0,16},{16,0},{1,17},{17,1},{2,18},{18,2},{3,19},{19,3},{4,20},{20... | collective-permute-start | bytes 9437192 | tf_op jit(solution)/shard_map/ppermute | solution.py:473
  1043.7 97.9 %collective-permute-start.35 = (bf16[3072,512]{1,0:T(8,128)(2,1)}, bf16[3072,512]{1,0:T(8,128)(2,1)}, u32[]{:S(2)}, u32[]{:S(2)}) collective-permute-start(bf16[3072,512]{1,0:T(8,128)(2,1)} %bitcast.34), channel_id=1, source_target_pairs={{0,8},{8,0},{1,9},{9,1},{2,10},{10,2},{3,11},{11,3},{4,12},{12,4},... | collective-permute-start | bytes 9437192 | tf_op jit(solution)/shard_map/ppermute | solution.py:473
  1054.7 60.4 %all-to-all-start.1 = ((bf16[4,176,512]{2,1,0:T(8,128)(2,1)}), bf16[4,176,512]{2,1,0:T(8,128)(2,1)S(1)}, u32[]{:S(2)}, u32[]{:S(2)}) async-start(bf16[4,176,512]{2,1,0:T(8,128)(2,1)} %bitcast.249), calls=%async_computation.4 | async-start | bytes 1441792 | tf_op jit(solution)/shard_map/all_to_all | solution.py:877
  1125.6 70.1 %collective-permute-start.36 = (bf16[3072,512]{1,0:T(8,128)(2,1)}, bf16[3072,512]{1,0:T(8,128)(2,1)}, u32[]{:S(2)}, u32[]{:S(2)}) collective-permute-start(bf16[3072,512]{1,0:T(8,128)(2,1)} %collective-permute-done.34), channel_id=1, source_target_pairs={{0,8},{8,0},{1,9},{9,1},{2,10},{10,2},{3,11},{11,3},{4,12},{12,4},... | collective-permute-start | bytes 9437192 | tf_op jit(solution)/shard_map/ppermute | solution.py:473
  1129.2 62.8 %collective-permute-start.46 = (bf16[2048,512]{1,0:T(8,128)(2,1)}, bf16[2048,512]{1,0:T(8,128)(2,1)}, u32[]{:S(2)}, u32[]{:S(2)}) collective-permute-start(bf16[2048,512]{1,0:T(8,128)(2,1)} %constant_dynamic-slice_fusion), channel_id=1, source_target_pairs={{0,16},{16,0},{1,17},{17,1},{2,18},{18,2},{3,19},{19,3},{4,20},{20... | collective-permute-start | bytes 6291464 | tf_op jit(solution)/shard_map/ppermute | solution.py:473
  1133.2 52.0 %all-to-all-start = ((bf16[4,176,512]{2,1,0:T(8,128)(2,1)}), bf16[4,176,512]{2,1,0:T(8,128)(2,1)}, u32[]{:S(2)}, u32[]{:S(2)}) async-start(bf16[4,176,512]{2,1,0:T(8,128)(2,1)} %bitcast.250), calls=%async_computation.1 | async-start | bytes 1441792 | tf_op jit(solution)/shard_map/all_to_all | solution.py:877
  1137.4 138.3 %reduce-scatter.7.cloned.1.call-start = ((), (), s32[]{:S(2)}) async-start(), calls=%async_computation.8 | async-start | bytes 2359296 | tf_op jit(solution)/shard_map/reduce_scatter | solution.py:882
  (86 other events, 1064.6 us)
Sparse Core Ops, SparseCore 0:
  240.1 213.4 all-gather.2
  653.3 53.4 reduce-scatter.8
  709.1 56.0 reduce-scatter.10
  767.3 82.0 reduce-scatter.4
  1195.9 79.8 reduce-scatter.6

commit v3 on v2

--- a/solution.py
+++ b/solution.py
@@ -341,193 +341,536 @@
     pl.semaphore_wait(bar, len(devices))
 
 
-def exchange_kernel(to_blocks, width, src, dst, ssem, rsem, lsem):
+def square():
+    return tuple(lax.axis_size(n) for n in ("sy", "ha", "hb")) == (2, 4, 2)
+
+
+def place(block, head, special):
+    if special:
+        ha = 2 * (block % 2) + block // 2
+        return (head // 2 + ha % 2) % 2, head % 2, ha
+    return head // 2, head % 2, block
+
+
+def own_place():
+    sy, sc, ha, _ = here()
+    if square():
+        return 2 * (ha % 2) + ha // 2, 2 * ((sy + ha) % 2) + sc
+    return ha, sy * 2 + sc
+
+
+def first_head(block):
+    return block % 2 if square() else block
+
+
+def home_of(head, special):
+    if special:
+        return 2 * (head % 2) + head // 2, 2 * ((head // 2 + head) % 2) + head % 2
+    return head, head
+
+
+def maybe_own(k, own, elsewhere, alone):
+    if k:
+        elsewhere()
+    else:
+        pl.when(jnp.logical_not(own))(elsewhere)
+        pl.when(own)(alone)
+
+
+def exchange_kernel(to_blocks, width, last_major, extra, src, *refs):
+    n_in, n_out = {None: (0, 0), "gather": (2, 2), "scatter": (1, 2)}[extra]
+    ins, dst, outs, sems = refs[:n_in], refs[n_in], refs[n_in + 1 : n_in + 1 + n_out], refs[n_in + 1 + n_out :]
+    ssem, rsem, lsem = sems[:3]
     sy, sc, a, b = here()
+    s = sy * 2 + sc
+    block, head = own_place()
+    special = square()
     size_a, size_b = lax.axis_size("ha"), lax.axis_size("hb")
     count = size_a * size_b
-    me = a * size_b + b
-
-    def peer(k):
-        return lax.rem(a + k // size_b, size_a), lax.rem(b + k % size_b, size_b)
-
-    def ends(k):
-        pa, pb = peer(k)
-        piece = pa * size_b + pb
+    bar = pltpu.get_barrier_semaphore()
+    same = s == block
+
+    def at(k):
+        i, pb = k // size_b, lax.rem(b + k % size_b, size_b)
         if to_blocks:
-            return src.at[:, pl.ds(pl.multiple_of(piece * width, 128), width)], dst.at[me]
-        return src.at[piece], dst.at[:, pl.ds(pl.multiple_of(me * width, 128), width)]
-
-    def at(k):
-        pa, pb = peer(k)
-        return sy, sc, pa, pb
-
-    greet([at(k) for k in range(1, count)])
-    copies = [remote(*ends(k), ssem, rsem, k - 1, at(k)) for k in range(1, count)]
-    for copy in copies:
-        copy.start()
-    local = pltpu.make_async_copy(*ends(0), lsem)
-    local.start()
-    local.wait()
-    for copy in copies:
-        copy.wait()
-
-
-def exchange(x, to_blocks, width, collective):
+            sender = (block // 2, block % 2, lax.rem(a + i, size_a), pb)
+            to = lax.rem(a - place(s, 0, special)[2] + first_head(s) + i + size_a, size_a)
+            piece = to * size_b + pb
+            source = src.at[:, pl.ds(pl.multiple_of(piece * width, 128), width)]
+            return sender, source, dst.at[a * size_b + b], place(s, to, special) + (pb,)
+        sender = place(s, lax.rem(first_head(s) + i, size_a), special) + (pb,)
+        to = lax.rem(head - first_head(block) + a + i + size_a, size_a)
+        column = b * size_a + head if last_major else head * size_b + b
+        far = dst.at[:, pl.ds(pl.multiple_of(column * width, 128), width)]
+        return sender, src.at[to * size_b + pb], far, (block // 2, block % 2, to, pb)
+
+    def copy(k):
+        _, source, far, receiver = at(k)
+        return remote(source, far, ssem, rsem, k, receiver)
+
+    def local():
+        return pltpu.make_async_copy(at(0)[1], at(0)[2], lsem.at[0])
+
+    def signal(device):
+        pl.semaphore_signal(bar, 1, device_id=device, device_id_type=MESH_ID)
+
+    to_x, to_y, to_core = (sy, sc, a, 1 - b), (1 - sy, sc, a, b), (sy, 1 - sc, a, b)
+    expected = count - same.astype(jnp.int32)
+    for k in range(count):
+        maybe_own(k, same, functools.partial(signal, at(k)[0]), lambda: None)
+    if extra in ("gather", "scatter"):
+        greeted = (to_x, to_y, to_core)[: 3 if extra == "gather" else 2]
+        for device in greeted:
+            signal(device)
+        expected = expected + len(greeted)
+    pl.semaphore_wait(bar, expected)
+    for k in range(count):
+        maybe_own(k, same, lambda: copy(k).start(), lambda: local().start())
+
+    if extra == "gather":
+        (more, own_w), (near, other_w) = ins, outs
+        gsem, hsem = sems[3:]
+        half = more.shape[0] // 2
+        low, high = pl.ds(0, half), pl.ds(half, half)
+        copies = [
+            remote(more, near.at[0], gsem, hsem, 0, to_x),
+            remote(more, near.at[1], gsem, hsem, 1, to_y),
+            remote(own_w, other_w, gsem, hsem, 4, to_core),
+        ]
+        for c in copies:
+            c.start()
+        copies[0].wait_recv()
+        copies.append(remote(near.at[0, high], near.at[2, high], gsem, hsem, 2, to_y))
+        copies[3].start()
+        copies[1].wait_recv()
+        copies.append(remote(near.at[1, low], near.at[2, low], gsem, hsem, 3, to_x))
+        copies[4].start()
+        for c in copies[2:]:
+            c.wait_recv()
+        for c in copies:
+            c.wait_send()
+    if extra == "scatter":
+        (parts,), (got, relay) = ins, outs
+        gsem, hsem = sems[3:]
+        half = parts.shape[1] // 2
+        low, high = pl.ds(0, half), pl.ds(half, half)
+        copies = [
+            remote(parts.at[3, low], relay.at[0], gsem, hsem, 0, to_x),
+            remote(parts.at[3, high], relay.at[1], gsem, hsem, 1, to_y),
+            remote(parts.at[1], got.at[0], gsem, hsem, 2, to_x),
+            remote(parts.at[2], got.at[1], gsem, hsem, 3, to_y),
+        ]
+        for c in copies:
+            c.start()
+        copies[0].wait_recv()
+        copies.append(remote(relay.at[0], got.at[2, low], gsem, hsem, 4, to_y))
+        copies[4].start()
+        copies[1].wait_recv()
+        copies.append(remote(relay.at[1], got.at[2, high], gsem, hsem, 5, to_x))
+        copies[5].start()
+        for c in copies[2:]:
+            c.wait_recv()
+        for c in copies:
+            c.wait_send()
+    for k in range(count):
+        maybe_own(k, same, lambda: copy(k).wait(), lambda: local().wait())
+
+
+def exchange(x, to_blocks, width, collective, extra=None, ins=(), outs=(), last_major=False):
     count = lax.axis_size("ha") * lax.axis_size("hb")
     tokens = x.shape[0] if to_blocks else x.shape[1]
     shape = (count, tokens, width) if to_blocks else (tokens, count * width)
+    any_space = pl.BlockSpec(memory_space=pl.ANY)
+    more = {None: 0, "gather": 5, "scatter": 6}[extra]
     return pl.pallas_call(
-        functools.partial(exchange_kernel, to_blocks, width),
-        out_shape=jax.ShapeDtypeStruct(shape, x.dtype),
-        in_specs=[pl.BlockSpec(memory_space=pl.ANY)],
-        out_specs=pl.BlockSpec(memory_space=pl.ANY),
+        functools.partial(exchange_kernel, to_blocks, width, last_major, extra),
+        out_shape=[jax.ShapeDtypeStruct(s, x.dtype) for s in (shape, *outs)],
+        in_specs=[any_space] * (1 + len(ins)),
+        out_specs=[any_space] * (1 + len(outs)),
         scratch_shapes=[
-            pltpu.SemaphoreType.DMA((count - 1,)),
-            pltpu.SemaphoreType.DMA((count - 1,)),
-            pltpu.SemaphoreType.DMA,
+            pltpu.SemaphoreType.DMA((count,)),
+            pltpu.SemaphoreType.DMA((count,)),
+            pltpu.SemaphoreType.DMA((1,)),
+        ]
+        + [pltpu.SemaphoreType.DMA((more,))] * (2 if more else 0),
+        compiler_params=pltpu.CompilerParams(collective_id=collective, has_side_effects=True),
+        cost_estimate=pl.CostEstimate(flops=0, bytes_accessed=x.size * 500, transcendentals=0),
+    )(x, *ins)
+
+
+def home_kernel(*refs):
+    src, grads, windows, shards, dst, grads_got, windows_got, shards_got = refs[:8]
+    ssem, rsem, lsem, gsem, hsem, usem, vsem = refs[8:]
+    sy, sc, a, b = here()
+    s = sy * 2 + sc
+    block, head = own_place()
+    special = square()
+    size_a, size_b = lax.axis_size("ha"), lax.axis_size("hb")
+    devices = src.shape[0]
+    me = (s * size_a + a) * size_b + b
+    homely = head == a
+    block_h, seq_h = home_of(head, special)
+    bar = pltpu.get_barrier_semaphore()
+
+    def peer(k):
+        i = lax.rem(me + k, devices)
+        rest = i // (size_a * size_b)
+        return i, (rest // 2, rest % 2, i // size_b % size_a, i % size_b)
+
+    def copy(k):
+        i, device = peer(k)
+        return remote(src.at[i], dst.at[me], ssem, rsem, k, device)
+
+    def grad_ends(k):
+        e = lax.rem(block - block_h + seq_h + k + size_a, size_a)
+        return grads.at[e], grads_got.at[block], (e // 2, e % 2, head, b)
+
+    def grad_copy(k):
+        source, far, device = grad_ends(k)
+        return remote(source, far, gsem, hsem, k, device)
+
+    def grad_local():
+        return pltpu.make_async_copy(*grad_ends(0)[:2], lsem.at[1])
+
+    def window_copy(k):
+        e = lax.rem(s + k, size_a)
+        return remote(windows.at[e], windows_got.at[s], gsem, hsem, size_a + k, (e // 2, e % 2, a, b))
+
+    def shard_copy(k):
+        pa, pb = lax.rem(a + k // size_b, size_a), lax.rem(b + k % size_b, size_b)
+        far = shards_got.at[a * size_b + b]
+        return remote(shards.at[pa * size_b + pb], far, usem, vsem, k, (sy, sc, pa, pb))
+
+    @pl.loop(1, devices)
+    def _(k):
+        pl.semaphore_signal(bar, 1, device_id=peer(k)[1], device_id_type=MESH_ID)
+
+    stay = [
+        pltpu.make_async_copy(shards.at[a * size_b + b], shards_got.at[a * size_b + b], lsem.at[3]),
+        pltpu.make_async_copy(src.at[me], dst.at[me], lsem.at[0]),
+        pltpu.make_async_copy(windows.at[s], windows_got.at[s], lsem.at[2]),
+    ]
+    for c in stay:
+        c.start()
+    pl.semaphore_wait(bar, devices - 1)
+    heads = size_a * size_b
+    for k in range(size_a):
+        maybe_own(k, homely, lambda: grad_copy(k).start(), lambda: grad_local().start())
+        if k:
+            window_copy(k).start()
+    for k in range(1, heads):
+        shard_copy(k).start()
+
+    @pl.loop(1, devices)
+    def _(k):
+        copy(k).start()
+
+    @pl.loop(1, devices)
+    def _(k):
+        copy(k).wait()
+
+    for k in range(size_a):
+        maybe_own(k, homely, lambda: grad_copy(k).wait(), lambda: grad_local().wait())
+        if k:
+            window_copy(k).wait()
+    for k in range(1, heads):
+        shard_copy(k).wait()
+    for c in stay:
+        c.wait()
+
+
+def send_home(x, grads, windows, shards, collective):
+    devices = 2 * lax.axis_size("sy") * lax.axis_size("ha") * lax.axis_size("hb")
+    vectors, share = x.shape[0], x.shape[1] // devices
+    x = jnp.transpose(x.reshape(vectors, devices, share), (1, 0, 2))
+    x = jnp.pad(x, ((0, 0), (0, 8 - vectors), (0, 128 - share)))
+    any_space = pl.BlockSpec(memory_space=pl.ANY)
+    ins = [x, grads, windows, shards]
+    size_a, heads = lax.axis_size("ha"), shards.shape[0]
+    out = pl.pallas_call(
+        home_kernel,
+        out_shape=[jax.ShapeDtypeStruct(v.shape, v.dtype) for v in ins],
+        in_specs=[any_space] * len(ins),
+        out_specs=[any_space] * len(ins),
+        scratch_shapes=[
+            pltpu.SemaphoreType.DMA((devices,)),
+            pltpu.SemaphoreType.DMA((devices,)),
+            pltpu.SemaphoreType.DMA((4,)),
+            pltpu.SemaphoreType.DMA((2 * size_a,)),
+            pltpu.SemaphoreType.DMA((2 * size_a,)),
+            pltpu.SemaphoreType.DMA((heads,)),
+            pltpu.SemaphoreType.DMA((heads,)),
         ],
         compiler_params=pltpu.CompilerParams(collective_id=collective, has_side_effects=True),
-        cost_estimate=pl.CostEstimate(flops=0, bytes_accessed=x.size * 500, transcendentals=0),
-    )(x)
-
-
-def gather_kernel(arrays, *refs):
-    srcs, dsts, (ssem, rsem, lsem) = refs[:arrays], refs[arrays : 2 * arrays], refs[2 * arrays :]
+        cost_estimate=pl.CostEstimate(flops=0, bytes_accessed=100000000, transcendentals=0),
+    )(*ins)
+    vectors = jnp.sum(out[0], axis=0)[:vectors, :share]
+    return vectors, jnp.sum(out[1].astype(F32), axis=0), out[2], jnp.sum(out[3].astype(F32), axis=0)
+
+
+def near_kernel(rows, src, weights, near, theirs, gsem, hsem):
     sy, sc, a, b = here()
+    to_x, to_y, to_core = (sy, sc, a, 1 - b), (1 - sy, sc, a, b), (sy, 1 - sc, a, b)
+    half = src.shape[0] // 2
+    low, high = pl.ds(0, half), pl.ds(half, half)
+    greet((to_x, to_y, to_core))
+    copies = [
+        remote(src, near.at[0], gsem, hsem, 0, to_x),
+        remote(src, near.at[1], gsem, hsem, 1, to_y),
+        remote(weights.at[:, pl.ds(0, rows)], theirs, gsem, hsem, 4, to_core),
+    ]
+    for copy in copies:
+        copy.start()
+    copies[0].wait_recv()
+    copies.append(remote(near.at[0, high], near.at[2, high], gsem, hsem, 2, to_y))
+    copies[3].start()
+    copies[1].wait_recv()
+    copies.append(remote(near.at[1, low], near.at[2, low], gsem, hsem, 3, to_x))
+    copies[4].start()
+    for copy in copies[2:]:
+        copy.wait_recv()
+    for copy in copies:
+        copy.wait_send()
+
+
+def gather_near(x, weights, rows, collective):
+    if not square():
+        return (lax.all_gather(x, QUAD, axis=0, tiled=True),), swap(weights[:, :rows], "sc")
+    any_space = pl.BlockSpec(memory_space=pl.ANY)
+    near, theirs = pl.pallas_call(
+        functools.partial(near_kernel, rows),
+        out_shape=[
+            jax.ShapeDtypeStruct((3,) + x.shape, x.dtype),
+            jax.ShapeDtypeStruct((weights.shape[0], rows, weights.shape[2]), weights.dtype),
+        ],
+        in_specs=[any_space] * 2,
+        out_specs=[any_space] * 2,
+        scratch_shapes=[pltpu.SemaphoreType.DMA((5,))] * 2,
+        compiler_params=pltpu.CompilerParams(collective_id=collective, has_side_effects=True),
+        cost_estimate=pl.CostEstimate(flops=0, bytes_accessed=x.size * 200, transcendentals=0),
+    )(x, weights)
+    return (x, near[0], near[1], near[2]), theirs
+
+
+def start_kernel(parts, src, w_in, w_out, dst, w_in_home, w_out_all, ssem, rsem, lsem, wsem, vsem):
+    sy, sc, a, b = here()
+    block, head = own_place()
     size = lax.axis_size("ha")
-    to_up, to_down, to_side = (sy, sc, a + 1, b), (sy, sc, a - 1, b), (sy, sc, a, 1 - b)
+    target = place(sy * 2 + sc, a, True) + (b,)
+    source = (block // 2, block % 2, head, b)
+    same = jnp.logical_and(sy * 2 + sc == block, a == head)
+    apart = jnp.logical_not(same)
+    to_x, to_y, to_core = (sy, sc, a, 1 - b), (1 - sy, sc, a, b), (sy, 1 - sc, a, b)
+    to_up, to_down = (sy, sc, a + 1, b), (sy, sc, a - 1, b)
     has_up, has_down = a < size - 1, a > 0
     bar = pltpu.get_barrier_semaphore()
 
     def signal(device):
         pl.semaphore_signal(bar, 1, device_id=device, device_id_type=MESH_ID)
 
-    def send(n, k, pa, device):
-        ref = dsts[n].at[pa * 2 + b]
-        return remote(ref, ref, ssem, rsem, 3 * size * n + k, device)
-
-    local = [pltpu.make_async_copy(s, d.at[a * 2 + b], lsem.at[n]) for n, (s, d) in enumerate(zip(srcs, dsts))]
-    for copy in local:
-        copy.start()
+    for device in (to_x, to_y, to_core):
+        signal(device)
+    pl.when(apart)(lambda: signal(source))
     pl.when(has_up)(lambda: signal(to_up))
     pl.when(has_down)(lambda: signal(to_down))
-    signal(to_side)
-    pl.semaphore_wait(bar, 1 + has_up.astype(jnp.int32) + has_down.astype(jnp.int32))
-    for copy in local:
-        copy.wait()
-
-    def spread(n, k, pa, up, down):
+    own_w = pltpu.make_async_copy(w_out, w_out_all.at[a * 2 + b], lsem.at[parts])
+    own_w.start()
+    pl.semaphore_wait(
+        bar, 3 + apart.astype(jnp.int32) + has_up.astype(jnp.int32) + has_down.astype(jnp.int32)
+    )
+
+    step = src.shape[0] // parts
+    count = 9
+    half = src.shape[1] // 2
+
+    def piece(z, x, r, lo=0, n=None):
+        return dst.at[z * 2 + x, pl.ds(r * step, step), pl.ds(lo, src.shape[1] if n is None else n)]
+
+    def make(k, r, ref, device):
+        return remote(ref, ref, ssem, rsem, count * r + k, device)
+
+    def home(r):
+        return remote(src.at[pl.ds(r * step, step)], piece(a, b, r), ssem, rsem, count * r, target)
+
+    def stay(r):
+        return pltpu.make_async_copy(src.at[pl.ds(r * step, step)], piece(a, b, r), lsem.at[r])
+
+    def w_home():
+        return pltpu.make_async_remote_copy(
+            src_ref=w_in,
+            dst_ref=w_in_home,
+            send_sem=wsem.at[0],
+            recv_sem=wsem.at[1],
+            device_id=target,
+            device_id_type=MESH_ID,
+        )
+
+    def w_stay():
+        return pltpu.make_async_copy(w_in, w_in_home, lsem.at[parts + 1])
+
+    for r in range(parts):
+        pl.when(apart)(lambda: home(r).start())
+        pl.when(same)(lambda: stay(r).start())
+
+    def send_w(k, pa, device):
+        ref = w_out_all.at[pa * 2 + b]
+        return remote(ref, ref, vsem.at[0], vsem.at[1], k, device)
+
+    def spread(k, pa, up, down):
         if up:
-            pl.when(has_up)(lambda: send(n, k, pa, to_up).start())
+            pl.when(has_up)(lambda: send_w(k, pa, to_up).start())
         if down:
-            pl.when(has_down)(lambda: send(n, size + k, pa, to_down).start())
-        send(n, 2 * size + pa, pa, to_side).start()
-
-    for n in range(arrays):
-        spread(n, 0, a, True, True)
-    for k in range(1, size):
-        for n in range(arrays):
-
-            @pl.when(a - k >= 0)
-            def _():
-                send(n, k - 1, a - k, to_side).wait_recv()
-                spread(n, k, a - k, True, False)
-
-            @pl.when(a + k < size)
-            def _():
-                send(n, size + k - 1, a + k, to_side).wait_recv()
-                spread(n, k, a + k, False, True)
-
-    for n in range(arrays):
-        for k in range(size):
-            ref = dsts[n].at[k * 2 + 1 - b]
-            remote(ref, ref, ssem, rsem, 3 * size * n + 2 * size + k, to_side).wait_recv()
-        for k in range(size):
-            send(n, 2 * size + k, k, to_side).wait_send()
-            pl.when(jnp.logical_and(has_up, a - k >= 0))(lambda: send(n, k, a - k, to_side).wait_send())
-            pl.when(jnp.logical_and(has_down, a + k < size))(
-                lambda: send(n, size + k, a + k, to_side).wait_send()
-            )
-
-
-def gather_block(xs, collective):
-    if (lax.axis_size("ha"), lax.axis_size("hb")) != (4, 2):
-        return [lax.all_gather(x, HEAD, axis=0) for x in xs]
-    n = len(xs)
+            pl.when(has_down)(lambda: send_w(size + k, pa, to_down).start())
+        send_w(2 * size + pa, pa, to_x).start()
+
+    def w_step(k):
+        @pl.when(a - k >= 0)
+        def _():
+            send_w(k - 1, a - k, to_x).wait_recv()
+            spread(k, a - k, True, False)
+
+        @pl.when(a + k < size)
+        def _():
+            send_w(size + k - 1, a + k, to_x).wait_recv()
+            spread(k, a + k, False, True)
+
+    across_y, across_c = (head + 2) % 4, head + 1 - 2 * (head % 2)
+    across = (across_y + 1) - 2 * (across_y % 2)
+    sent = []
+
+    def go(copy):
+        copy.start()
+        sent.append(copy)
+
+    def arrive(k, r, ref):
+        make(k, r, ref, to_x).wait_recv()
+
+    def stage_0(r):
+        pl.when(apart)(lambda: arrive(0, r, piece(head, b, r)))
+        pl.when(same)(lambda: stay(r).wait())
+        for k, device in ((1, to_x), (2, to_y), (3, to_core)):
+            go(make(k, r, piece(head, b, r), device))
+
+    def stage_1(r):
+        arrive(1, r, piece(head, 1 - b, r))
+        go(make(4, r, piece(head, 1 - b, r, half, half), to_y))
+        go(make(5, r, piece(head, 1 - b, r), to_core))
+        arrive(2, r, piece(across_y, b, r))
+        go(make(6, r, piece(across_y, b, r, 0, half), to_x))
+        go(make(7, r, piece(across_y, b, r), to_core))
+
+    def stage_2(r):
+        arrive(4, r, piece(across_y, 1 - b, r, half, half))
+        arrive(6, r, piece(across_y, 1 - b, r, 0, half))
+        go(make(8, r, piece(across_y, 1 - b, r), to_core))
+
+    def stage_3(r):
+        arrive(3, r, piece(across_c, b, r))
+        arrive(5, r, piece(across_c, 1 - b, r))
+        arrive(7, r, piece(across, b, r))
+        arrive(8, r, piece(across, 1 - b, r))
+
+    stages = (stage_0, stage_1, stage_2, stage_3)
+    for t in range(parts + 3):
+        for i, stage in enumerate(stages):
+            if 0 <= t - i < parts:
+                stage(t - i)
+        if t == 0:
+            pl.when(apart)(lambda: w_home().start())
+            pl.when(same)(lambda: w_stay().start())
+            own_w.wait()
+            spread(0, a, True, True)
+        elif t < size:
+            w_step(t)
+    for k in range(parts + 3, size):
+        w_step(k)
+    pl.when(apart)(lambda: w_home().wait_recv())
+    pl.when(same)(lambda: w_stay().wait())
+    for k in range(size):
+        ref = w_out_all.at[k * 2 + 1 - b]
+        remote(ref, ref, vsem.at[0], vsem.at[1], 2 * size + k, to_x).wait_recv()
+        send_w(2 * size + k, k, to_x).wait_send()
+        pl.when(jnp.logical_and(has_up, a - k >= 0))(lambda: send_w(k, a - k, to_x).wait_send())
+        pl.when(jnp.logical_and(has_down, a + k < size))(lambda: send_w(size + k, a + k, to_x).wait_send())
+    for copy in sent:
+        copy.wait_send()
+    for r in range(parts):
+        pl.when(apart)(lambda: home(r).wait_send())
+    pl.when(apart)(lambda: w_home().wait_send())
+
+
+def start(x, w_in, w_out, collective):
+    if not square():
+        size = lax.axis_size("ha")
+        perm = [(s * size + z, z * size + s) for s in range(size) for z in range(size)]
+        x, w_in = (lax.ppermute(v, ("sy", "sc", "ha"), perm) for v in (x, w_in))
+        return lax.all_gather(x, ("sy", "sc", "hb"), axis=0), w_in, lax.all_gather(w_out, HEAD, axis=0)
+    parts = x.shape[0]
     return pl.pallas_call(
-        functools.partial(gather_kernel, n),
-        out_shape=[jax.ShapeDtypeStruct((8,) + x.shape, x.dtype) for x in xs],
-        in_specs=[pl.BlockSpec(memory_space=pl.ANY)] * n,
-        out_specs=[pl.BlockSpec(memory_space=pl.ANY)] * n,
+        functools.partial(start_kernel, parts),
+        out_shape=[
+            jax.ShapeDtypeStruct((8,) + x.shape, x.dtype),
+            jax.ShapeDtypeStruct(w_in.shape, w_in.dtype),
+            jax.ShapeDtypeStruct((8,) + w_out.shape, w_out.dtype),
+        ],
+        in_specs=[pl.BlockSpec(memory_space=pl.ANY)] * 3,
+        out_specs=[pl.BlockSpec(memory_space=pl.ANY)] * 3,
         scratch_shapes=[
-            pltpu.SemaphoreType.DMA((12 * n,)),
-            pltpu.SemaphoreType.DMA((12 * n,)),
-            pltpu.SemaphoreType.DMA((n,)),
+            pltpu.SemaphoreType.DMA((9 * parts,)),
+            pltpu.SemaphoreType.DMA((9 * parts,)),
+            pltpu.SemaphoreType.DMA((parts + 2,)),
+            pltpu.SemaphoreType.DMA((2,)),
+            pltpu.SemaphoreType.DMA((2, 12)),
         ],
         compiler_params=pltpu.CompilerParams(collective_id=collective, has_side_effects=True),
-        cost_estimate=pl.CostEstimate(flops=0, bytes_accessed=xs[0].size * 600, transcendentals=0),
-    )(*xs)
+        cost_estimate=pl.CostEstimate(flops=0, bytes_accessed=x.size * 400, transcendentals=0),
+    )(x, w_in, w_out)
 
 
 def swap(x, axis):
     return lax.ppermute(x, axis, [(0, 1), (1, 0)])
 
 
+def seat(block, head, size, special):
+    sy, sc, ha = place(block, head, special)
+    return (sy * 2 + sc) * size + ha
+
+
 def chain_pieces(x, backward):
-    size = lax.axis_size("sy") * 2
+    size, special = lax.axis_size("ha"), square()
     out = []
     for k in range(1, size):
-        if backward:
-            perm = [(i, i - k) for i in range(k, size)]
-        else:
-            perm = [(i, i + k) for i in range(size - k)]
-        out.append(lax.ppermute(x, SEQ, perm))
+        perm = []
+        for i in range(size - k):
+            ends = (i + k, i) if backward else (i, i + k)
+            perm += [tuple(seat(e, h, size, special) for e in ends) for h in range(size)]
+        out.append(lax.ppermute(x, SEQ + ("ha",), perm))
     return out
 
 
-def tie(x, *after):
-    return lax.optimization_barrier((x, *jax.tree.leaves(after)))[0]
-
-
-def my_columns(x):
-    size = x.shape[1] // (lax.axis_size("sy") * 2)
-    place = lax.axis_index("sy") * 2 + lax.axis_index("sc")
-    return lax.dynamic_slice_in_dim(x, place * size, size, 1)
-
-
-def seq_pieces(x):
-    if lax.axis_size("sy") != 2:
-        return list(lax.all_gather(x, SEQ, axis=0))
-    along_y = swap(x, "sy")
-    other, other_y = swap(x, "sc"), swap(along_y, "sc")
-    return [x, along_y, other, other_y]
-
-
-def piece_places(count):
-    if lax.axis_size("sy") != 2:
-        return list(range(count))
-    y, c = lax.axis_index("sy"), lax.axis_index("sc")
-    return [y * 2 + c, (1 - y) * 2 + c, y * 2 + 1 - c, (1 - y) * 2 + 1 - c]
-
-
-def by_columns(a, pieces):
-    parts = [dot(a, p) for p in pieces]
-    if lax.axis_size("sy") == 2:
-        y, c = lax.axis_index("sy") == 0, lax.axis_index("sc") == 0
-        rows = [(jnp.where(y, parts[k], parts[k + 1]), jnp.where(y, parts[k + 1], parts[k])) for k in (0, 2)]
-        parts = []
-        for own, other in zip(*rows):
-            parts += [jnp.where(c, own, other), jnp.where(c, other, own)]
-    return jnp.concatenate(parts, axis=1)
-
-
-def by_columns_back(a, pieces):
-    size = pieces[0].shape[1]
-    total = None
-    for p, place in zip(pieces, piece_places(len(pieces))):
-        part = dot(lax.dynamic_slice_in_dim(a, place * size, size, 1), p, NT)
-        total = part if total is None else total + part
-    return total
+def tie(*values):
+    return lax.optimization_barrier(values)
+
+
+def my_columns(x, by_core):
+    parts, place_of = lax.axis_size("sy") * 2, lax.axis_index("sy") * 2 + lax.axis_index("sc")
+    if by_core:
+        parts, place_of = 2, lax.axis_index("sc")
+    size = x.shape[1] // parts
+    return lax.dynamic_slice_in_dim(x, place_of * size, size, 1)
+
+
+def by_halves(a, own, other):
+    own, other = dot(a, own), dot(a, other)
+    first = lax.axis_index("sc") == 0
+    return jnp.concatenate([jnp.where(first, own, other), jnp.where(first, other, own)], axis=1)
+
+
+def by_halves_back(a, own, other):
+    size = own.shape[1]
+    core = lax.axis_index("sc")
+    ours, theirs = (lax.dynamic_slice_in_dim(a, i * size, size, 1) for i in (core, 1 - core))
+    return dot(ours, own, NT) + dot(theirs, other, NT)
 
 
 def unit_window(x, size):
@@ -555,8 +898,8 @@
 
     def work(w, first):
         x, c = n2[...], cot[...]
-        units, width = w.shape[0] * w.shape[2], w.shape[3]
-        w_gate, w_up, w_down = (w[:, i].reshape(units, width) for i in range(3))
+        window, width = w.shape[1] // 3, w.shape[2]
+        w_gate, w_up, w_down = (w[:, i * window : (i + 1) * window].reshape(-1, width) for i in range(3))
         gate, up, gh = dot(x, w_gate, NT), dot(x, w_up, NT), dot(c, w_down, NT)
         sig = jax.nn.sigmoid(gate)
         act = gate * sig
@@ -584,11 +927,11 @@
 
 def ff_chunk(n2, cot, mine, theirs, place, chunks, kept):
     tokens, width = n2.shape
-    units = mine.shape[0] * mine.shape[2]
+    units = theirs.shape[0] * theirs.shape[1] // 3
     keep = jax.ShapeDtypeStruct((2, chunks, tokens, units), BF)
     held_shape = jax.ShapeDtypeStruct((chunks, tokens, width), BF)
     whole = pl.BlockSpec((tokens, width), lambda i, m: (0, 0))
-    weights = pl.BlockSpec(mine.shape, lambda i, m: (0, 0, 0, 0), pipeline_mode=pl.Buffered(1))
+    weights = pl.BlockSpec(theirs.shape, lambda i, m: (0, 0, 0), pipeline_mode=pl.Buffered(1))
     piece = pl.BlockSpec((1, 1, tokens, units), lambda i, m: (i, m[0], 0, 0))
     held = pl.BlockSpec((1, tokens, width), lambda i, m: (m[0], 0, 0))
     old = [] if kept is None else list(kept)
@@ -612,68 +955,78 @@
     )(place, n2, cot, mine, theirs, *old)
 
 
-def branch_kernel(hidden, mine, theirs, out):
+def branch_kernel(order, hidden, mine, theirs, out):
     width = out.shape[1]
-    part = dot(hidden[0, 0], mine[:, 0].reshape(-1, width)) + dot(hidden[1, 0], theirs[:, 0].reshape(-1, width))
+    part = dot(hidden[0, 0], mine[...].reshape(-1, width)) + dot(hidden[1, 0], theirs[...].reshape(-1, width))
     out[...] = part.astype(BF)
 
 
 def branch_product(hidden, mine, theirs):
     _, chunks, tokens, units = hidden.shape
-    width = mine.shape[3]
-    weights = pl.BlockSpec(
-        (mine.shape[0], 1) + mine.shape[2:], lambda i: (0, 2, 0, 0), pipeline_mode=pl.Buffered(1)
-    )
+    size, rows, width = theirs.shape
+    weights = pl.BlockSpec((size, rows // 3, width), lambda i, m: (0, 2, 0), pipeline_mode=pl.Buffered(1))
+    y, b = lax.axis_index("sy"), lax.axis_index("hb")
+    turns = ((y, b), (y, 1 - b), (1 - y, b), (1 - y, 1 - b))[:chunks]
+    order = jnp.stack([p * 2 + q if chunks > 1 else 0 * p for p, q in turns]).astype(jnp.int32)
     return pl.pallas_call(
         branch_kernel,
         out_shape=jax.ShapeDtypeStruct((chunks * tokens, width), BF),
-        grid=(chunks,),
-        in_specs=[pl.BlockSpec((2, 1, tokens, units), lambda i: (0, i, 0, 0)), weights, weights],
-        out_specs=pl.BlockSpec((tokens, width), lambda i: (i, 0)),
+        grid_spec=pltpu.PrefetchScalarGridSpec(
+            num_scalar_prefetch=1,
+            grid=(chunks,),
+            in_specs=[pl.BlockSpec((2, 1, tokens, units), lambda i, m: (0, i, 0, 0)), weights, weights],
+            out_specs=pl.BlockSpec((tokens, width), lambda i, m: (m[i], 0)),
+        ),
         compiler_params=pltpu.CompilerParams(vmem_limit_bytes=40 * 1024 * 1024),
         cost_estimate=pl.CostEstimate(
             flops=chunks * tokens * units * width * 4, bytes_accessed=12 * units * width, transcendentals=0
         ),
-    )(hidden, mine, theirs)
+    )(order, hidden, mine, theirs)
 
 
 QUAD = ("sy", "hb")
-
-
-def ring_gather(x):
-    half = x.shape[0] // 2
-    from_x, from_y = swap(x, "hb"), swap(x, "sy")
-    across = jnp.concatenate([swap(from_y[:half], "hb"), swap(from_x[half:], "sy")], axis=0)
-    return x, from_x, from_y, across
 
 
 def add_low(a, b):
     return (a.astype(F32) + b.astype(F32)).astype(BF)
 
 
-def ring_sum(parts, meanwhile=lambda stage: ()):
+def ring_sum(parts, meanwhile):
     own, to_x, to_y, across = parts
     half = own.shape[0] // 2
     via_x, via_y = swap(across[:half], "hb"), swap(across[half:], "sy")
     x_low, y_high = swap(to_x[:half], "hb"), swap(to_y[half:], "sy")
     work = meanwhile(0)
-    via_x, via_y = tie(via_x, *work), tie(via_y, *work)
+    via_x, via_y, *work = tie(via_x, via_y, *work)
+    meanwhile(0, work)
     y_low = swap(add_low(to_y[:half], via_x), "sy")
     x_high = swap(add_low(to_x[half:], via_y), "hb")
     work = meanwhile(1)
-    y_low, x_high = tie(y_low, *work), tie(x_high, *work)
+    y_low, x_high, *work = tie(y_low, x_high, *work)
+    meanwhile(1, work)
     low = own[:half].astype(F32) + x_low.astype(F32) + y_low.astype(F32)
     high = own[half:].astype(F32) + x_high.astype(F32) + y_high.astype(F32)
     return jnp.concatenate([low, high], axis=0)
 
 
-def quad_gather(x):
-    if (lax.axis_size("sy"), lax.axis_size("hb")) == (2, 2):
-        return ring_gather(x)
-    return (lax.all_gather(x, QUAD, axis=0, tiled=True),)
-
-
-def quad_sum(parts, meanwhile=lambda stage: ()):
+def seq_sum(a, b):
+    size_y, core, y = lax.axis_size("sy"), lax.axis_index("sc"), lax.axis_index("sy")
+    size = b.shape[1] // (size_y * 2)
+
+    def columns(x, i):
+        return lax.dynamic_slice_in_dim(x, i * size, size, 1)
+
+    def of_core(c):
+        return jnp.concatenate([columns(b, i * 2 + c) for i in range(size_y)], axis=1)
+
+    given = swap(dot(a, of_core(1 - core), TN).astype(BF), "sc")
+    part = (dot(a, of_core(core), TN) + given.astype(F32)).astype(BF)
+    if size_y != 2:
+        return lax.psum_scatter(part, "sy", scatter_dimension=1, tiled=True)
+    return add_low(columns(part, y), swap(columns(part, 1 - y), "sy"))
+
+
+def quad_sum(parts, meanwhile):
     if len(parts) == 4:
         return ring_sum(parts, meanwhile)
     for stage in (0, 1):
@@ -681,17 +1034,21 @@
     return lax.psum_scatter(parts[0], QUAD, scatter_dimension=0, tiled=True).astype(F32)
 
 
-def ff_group(n2, cots, mine, theirs):
+def ff_group(chunks, cots, mine, theirs):
     kept, parts = None, []
-    for i, (chunk, cot) in enumerate(zip(quad_gather(n2), cots)):
-        place = jnp.full((1,), i, jnp.int32)
-        *kept, part = ff_chunk(chunk, cot, mine, theirs, place, len(cots), kept)
+    for i, (chunk, cot) in enumerate(zip(chunks, cots)):
+        where = jnp.full((1,), i, jnp.int32)
+        *kept, part = ff_chunk(chunk, cot, mine, theirs, where, len(cots), kept)
         parts.append(part)
     grads, branch = [], []
     flat = [k.reshape((2, -1, k.shape[-1]) if k.ndim == 4 else (-1, k.shape[-1])) for k in kept]
     pairs = [(flat[0], flat[3]), (flat[1], flat[3]), (flat[2], flat[4])]
 
-    def meanwhile(stage):
+    def meanwhile(stage, results=None):
+        if results is not None:
+            grads[:] = results[:3]
+            branch[:] = results[3:]
+            return None
         if stage == 0:
             grads.extend(swap(dot(a[1], b, TN).astype(BF), "sc") for a, b in pairs)
             return grads
@@ -734,7 +1091,7 @@
     xw = vw + 128
     length = sub_len * count
     tokens = rows_n * sub_len
-    meta = (lax.axis_index("sy") * 2 + lax.axis_index("sc")).astype(jnp.int32).reshape(1)
+    meta = own_place()[0].astype(jnp.int32).reshape(1)
     pa, pb, frows, align = feature_tables(nh)
     scalars = (doc_lengths, meta)
 
@@ -746,15 +1103,14 @@
     w_in = jnp.concatenate([w_value.T, w_query.T, w_key.T, pad], axis=0)
     units = down_weight.shape[0]
     windows = [unit_window(w, blocks) for w in (gate_weight.T, up_weight.T, down_weight)]
-    w_in_piece = my_columns(w_in)
-    to_fetch = jnp.concatenate(windows + [w_in_piece.reshape(-1, width)], axis=0)
-    normed_full, w_out_piece = gather_block([(normed_one * attn_gain).astype(BF), my_columns(w_out)], 3)
-    fetched = lax.all_gather(tie(to_fetch, normed_full), "ha", axis=0)
-    w_out_pieces = seq_pieces(w_out_piece.reshape(-1, w_out_piece.shape[-1]))
+    w_in_piece = my_columns(w_in, False)
+    to_fetch = jnp.concatenate(windows, axis=0)
+    normed_full, w_in_home, w_out_piece = start((normed_one * attn_gain).astype(BF), w_in, my_columns(w_out, True), 3)
+    to_fetch, normed_full = tie(to_fetch, normed_full)
+    fetched = lax.all_gather(to_fetch, "ha", axis=0)
     window = windows[0].shape[0]
-    mine = fetched[:, : 3 * window].reshape(size_a, 3, window, width)
-
-    qkv = jnp.einsum("grtd,cd->grtc", normed_full, w_in, preferred_element_type=F32).astype(BF)
+
+    qkv = jnp.einsum("grtd,cd->grtc", normed_full, w_in_home, preferred_element_type=F32).astype(BF)
     pair = nh * rows_n * length * length
     (states,) = row_call(
         functools.partial(state_kernel, nh, vd, docs),
@@ -777,7 +1133,7 @@
         functools.partial(attend_kernel, nh, vd, docs, blocks),
         rows_n,
         scalars,
-        [(qkv, 1), (tie(num, w_out_pieces), 0), (den, 0), (pa, None), (pb, None), (frows, None)]
+        [(qkv, 1), (num, 0), (den, 0), (pa, None), (pb, None), (frows, None)]
         + [(e, 0) for e in earlier],
         [
             ((count, rows_n, sub_len, vw), BF, 1),
@@ -786,18 +1142,27 @@
         ],
         nh * rows_n * length * 256 * 256 * 6,
     )
-    flat_cot = tie(cot.reshape(tokens, width), earlier)
-    cots = quad_gather(flat_cot)
-    attended = exchange(tie(att, cots).reshape(count, tokens, vw), False, vw, 0)
-    attn_branch = by_columns(attended, w_out_pieces).reshape(rows_n, sub_len, width)
+    flat_cot, to_owners = cot.reshape(tokens, width), att.reshape(count, tokens, vw)
+    if square():
+        attended, near, w_out_other = exchange(
+            to_owners, False, vw, 0, "gather", (flat_cot, w_out_piece), ((3, tokens, width), w_out_piece.shape)
+        )
+        cots = (flat_cot, near[0], near[1], near[2])
+    else:
+        (attended,) = exchange(to_owners, False, vw, 0)
+        cots = (lax.all_gather(flat_cot, QUAD, axis=0, tiled=True),)
+        w_out_other = swap(w_out_piece, "sc")
+    w_out_halves = [w.reshape(count * vw, width // 2) for w in (w_out_piece, w_out_other)]
+    attn_branch = by_halves(attended, *w_out_halves).reshape(rows_n, sub_len, width)
     middle = x + attn_branch + out_bias
     scale_two = rms_scale(middle)
     normed_two = middle * scale_two
     normed_two_low = (normed_two * mlp_gain).astype(BF)
 
-    theirs = swap(tie(mine, attended), "sc")
-    n2 = normed_two_low.reshape(tokens, width)
-    grad_two, ff_grads, branch = ff_group(n2, cots, mine, theirs)
+    chunks, theirs = gather_near(normed_two_low.reshape(tokens, width), fetched, 3 * window, 4)
+    w_in_piece, chunks = tie(w_in_piece, chunks)
+    w_in_all = lax.all_gather(w_in_piece, ("sy", "sc", "hb", "ha"), axis=0)
+    grad_two, ff_grads, branch = ff_group(chunks, cots, fetched, theirs)
     grad_two = grad_two.reshape(rows_n, sub_len, width)
     gain_two_part = jnp.sum(grad_two * normed_two, axis=(0, 1))
     scaled = grad_two * mlp_gain
@@ -808,17 +1173,17 @@
     grad_branch = grad_middle.astype(BF)
 
     flat_branch = grad_branch.reshape(tokens, width)
-    grad_att = by_columns_back(flat_branch, w_out_pieces).astype(BF)
-    step = branch.shape[0] // len(cots)
-    branch = tie(branch, grad_att)
-    branch = quad_sum([branch[i * step : (i + 1) * step] for i in range(len(cots))])
-    output = (middle + branch.reshape(rows_n, sub_len, width)).astype(BF)
-    grad_att = exchange(grad_att, True, vw, 1).reshape(count, rows_n, sub_len, vw)
-    near = tie(fetched[:, 3 * window :].reshape((size_a,) + w_in_piece.shape), grad_att)
-    side = lax.axis_index("hb") == 0
-    aside = swap(near, "hb")
-    w_in_piece = jnp.stack([jnp.where(side, near, aside), jnp.where(side, aside, near)], axis=1)
-    w_in_pieces = seq_pieces(w_in_piece.reshape(-1, w_in_piece.shape[-1]))
+    grad_att = by_halves_back(flat_branch, *w_out_halves).astype(BF)
+    branch, w_in_all = tie(branch, w_in_all)
+    branch = lax.psum_scatter(branch, QUAD, scatter_dimension=0, tiled=True)
+    (grad_att,) = exchange(grad_att, True, vw, 1)
+    ff_grads, branch, grad_att = tie(jnp.concatenate(ff_grads, axis=1), branch, grad_att)
+    ff_grads = lax.psum_scatter(ff_grads, "ha", scatter_dimension=0, tiled=True)
+    grad_att = grad_att.reshape(count, rows_n, sub_len, vw)
+    output = (middle + branch.astype(F32).reshape(rows_n, sub_len, width)).astype(BF)
+    grad_w_out = seq_sum(attended, flat_branch).reshape(count, vw, width // blocks)
+    ff_grads = jnp.transpose(ff_grads.reshape(-1, 3, blocks, width // blocks), (2, 1, 0, 3))
+    ff_grads = ff_grads.reshape(blocks, -1, width // blocks)
     gn, grad_states = row_call(
         functools.partial(back_state_kernel, nh, vd, docs),
         rows_n,
@@ -844,8 +1209,10 @@
         [((count, rows_n, sub_len, xw), BF, 1)],
         nh * rows_n * length * 256 * 256 * 6,
     )
-    grad_in = exchange(gqkv.reshape(count, tokens, xw), False, xw, 2)
-    grad_one = by_columns(grad_in, w_in_pieces).reshape(rows_n, sub_len, width)
+    (grad_in,) = exchange(gqkv.reshape(count, tokens, xw), False, xw, 2, last_major=True)
+    w_in_all = w_in_all.reshape(blocks, count * xw, width // blocks)
+    grad_one = jnp.concatenate([dot(grad_in, w_in_all[i]) for i in range(blocks)], axis=1)
+    grad_one = grad_one.reshape(rows_n, sub_len, width)
     gain_one_part = jnp.sum(grad_one * normed_one, axis=(0, 1))
     scaled = grad_one * attn_gain
     input_grad = (
@@ -853,49 +1220,13 @@
         + scale_one * (scaled - normed_one * jnp.mean(scaled * normed_one, axis=-1, keepdims=True))
     ).astype(BF)
 
-    def seq_sum(a, b):
-        part = dot(a, b, TN).astype(BF).reshape(a.shape[1], blocks // 2, 2, width // blocks)
-        core = lax.axis_index("sc")
-        ours, given = (
-            lax.dynamic_index_in_dim(part, i, 2, False).reshape(a.shape[1], -1) for i in (core, 1 - core)
-        )
-        part = add_low(ours, swap(given, "sc"))
-        if lax.axis_size("sy") != 2:
-            return lax.psum_scatter(part, "sy", scatter_dimension=1, tiled=True)
-        y = lax.axis_index("sy")
-        size = width // blocks
-        kept, sent = (lax.dynamic_slice_in_dim(part, i * size, size, 1) for i in (y, 1 - y))
-        return (kept.astype(F32) + swap(sent, "sy").astype(F32)).astype(BF)
-
     flat_tokens = count * tokens
-    grad_w_in = seq_sum(gqkv.reshape(flat_tokens, xw), normed_full.reshape(flat_tokens, width)).astype(F32)
-    grad_w_out = seq_sum(attended, flat_branch)
-
-    def ff_home(part):
-        part = lax.psum_scatter(part, "ha", scatter_dimension=0, tiled=True)
-        part = part.reshape(part.shape[0], blocks, width // blocks)
-        part = lax.all_to_all(jnp.transpose(part, (1, 0, 2)), SEQ, 0, 0, tiled=True)
-        return windows_joined(part.astype(F32), units)
-
-    grad_gate_w, grad_up_w, grad_down_w = (ff_home(g) for g in ff_grads)
-    grad_w_out = tie(grad_w_out, grad_down_w)
-    grad_w_out = lax.psum_scatter(grad_w_out, HEAD, scatter_dimension=0, tiled=True).astype(F32)
+    grad_w_in = dot(gqkv.reshape(flat_tokens, xw), normed_full.reshape(flat_tokens, width), TN)
+    grad_w_in = jnp.transpose(grad_w_in.astype(BF).reshape(xw, blocks, width // blocks), (1, 0, 2))
     vectors = jnp.stack([gain_one_part, bias_part, gain_two_part])
-    if (lax.axis_size("sy"), size_a, size_b) == (2, 4, 2):
-        vectors = vectors.reshape(3, 2, 2, 4, 2, -1)
-        for axis, where in (("sc", 2), ("sy", 1), ("hb", 4)):
-            i = lax.axis_index(axis)
-            given = swap(lax.dynamic_slice_in_dim(vectors, 1 - i, 1, where), axis)
-            vectors = lax.dynamic_slice_in_dim(vectors, i, 1, where) + given
-        vectors = vectors.reshape(3, 4, -1)
-        i = lax.axis_index("ha")
-        total = lax.dynamic_index_in_dim(vectors, i, 1, False)
-        for k in range(1, 4):
-            piece = lax.dynamic_index_in_dim(vectors, lax.rem(i + k, 4), 1, False)
-            total = total + lax.ppermute(piece, "ha", [(z, (z + k) % 4) for z in range(4)])
-        vectors = total
-    else:
-        vectors = lax.psum_scatter(vectors, every, scatter_dimension=1, tiled=True)
+    vectors, grad_w_in, ff_grads, grad_w_out = send_home(vectors, grad_w_in, ff_grads, grad_w_out, 5)
+    ff_grads = ff_grads.astype(F32).reshape(blocks, 3, -1, width // blocks)
+    grad_gate_w, grad_up_w, grad_down_w = (windows_joined(ff_grads[:, i], units) for i in range(3))
     qk_cut = vw + nh * FEAT
     return (
         jnp.transpose(output, (1, 0, 2)),

time: 1290 us -> 1160 us (0.90)
  waiting for transfers between devices: 350 us -> 198 us
  Pallas kernels: 574 us -> 693 us
  starting transfers between devices: 73.3 us -> 16 us
  local copies, waits for them, and re-layouts: 91.2 us -> 72.2 us
  matrix products: 107 us -> 89.2 us
    pallas_call x4 -> x6, Pallas kernels: 393 us -> 511 us  [the longest x3 175 us: exchange(): pl.pallas_call(functools.partial(exchange_kernel, to_blocks, width, last_...]
    all_to_all x3 -> x0, waiting for transfers between devices: 86.5 us -> none  [ff_home(): part = lax.all_to_all(jnp.transpose(part, (1, 0, 2)), SEQ, 0, 0, tiled=True)]
    ppermute x38 -> x11, waiting for transfers between devices: 150 us -> 78.6 us  [swap(): return lax.ppermute(x, axis, [(0, 1), (1, 0)])]
    ppermute x9 -> x6, waiting for transfers between devices: 40.9 us -> 80.5 us  [chain_pieces(): out.append(lax.ppermute(x, SEQ + ('ha',), perm))]
    reduce_scatter x4 -> x2, waiting for transfers between devices: 40.4 us -> 9.4 us  [the longest x1 9.4 us: on_device(): branch = lax.psum_scatter(branch, QUAD, scatter_dimension=0, tiled=True)]
    ppermute x38 -> x11, starting transfers between devices: 36.4 us -> 6.81 us  [swap(): return lax.ppermute(x, axis, [(0, 1), (1, 0)])]
    dot_general x20 -> x17, matrix products: 96.3 us -> 77.9 us  [dot(): return lax.dot_general(a, b, dims, preferred_element_type=F32)]
    ppermute x9 -> x6, starting transfers between devices: 24.6 us -> 8.47 us  [chain_pieces(): out.append(lax.ppermute(x, SEQ + ('ha',), perm))]
  transfers between devices with their start and end apart: 55 -> 21, of which waited for: 21 -> 14; matrix products, arithmetic and copies ran while one was open for 17% -> 14% of each run, Pallas kernels for 20% -> 31%
where the time goes in v3:
time: 1160 us; the launch traced here: 1150 us
  Pallas kernels  693 us (60%)
  waiting for transfers between devices  198 us (17%)
  matrix products  89.2 us (8%)
  local copies, waits for them, and re-layouts  72.2 us (6%)
  other arithmetic  68.6 us (6%)
  starting transfers between devices  16 us (1%)
  between operations  15.1 us (1%)
    pallas_call x3, Pallas kernels, exchange(): pl.pallas_call(functools.partial(exchange_kernel, to_blocks, width, last_...  175 us
    pallas_call x1, Pallas kernels, start(): pl.pallas_call(functools.partial(start_kernel, parts), out_shape=[jax.Sha...  168 us
    pallas_call x1, Pallas kernels, send_home(): pl.pallas_call(home_kernel, out_shape=[jax.ShapeDtypeStruct(v.shape, v.dt...  113 us
    pallas_call x4, Pallas kernels, ff_chunk(): pl.pallas_call(ff_kernel, out_shape=(keep, keep, keep, held_shape, held_s...  99.4 us
    ppermute x6, waiting for transfers between devices, chain_pieces(): out.append(lax.ppermute(x, SEQ + ('ha',), perm))  80.5 us
    ppermute x11, waiting for transfers between devices, swap(): return lax.ppermute(x, axis, [(0, 1), (1, 0)])  78.6 us
    dot_general x17, matrix products, dot(): return lax.dot_general(a, b, dims, preferred_element_type=F32)  77.9 us
    pallas_call x6, Pallas kernels, row_call(): pl.pallas_call(kernel, out_shape=tuple((jax.ShapeDtypeStruct(s, t) for s,...  67.9 us
  transfers between devices with their start and end apart: 21, of which 14 were waited for; matrix products, arithmetic and copies ran while one was open for 14% of the time, Pallas kernels for 31%

profile of v3, /device:TPU:0, one launch (start us, length us, event | category | flops | bytes accessed | tf_op | source)
XLA Modules:
  0.0 1152.1 jit_solution(17536487867515900327)
XLA Ops:
  23.8 167.9 %shard_map.256 = (bf16[8,3,128,2048]{3,2,1,0:T(8,128)(2,1)}, bf16[384,2048]{1,0:T(8,128)(2,1)}, bf16[8,256,1024]{2,1,0:T(8,128)(2,1)}) custom-call(bf16[3,128,2048]{2,1,0:T(8,128)(2,1)} %fusion.5.src, bf16[384,2048]{1,0:T(8,128)(2,1)} %maximum_maximum_fusion.w_in, bf16[256,1024]{1,0:T(8,128)(2,1)} %constant_dynamic-slice_fusion.6.w_out), custom_call_target="tpu_custom_call" | custom-call | bytes 314572800 | tf_op jit(solution)/shard_map/pallas_call | solution.py:809
  191.8 11.2 convolution_convert_fusion.4.x_ref
  215.4 10.8 shard_map.257
  229.7 17.9 %collective-permute-done.1.rest_1_ = bf16[3,2,136,256]{3,2,1,0:T(8,128)(2,1)S(1)} collective-permute-done((bf16[3,2,136,256]{3,2,1,0:T(8,128)(2,1)}, bf16[3,2,136,256]{3,2,1,0:T(8,128)(2,1)S(1)}, u32[]{:S(2)}, u32[]{:S(2)}) %collective-permute-start.1) | collective-permute-done | bytes 417824 | tf_op jit(solution)/shard_map/ppermute | solution.py:847
  247.6 16.6 %collective-permute-done.2.rest_2_ = bf16[3,2,136,256]{3,2,1,0:T(8,128)(2,1)S(1)} collective-permute-done((bf16[3,2,136,256]{3,2,1,0:T(8,128)(2,1)}, bf16[3,2,136,256]{3,2,1,0:T(8,128)(2,1)S(1)}, u32[]{:S(2)}, u32[]{:S(2)}) %collective-permute-start.2) | collective-permute-done | bytes 417824 | tf_op jit(solution)/shard_map/ppermute | solution.py:847
  265.0 9.1 shard_map.259
  274.1 75.5 %shard_map.260 = (bf16[384,2048]{1,0:T(8,128)(2,1)}, bf16[3,384,2048]{2,1,0:T(8,128)(2,1)}, bf16[8,256,1024]{2,1,0:T(8,128)(2,1)}) custom-call(bf16[8,384,256]{2,1,0:T(8,128)(2,1)} %bitcast.221, bf16[384,2048]{1,0:T(8,128)(2,1)} %bitcast.219, bf16[8,256,1024]{2,1,0:T(8,128)(2,1)} %get-tuple-element.86.refs_1_), custom_call_target="tpu_custom_call" | custom-call | bytes 393216000 | tf_op jit(solution)/shard_map/pallas_call | solution.py:485
  360.9 29.8 %all-gather.5.cloned.1.call-done = bf16[2112,2048]{1,0:T(8,128)(2,1)} async-done(((bf16[528,2048]{1,0:T(8,128)(2,1)}), bf16[2112,2048]{1,0:T(8,128)(2,1)}) %all-gather.5.cloned.1.call-update) | async-done | bytes 8650768 | tf_op jit(solution)/shard_map/all_gather | solution.py:1110
  390.7 56.2 %shard_map.261 = (bf16[3,384,2048]{2,1,0:T(8,128)(2,1)}, bf16[4,528,2048]{2,1,0:T(8,128)(2,1)}) custom-call(bf16[384,2048]{1,0:T(8,128)(2,1)} %bitcast.223, bf16[4,528,2048]{2,1,0:T(8,128)(2,1)} %bitcast.192), custom_call_target="tpu_custom_call" | custom-call | bytes 157286400 | tf_op jit(solution)/shard_map/pallas_call | solution.py:640
  456.6 24.6 %shard_map.262 = (bf16[2,4,384,704]{3,2,1,0:T(8,128)(2,1)}, bf16[2,4,384,704]{3,2,1,0:T(8,128)(2,1)}, bf16[2,4,384,704]{3,2,1,0:T(8,128)(2,1)}, bf16[4,384,2048]...) custom-call(s32[1]{0:T(128)} %constant.80.clone.1.meta, bf16[384,2048]{1,0:T(8,128)(2,1)} %bitcast.224, ...), custom_call_target="tpu_custom_call" | custom-call | flops 11072962560 | bytes 23592960 | tf_op jit(solution)/shard_map/pallas_call | solution.py:938
  481.2 24.9 %shard_map.263 = (bf16[2,4,384,704]{3,2,1,0:T(8,128)(2,1)}, bf16[2,4,384,704]{3,2,1,0:T(8,128)(2,1)}, bf16[2,4,384,704]{3,2,1,0:T(8,128)(2,1)}, bf16[4,384,2048]...) custom-call(s32[1]{0:T(128)} %constant.79.clone.1.meta, ...), custom_call_target="tpu_custom_call", output_to_operand_aliasing={{0}: (5, {}), {1}: (6, {}), {2}: (7, {}), {3}: (8, {}), {4}... | custom-call | flops 11072962560 | bytes 23592960 | tf_op jit(solution)/shard_map/pallas_call | solution.py:938
  506.1 25.0 %shard_map.264 = (bf16[2,4,384,704]{3,2,1,0:T(8,128)(2,1)}, bf16[2,4,384,704]{3,2,1,0:T(8,128)(2,1)}, bf16[2,4,384,704]{3,2,1,0:T(8,128)(2,1)}, bf16[4,384,2048]...) custom-call(s32[1]{0:T(128)} %constant.78.clone.1.meta, ...), custom_call_target="tpu_custom_call", output_to_operand_aliasing={{0}: (5, {}), {1}: (6, {}), {2}: (7, {}), {3}: (8, {}), {4}... | custom-call | flops 11072962560 | bytes 23592960 | tf_op jit(solution)/shard_map/pallas_call | solution.py:938
  531.1 24.9 %shard_map.265 = (bf16[2,4,384,704]{3,2,1,0:T(8,128)(2,1)}, bf16[2,4,384,704]{3,2,1,0:T(8,128)(2,1)}, bf16[2,4,384,704]{3,2,1,0:T(8,128)(2,1)}, bf16[4,384,2048]...) custom-call(s32[1]{0:T(128)} %constant.81.clone.1.meta, ...), custom_call_target="tpu_custom_call", output_to_operand_aliasing={{0}: (5, {}), {1}: (6, {}), {2}: (7, {}), {3}: (8, {}), {4}... | custom-call | flops 11072962560 | bytes 23592960 | tf_op jit(solution)/shard_map/pallas_call | solution.py:938
  590.1 6.5 fusion.43
  596.7 6.8 fusion.42
  603.5 14.0 %shard_map.266 = bf16[1536,2048]{1,0:T(8,128)(2,1)S(1)} custom-call(s32[4]{0:T(128)S(1)} %pad_add_fusion.order, bf16[2,4,384,704]{3,2,1,0:T(8,128)(2,1)S(1)} %bitcast.191, bf16[4,528,2048]{2,1,0:T(8,128)(2,1)} %bitcast.197, bf16[4,528,2048]{2,1,0:T(8,128)(2,1)} %get-tuple-element.93.theirs), custom_call_target="tpu_custom_call" | custom-call | flops 8858370048 | bytes 17301504 | tf_op jit(solution)/shard_map/pallas_call | solution.py:971
  624.1 10.8 add_convert_fusion.1
  647.3 19.7 %collective-permute-done.10 = bf16[192,2048]{1,0:T(8,128)(2,1)S(1)} collective-permute-done((bf16[192,2048]{1,0:T(8,128)(2,1)S(1)}, bf16[192,2048]{1,0:T(8,128)(2,1)S(1)}, u32[]{:S(2)}, u32[]{:S(2)}) %collective-permute-start.10) | collective-permute-done | bytes 786464 | tf_op jit(solution)/shard_map/ppermute | solution.py:831
  685.6 58.7 %shard_map.267 = bf16[8,384,256]{2,1,0:T(8,128)(2,1)} custom-call(bf16[384,2048]{1,0:T(8,128)(2,1)} %add_convert_fusion.5.src), custom_call_target="tpu_custom_call" | custom-call | bytes 393216000 | tf_op jit(solution)/shard_map/pallas_call | solution.py:485
  744.3 7.2 pad_maximum_fusion
  751.5 9.4 reduce-scatter.3.cloned.1.call-done
  767.0 7.5 collective-permute-done.15
  782.8 47.7 %collective-permute-done.16 = bf16[2048,512]{1,0:T(8,128)(2,1)S(1)} collective-permute-done((bf16[2048,512]{1,0:T(8,128)(2,1)}, bf16[2048,512]{1,0:T(8,128)(2,1)S(1)}, u32[]{:S(2)}, u32[]{:S(2)}) %collective-permute-start.16) | collective-permute-done | bytes 2097184 | tf_op jit(solution)/shard_map/ppermute | solution.py:831
  834.0 9.4 fusion.35
  843.4 9.5 shard_map.268
  857.0 22.7 %shard_map.269 = (f32[3,1024,128]{2,1,0:T(8,128)}, f32[3,1024,256]{2,1,0:T(8,128)}) custom-call(s32[3,8]{1,0:T(4,128)} %lens.11, s32[1]{0:T(128)} %bitcast.1.meta, bf16[8,3,128,384]{3,2,1,0:T(8,128)(2,1)} %convolution_convert_fusion.4.x_ref, bf16[3,1024,512]{2,1,0:T(8,128)(2,1)} %get-tuple-element.137.gn_ref, ...), custom_call_target="tpu_custom_call" | custom-call | flops 12884901888 | bytes 11436032 | tf_op jit(solution)/shard_map/pallas_call | solution.py:304
  881.4 22.1 %collective-permute-done.12.rest_0_ = bf16[3,2,136,256]{3,2,1,0:T(8,128)(2,1)S(1)} collective-permute-done((bf16[3,2,136,256]{3,2,1,0:T(8,128)(2,1)}, bf16[3,2,136,256]{3,2,1,0:T(8,128)(2,1)S(1)}, u32[]{:S(2)}, u32[]{:S(2)}) %collective-permute-start.12) | collective-permute-done | bytes 417824 | tf_op jit(solution)/shard_map/ppermute | solution.py:847
  905.1 18.8 %collective-permute-done.14.rest_2_ = bf16[3,2,136,256]{3,2,1,0:T(8,128)(2,1)S(1)} collective-permute-done((bf16[3,2,136,256]{3,2,1,0:T(8,128)(2,1)}, bf16[3,2,136,256]{3,2,1,0:T(8,128)(2,1)S(1)}, u32[]{:S(2)}, u32[]{:S(2)}) %collective-permute-start.14) | collective-permute-done | bytes 417824 | tf_op jit(solution)/shard_map/ppermute | solution.py:847
  924.7 9.6 shard_map.270
  934.2 40.5 %shard_map.271 = bf16[384,3072]{1,0:T(8,128)(2,1)} custom-call(bf16[8,384,384]{2,1,0:T(8,128)(2,1)} %bitcast.216), custom_call_target="tpu_custom_call" | custom-call | bytes 589824000 | tf_op jit(solution)/shard_map/pallas_call | solution.py:485
  987.2 9.6 bitcast_convert_fusion
  1013.9 112.7 %shard_map.272 = (f32[32,8,128]{2,1,0:T(8,128)}, bf16[4,384,512]{2,1,0:T(8,128)(2,1)}, bf16[4,528,512]{2,1,0:T(8,128)(2,1)}, bf16[8,256,512]{2,1,0:T(8,128)(2,1)}) custom-call(f32[32,8,128]{2,1,0:T(8,128)} %pad.4.refs_0_, bf16[4,384,512]{2,1,0:T(8,128)(2,1)} %bitcast.226, bf16[4,528,512]{2,1,0:T(8,128)(2,1)} %bitcast.217, bf16[8,256,512]{2,1,0:T(8,128)(2,1)} %bitcast.218), custom_call_target="tpu_custom_call" | custom-call | bytes 100000000 | tf_op jit(solution)/shard_map/pallas_call | solution.py:590
  (232 shorter events, 199.4 us)
Async XLA Ops:
  7.2 10.4 copy-start
  7.2 383.6 %all-gather.5.cloned.1.call-start = ((), (), s32[]{:S(2)}) async-start(), calls=%async_computation.4 | async-start | bytes 10813440 | tf_op jit(solution)/shard_map/all_gather | solution.py:1110
  191.7 450.8 %all-gather.7.cloned.1.call-start = ((), (), s32[]{:S(2)}) async-start(), calls=%async_computation.5 | async-start | bytes 12976128 | tf_op jit(solution)/shard_map/all_gather | solution.py:1164
  209.2 20.5 %collective-permute-start = (bf16[3,2,136,256]{3,2,1,0:T(8,128)(2,1)}, bf16[3,2,136,256]{3,2,1,0:T(8,128)(2,1)S(1)}, u32[]{:S(2)}, u32[]{:S(2)}) collective-permute-start(bf16[3,2,136,256]{3,2,1,0:T(8,128)(2,1)} %shard_map.258), channel_id=1, source_target_pairs={{0,4},{8,12},{16,20},{24,28},{4,18},{12,26},{20,2},{28,10},{18,22}... | collective-permute-start | bytes 1253384 | tf_op jit(solution)/shard_map/ppermute | solution.py:847
  210.5 37.1 %collective-permute-start.1 = (bf16[3,2,136,256]{3,2,1,0:T(8,128)(2,1)}, bf16[3,2,136,256]{3,2,1,0:T(8,128)(2,1)S(1)}, u32[]{:S(2)}, u32[]{:S(2)}) collective-permute-start(bf16[3,2,136,256]{3,2,1,0:T(8,128)(2,1)} %shard_map.258), channel_id=1, source_target_pairs={{0,18},{8,26},{16,2},{24,10},{4,22},{12,30},{20,6},{28,14},{1,19},... | collective-permute-start | bytes 1253384 | tf_op jit(solution)/shard_map/ppermute | solution.py:847
  211.8 52.4 %collective-permute-start.2 = (bf16[3,2,136,256]{3,2,1,0:T(8,128)(2,1)}, bf16[3,2,136,256]{3,2,1,0:T(8,128)(2,1)S(1)}, u32[]{:S(2)}, u32[]{:S(2)}) collective-permute-start(bf16[3,2,136,256]{3,2,1,0:T(8,128)(2,1)} %shard_map.258), channel_id=1, source_target_pairs={{0,22},{8,30},{16,6},{24,14},{1,23},{9,31},{17,7},{25,15}} | collective-permute-start | bytes 1253384 | tf_op jit(solution)/shard_map/ppermute | solution.py:847
  229.7 34.5 %copy-start.43 = (bf16[3,2,136,256]{3,2,1,0:T(8,128)(2,1)}, bf16[3,2,136,256]{3,2,1,0:T(8,128)(2,1)S(1)}, u32[]{:S(2)}) copy-start(bf16[3,2,136,256]{3,2,1,0:T(8,128)(2,1)S(1)} %collective-permute-done.rest_0_) | copy-start | bytes 1253380
  247.6 16.6 %copy-start.44 = (bf16[3,2,136,256]{3,2,1,0:T(8,128)(2,1)}, bf16[3,2,136,256]{3,2,1,0:T(8,128)(2,1)S(1)}, u32[]{:S(2)}) copy-start(bf16[3,2,136,256]{3,2,1,0:T(8,128)(2,1)S(1)} %collective-permute-done.1.rest_1_) | copy-start | bytes 1253380
  451.7 309.3 %reduce-scatter.3.cloned.1.call-start = ((), (), s32[]{:S(2)}) async-start(), calls=%async_computation.2 | async-start | bytes 7864320 | tf_op jit(solution)/shard_map/reduce_scatter | solution.py:1178
  556.0 7.7 slice-start.4
  558.9 61.2 %collective-permute-start.3 = (bf16[192,2048]{1,0:T(8,128)(2,1)}, bf16[192,2048]{1,0:T(8,128)(2,1)S(1)}, u32[]{:S(2)}, u32[]{:S(2)}) collective-permute-start(bf16[192,2048]{1,0:T(8,128)(2,1)} %get-tuple-element.229), channel_id=1, source_target_pairs={{0,1},{1,0},{2,3},{3,2},{4,5},{5,4},{6,7},{7,6},{8,9},{9,8},{10,11... | collective-permute-start | bytes 2359304 | tf_op jit(solution)/shard_map/ppermute | solution.py:831
  559.7 60.4 %collective-permute-start.4 = (bf16[192,2048]{1,0:T(8,128)(2,1)}, bf16[192,2048]{1,0:T(8,128)(2,1)S(1)}, u32[]{:S(2)}, u32[]{:S(2)}) collective-permute-start(bf16[192,2048]{1,0:T(8,128)(2,1)} %get-tuple-element.228), channel_id=1, source_target_pairs={{0,16},{16,0},{1,17},{17,1},{2,18},{18,2},{3,19},{19,3},{4,20},{20... | collective-permute-start | bytes 2359304 | tf_op jit(solution)/shard_map/ppermute | solution.py:831
  570.2 49.9 %collective-permute-start.5 = (bf16[704,2048]{1,0:T(8,128)(2,1)}, bf16[704,2048]{1,0:T(8,128)(2,1)}, u32[]{:S(2)}, u32[]{:S(2)}) collective-permute-start(bf16[704,2048]{1,0:T(8,128)(2,1)} %convolution_convert_fusion.3), channel_id=1, source_target_pairs={{0,8},{8,0},{1,9},{9,1},{2,10},{10,2},{3,11},{11,3},{4,12},{12,4},... | collective-permute-start | bytes 8650760 | tf_op jit(solution)/shard_map/ppermute | solution.py:831
  570.2 7.3 slice-start.6
  570.6 6.9 slice-start.7
  576.7 43.4 %collective-permute-start.6 = (bf16[704,2048]{1,0:T(8,128)(2,1)}, bf16[704,2048]{1,0:T(8,128)(2,1)}, u32[]{:S(2)}, u32[]{:S(2)}) collective-permute-start(bf16[704,2048]{1,0:T(8,128)(2,1)} %convolution_convert_fusion.2), channel_id=1, source_target_pairs={{0,8},{8,0},{1,9},{9,1},{2,10},{10,2},{3,11},{11,3},{4,12},{12,4},... | collective-permute-start | bytes 8650760 | tf_op jit(solution)/shard_map/ppermute | solution.py:831
  583.6 36.5 %collective-permute-start.7 = (bf16[704,2048]{1,0:T(8,128)(2,1)}, bf16[704,2048]{1,0:T(8,128)(2,1)}, u32[]{:S(2)}, u32[]{:S(2)}) collective-permute-start(bf16[704,2048]{1,0:T(8,128)(2,1)} %convolution_convert_fusion.1), channel_id=1, source_target_pairs={{0,8},{8,0},{1,9},{9,1},{2,10},{10,2},{3,11},{11,3},{4,12},{12,4},... | collective-permute-start | bytes 8650760 | tf_op jit(solution)/shard_map/ppermute | solution.py:831
  621.7 20.0 %collective-permute-start.8 = (bf16[192,2048]{1,0:T(8,128)(2,1)S(1)}, bf16[192,2048]{1,0:T(8,128)(2,1)S(1)}, u32[]{:S(2)}, u32[]{:S(2)}) collective-permute-start(bf16[192,2048]{1,0:T(8,128)(2,1)S(1)} %add_convert_fusion.7), channel_id=1, source_target_pairs={{0,16},{16,0},{1,17},{17,1},{2,18},{18,2},{3,19},{19,3},{4,20},{20... | collective-permute-start | bytes 2359304 | tf_op jit(solution)/shard_map/ppermute | solution.py:831
  622.8 19.7 %collective-permute-start.9 = (bf16[192,2048]{1,0:T(8,128)(2,1)S(1)}, bf16[192,2048]{1,0:T(8,128)(2,1)S(1)}, u32[]{:S(2)}, u32[]{:S(2)}) collective-permute-start(bf16[192,2048]{1,0:T(8,128)(2,1)S(1)} %add_convert_fusion.6), channel_id=1, source_target_pairs={{0,1},{1,0},{2,3},{3,2},{4,5},{5,4},{6,7},{7,6},{8,9},{9,8},{10,11... | collective-permute-start | bytes 2359304 | tf_op jit(solution)/shard_map/ppermute | solution.py:831
  643.4 364.1 %reduce-scatter.5.cloned.1.call-start = ((), (), s32[]{:S(2)}) async-start(), calls=%async_computation.3 | async-start | bytes 10813440 | tf_op jit(solution)/shard_map/reduce_scatter | solution.py:1181
  645.2 21.8 %collective-permute-start.10 = (bf16[192,2048]{1,0:T(8,128)(2,1)S(1)}, bf16[192,2048]{1,0:T(8,128)(2,1)S(1)}, u32[]{:S(2)}, u32[]{:S(2)}) collective-permute-start(bf16[192,2048]{1,0:T(8,128)(2,1)S(1)} %slice.184), channel_id=1, source_target_pairs={{0,1},{1,0},{2,3},{3,2},{4,5},{5,4},{6,7},{7,6},{8,9},{9,8},{10,11... | collective-permute-start | bytes 2359304 | tf_op jit(solution)/shard_map/ppermute | solution.py:831
  646.5 22.8 %collective-permute-start.11 = (bf16[192,2048]{1,0:T(8,128)(2,1)S(1)}, bf16[192,2048]{1,0:T(8,128)(2,1)S(1)}, u32[]{:S(2)}, u32[]{:S(2)}) collective-permute-start(bf16[192,2048]{1,0:T(8,128)(2,1)S(1)} %slice.186), channel_id=1, source_target_pairs={{0,16},{16,0},{1,17},{17,1},{2,18},{18,2},{3,19},{19,3},{4,20},{20... | collective-permute-start | bytes 2359304 | tf_op jit(solution)/shard_map/ppermute | solution.py:831
  761.2 13.4 %copy-start.42 = (bf16[384,2048]{1,0:T(8,128)(2,1)S(1)}, bf16[384,2048]{1,0:T(8,128)(2,1)}, u32[]{:S(2)}) copy-start(bf16[384,2048]{1,0:T(8,128)(2,1)} %get-tuple-element.87) | copy-start | bytes 4718596
  767.0 7.5 collective-permute-start.15
  782.6 47.9 %collective-permute-start.16 = (bf16[2048,512]{1,0:T(8,128)(2,1)}, bf16[2048,512]{1,0:T(8,128)(2,1)S(1)}, u32[]{:S(2)}, u32[]{:S(2)}) collective-permute-start(bf16[2048,512]{1,0:T(8,128)(2,1)} %constant_dynamic-slice_fusion), channel_id=1, source_target_pairs={{0,16},{16,0},{1,17},{17,1},{2,18},{18,2},{3,19},{19,3},{4,20},{20... | collective-permute-start | bytes 6291464 | tf_op jit(solution)/shard_map/ppermute | solution.py:831
  852.9 50.6 %collective-permute-start.12 = (bf16[3,2,136,256]{3,2,1,0:T(8,128)(2,1)}, bf16[3,2,136,256]{3,2,1,0:T(8,128)(2,1)S(1)}, u32[]{:S(2)}, u32[]{:S(2)}) collective-permute-start(bf16[3,2,136,256]{3,2,1,0:T(8,128)(2,1)} %get-tuple-element.141), channel_id=1, source_target_pairs={{4,0},{12,8},{20,16},{28,24},{18,4},{26,12},{2,20},{10,28},{22,18}... | collective-permute-start | bytes 1253384 | tf_op jit(solution)/shard_map/ppermute | solution.py:847
  854.2 50.9 %collective-permute-start.13 = (bf16[3,2,136,256]{3,2,1,0:T(8,128)(2,1)}, bf16[3,2,136,256]{3,2,1,0:T(8,128)(2,1)S(1)}, u32[]{:S(2)}, u32[]{:S(2)}) collective-permute-start(bf16[3,2,136,256]{3,2,1,0:T(8,128)(2,1)} %get-tuple-element.141), channel_id=1, source_target_pairs={{18,0},{26,8},{2,16},{10,24},{22,4},{30,12},{6,20},{14,28},{19,1},... | collective-permute-start | bytes 1253384 | tf_op jit(solution)/shard_map/ppermute | solution.py:847
  855.5 68.4 %collective-permute-start.14 = (bf16[3,2,136,256]{3,2,1,0:T(8,128)(2,1)}, bf16[3,2,136,256]{3,2,1,0:T(8,128)(2,1)S(1)}, u32[]{:S(2)}, u32[]{:S(2)}) collective-permute-start(bf16[3,2,136,256]{3,2,1,0:T(8,128)(2,1)} %get-tuple-element.141), channel_id=1, source_target_pairs={{22,0},{30,8},{6,16},{14,24},{23,1},{31,9},{7,17},{15,25}} | collective-permute-start | bytes 1253384 | tf_op jit(solution)/shard_map/ppermute | solution.py:847
  857.0 22.7 %copy-start.5 = (f32[3,128,2048]{2,1,0:T(8,128)S(1)}, f32[3,128,2048]{2,1,0:T(8,128)}, u32[]{:S(2)}) copy-start(f32[3,128,2048]{2,1,0:T(8,128)} %copy-done.3) | copy-start | bytes 9437188
  857.0 22.7 %copy-start.21 = (bf16[384,2048]{1,0:T(8,128)(2,1)S(1)}, bf16[384,2048]{1,0:T(8,128)(2,1)}, u32[]{:S(2)}) copy-start(bf16[384,2048]{1,0:T(8,128)(2,1)} %reduce-scatter.3.cloned.1.call-done) | copy-start | bytes 4718596
  903.4 20.5 %copy-start.29 = (bf16[3,2,136,256]{3,2,1,0:T(8,128)(2,1)}, bf16[3,2,136,256]{3,2,1,0:T(8,128)(2,1)S(1)}, u32[]{:S(2)}) copy-start(bf16[3,2,136,256]{3,2,1,0:T(8,128)(2,1)S(1)} %collective-permute-done.12.rest_0_) | copy-start | bytes 1253380
  905.1 18.8 %copy-start.30 = (bf16[3,2,136,256]{3,2,1,0:T(8,128)(2,1)}, bf16[3,2,136,256]{3,2,1,0:T(8,128)(2,1)S(1)}, u32[]{:S(2)}) copy-start(bf16[3,2,136,256]{3,2,1,0:T(8,128)(2,1)S(1)} %collective-permute-done.13.rest_1_) | copy-start | bytes 1253380
  (43 other events, 146.6 us)
Sparse Core Ops, SparseCore 0:
  191.8 198.8 all-gather.4
  451.8 105.3 all-gather.6
  642.7 118.1 reduce-scatter.2
  763.2 193.4 reduce-scatter.4

commit v4 on v3

--- a/solution.py
+++ b/solution.py
@@ -433,18 +433,21 @@
         half = more.shape[0] // 2
         low, high = pl.ds(0, half), pl.ds(half, half)
         copies = [
-            remote(more, near.at[0], gsem, hsem, 0, to_x),
-            remote(more, near.at[1], gsem, hsem, 1, to_y),
+            remote(more, near.at[1], gsem, hsem, 0, to_x),
+            remote(more, near.at[2], gsem, hsem, 1, to_y),
             remote(own_w, other_w, gsem, hsem, 4, to_core),
         ]
         for c in copies:
             c.start()
+        stay = pltpu.make_async_copy(more, near.at[0], lsem.at[1])
+        stay.start()
         copies[0].wait_recv()
-        copies.append(remote(near.at[0, high], near.at[2, high], gsem, hsem, 2, to_y))
+        copies.append(remote(near.at[1, high], near.at[3, high], gsem, hsem, 2, to_y))
         copies[3].start()
         copies[1].wait_recv()
-        copies.append(remote(near.at[1, low], near.at[2, low], gsem, hsem, 3, to_x))
+        copies.append(remote(near.at[2, low], near.at[3, low], gsem, hsem, 3, to_x))
         copies[4].start()
+        stay.wait()
         for c in copies[2:]:
             c.wait_recv()
         for c in copies:
@@ -490,7 +493,7 @@
         scratch_shapes=[
             pltpu.SemaphoreType.DMA((count,)),
             pltpu.SemaphoreType.DMA((count,)),
-            pltpu.SemaphoreType.DMA((1,)),
+            pltpu.SemaphoreType.DMA((2,)),
         ]
         + [pltpu.SemaphoreType.DMA((more,))] * (2 if more else 0),
         compiler_params=pltpu.CompilerParams(collective_id=collective, has_side_effects=True),
@@ -537,28 +540,26 @@
         return remote(windows.at[e], windows_got.at[s], gsem, hsem, size_a + k, (e // 2, e % 2, a, b))
 
     def shard_copy(k):
-        pa, pb = lax.rem(a + k // size_b, size_a), lax.rem(b + k % size_b, size_b)
-        far = shards_got.at[a * size_b + b]
-        return remote(shards.at[pa * size_b + pb], far, usem, vsem, k, (sy, sc, pa, pb))
+        pa = lax.rem(a + k, size_a)
+        return remote(shards.at[pa], shards_got.at[a], usem, vsem, k, (sy, sc, pa, b))
 
     @pl.loop(1, devices)
     def _(k):
         pl.semaphore_signal(bar, 1, device_id=peer(k)[1], device_id_type=MESH_ID)
 
     stay = [
-        pltpu.make_async_copy(shards.at[a * size_b + b], shards_got.at[a * size_b + b], lsem.at[3]),
+        pltpu.make_async_copy(shards.at[a], shards_got.at[a], lsem.at[3]),
         pltpu.make_async_copy(src.at[me], dst.at[me], lsem.at[0]),
         pltpu.make_async_copy(windows.at[s], windows_got.at[s], lsem.at[2]),
     ]
     for c in stay:
         c.start()
     pl.semaphore_wait(bar, devices - 1)
-    heads = size_a * size_b
     for k in range(size_a):
         maybe_own(k, homely, lambda: grad_copy(k).start(), lambda: grad_local().start())
         if k:
             window_copy(k).start()
-    for k in range(1, heads):
+    for k in range(1, size_a):
         shard_copy(k).start()
 
     @pl.loop(1, devices)
@@ -573,7 +574,7 @@
         maybe_own(k, homely, lambda: grad_copy(k).wait(), lambda: grad_local().wait())
         if k:
             window_copy(k).wait()
-    for k in range(1, heads):
+    for k in range(1, size_a):
         shard_copy(k).wait()
     for c in stay:
         c.wait()
@@ -608,25 +609,28 @@
     return vectors, jnp.sum(out[1].astype(F32), axis=0), out[2], jnp.sum(out[3].astype(F32), axis=0)
 
 
-def near_kernel(rows, src, weights, near, theirs, gsem, hsem):
+def near_kernel(rows, src, weights, near, theirs, gsem, hsem, lsem):
     sy, sc, a, b = here()
     to_x, to_y, to_core = (sy, sc, a, 1 - b), (1 - sy, sc, a, b), (sy, 1 - sc, a, b)
     half = src.shape[0] // 2
     low, high = pl.ds(0, half), pl.ds(half, half)
     greet((to_x, to_y, to_core))
     copies = [
-        remote(src, near.at[0], gsem, hsem, 0, to_x),
-        remote(src, near.at[1], gsem, hsem, 1, to_y),
+        remote(src, near.at[1], gsem, hsem, 0, to_x),
+        remote(src, near.at[2], gsem, hsem, 1, to_y),
         remote(weights.at[:, pl.ds(0, rows)], theirs, gsem, hsem, 4, to_core),
     ]
     for copy in copies:
         copy.start()
+    stay = pltpu.make_async_copy(src, near.at[0], lsem)
+    stay.start()
     copies[0].wait_recv()
-    copies.append(remote(near.at[0, high], near.at[2, high], gsem, hsem, 2, to_y))
+    copies.append(remote(near.at[1, high], near.at[3, high], gsem, hsem, 2, to_y))
     copies[3].start()
     copies[1].wait_recv()
-    copies.append(remote(near.at[1, low], near.at[2, low], gsem, hsem, 3, to_x))
+    copies.append(remote(near.at[2, low], near.at[3, low], gsem, hsem, 3, to_x))
     copies[4].start()
+    stay.wait()
     for copy in copies[2:]:
         copy.wait_recv()
     for copy in copies:
@@ -635,21 +639,21 @@
 
 def gather_near(x, weights, rows, collective):
     if not square():
-        return (lax.all_gather(x, QUAD, axis=0, tiled=True),), swap(weights[:, :rows], "sc")
+        return lax.all_gather(x, QUAD, axis=0, tiled=True)[None], swap(weights[:, :rows], "sc")
     any_space = pl.BlockSpec(memory_space=pl.ANY)
     near, theirs = pl.pallas_call(
         functools.partial(near_kernel, rows),
         out_shape=[
-            jax.ShapeDtypeStruct((3,) + x.shape, x.dtype),
+            jax.ShapeDtypeStruct((4,) + x.shape, x.dtype),
             jax.ShapeDtypeStruct((weights.shape[0], rows, weights.shape[2]), weights.dtype),
         ],
         in_specs=[any_space] * 2,
         out_specs=[any_space] * 2,
-        scratch_shapes=[pltpu.SemaphoreType.DMA((5,))] * 2,
+        scratch_shapes=[pltpu.SemaphoreType.DMA((5,))] * 2 + [pltpu.SemaphoreType.DMA],
         compiler_params=pltpu.CompilerParams(collective_id=collective, has_side_effects=True),
         cost_estimate=pl.CostEstimate(flops=0, bytes_accessed=x.size * 200, transcendentals=0),
     )(x, weights)
-    return (x, near[0], near[1], near[2]), theirs
+    return near, theirs
 
 
 def start_kernel(parts, src, w_in, w_out, dst, w_in_home, w_out_all, ssem, rsem, lsem, wsem, vsem):
@@ -892,12 +896,11 @@
     return jnp.concatenate(pieces, axis=0)
 
 
-def ff_kernel(meta, n2, cot, mine, theirs, *rest):
-    gg_out, gu_out, hid_out, n2_out, cot_out, part_out, acc = rest[-7:]
-    shard = pl.program_id(0)
+def ff_kernel(n2, cot, mine, theirs, gg_out, gu_out, hid_out, part_out, acc):
+    shard = pl.program_id(1)
 
     def work(w, first):
-        x, c = n2[...], cot[...]
+        x, c = n2[0], cot[0]
         window, width = w.shape[1] // 3, w.shape[2]
         w_gate, w_up, w_down = (w[:, i * window : (i + 1) * window].reshape(-1, width) for i in range(3))
         gate, up, gh = dot(x, w_gate, NT), dot(x, w_up, NT), dot(c, w_down, NT)
@@ -911,10 +914,8 @@
         back = dot(gg, w_gate) + dot(gu, w_up)
         if first:
             acc[...] = back
-            n2_out[0] = x
-            cot_out[0] = c
         else:
-            part_out[...] = (acc[...] + back).astype(BF)
+            part_out[0] = (acc[...] + back).astype(BF)
 
     @pl.when(shard == 0)
     def _():
@@ -925,34 +926,27 @@
         work(theirs, False)
 
 
-def ff_chunk(n2, cot, mine, theirs, place, chunks, kept):
-    tokens, width = n2.shape
+def ff_pass(n2, cots, mine, theirs):
+    chunks, tokens, width = n2.shape
     units = theirs.shape[0] * theirs.shape[1] // 3
     keep = jax.ShapeDtypeStruct((2, chunks, tokens, units), BF)
-    held_shape = jax.ShapeDtypeStruct((chunks, tokens, width), BF)
-    whole = pl.BlockSpec((tokens, width), lambda i, m: (0, 0))
-    weights = pl.BlockSpec(theirs.shape, lambda i, m: (0, 0, 0), pipeline_mode=pl.Buffered(1))
-    piece = pl.BlockSpec((1, 1, tokens, units), lambda i, m: (i, m[0], 0, 0))
-    held = pl.BlockSpec((1, tokens, width), lambda i, m: (m[0], 0, 0))
-    old = [] if kept is None else list(kept)
+    whole = pl.BlockSpec((1, tokens, width), lambda c, i: (c, 0, 0))
+    weights = pl.BlockSpec(theirs.shape, lambda c, i: (0, 0, 0), pipeline_mode=pl.Buffered(1))
+    piece = pl.BlockSpec((1, 1, tokens, units), lambda c, i: (i, c, 0, 0))
     return pl.pallas_call(
         ff_kernel,
-        out_shape=(keep, keep, keep, held_shape, held_shape, jax.ShapeDtypeStruct((tokens, width), BF)),
-        grid_spec=pltpu.PrefetchScalarGridSpec(
-            num_scalar_prefetch=1,
-            grid=(2,),
-            in_specs=[whole, whole, weights, weights] + [pl.BlockSpec(memory_space=pl.ANY)] * len(old),
-            out_specs=[piece, piece, piece, held, held, whole],
-            scratch_shapes=[pltpu.VMEM((tokens, width), F32)],
-        ),
-        input_output_aliases={5 + i: i for i in range(len(old))},
-        compiler_params=pltpu.CompilerParams(vmem_limit_bytes=58 * 1024 * 1024),
+        out_shape=(keep, keep, keep, jax.ShapeDtypeStruct((chunks, tokens, width), BF)),
+        grid=(chunks, 2),
+        in_specs=[whole, whole, weights, weights],
+        out_specs=[piece, piece, piece, whole],
+        scratch_shapes=[pltpu.VMEM((tokens, width), F32)],
+        compiler_params=pltpu.CompilerParams(vmem_limit_bytes=60 * 1024 * 1024),
         cost_estimate=pl.CostEstimate(
-            flops=tokens * width * units * 20,
-            bytes_accessed=12 * units * width + 8 * tokens * width,
+            flops=chunks * tokens * width * units * 20,
+            bytes_accessed=12 * units * width + 8 * chunks * tokens * width,
             transcendentals=0,
         ),
-    )(place, n2, cot, mine, theirs, *old)
+    )(n2, cots, mine, theirs)
 
 
 def branch_kernel(order, hidden, mine, theirs, out):
@@ -1009,21 +1003,17 @@
     return jnp.concatenate([low, high], axis=0)
 
 
-def seq_sum(a, b):
-    size_y, core, y = lax.axis_size("sy"), lax.axis_index("sc"), lax.axis_index("sy")
+def core_sum(a, b):
+    size_y, core = lax.axis_size("sy"), lax.axis_index("sc")
     size = b.shape[1] // (size_y * 2)
 
-    def columns(x, i):
-        return lax.dynamic_slice_in_dim(x, i * size, size, 1)
-
     def of_core(c):
-        return jnp.concatenate([columns(b, i * 2 + c) for i in range(size_y)], axis=1)
+        columns = [lax.dynamic_slice_in_dim(b, (i * 2 + c) * size, size, 1) for i in range(size_y)]
+        return jnp.concatenate(columns, axis=1)
 
     given = swap(dot(a, of_core(1 - core), TN).astype(BF), "sc")
     part = (dot(a, of_core(core), TN) + given.astype(F32)).astype(BF)
-    if size_y != 2:
-        return lax.psum_scatter(part, "sy", scatter_dimension=1, tiled=True)
-    return add_low(columns(part, y), swap(columns(part, 1 - y), "sy"))
+    return jnp.stack([part[:, i * size : (i + 1) * size] for i in range(size_y)])
 
 
 def quad_sum(parts, meanwhile):
@@ -1035,13 +1025,10 @@
 
 
 def ff_group(chunks, cots, mine, theirs):
-    kept, parts = None, []
-    for i, (chunk, cot) in enumerate(zip(chunks, cots)):
-        where = jnp.full((1,), i, jnp.int32)
-        *kept, part = ff_chunk(chunk, cot, mine, theirs, where, len(cots), kept)
-        parts.append(part)
+    *kept, part = ff_pass(chunks, cots, mine, theirs)
     grads, branch = [], []
-    flat = [k.reshape((2, -1, k.shape[-1]) if k.ndim == 4 else (-1, k.shape[-1])) for k in kept]
+    width = chunks.shape[-1]
+    flat = [k.reshape(2, -1, k.shape[-1]) for k in kept] + [chunks.reshape(-1, width), cots.reshape(-1, width)]
     pairs = [(flat[0], flat[3]), (flat[1], flat[3]), (flat[2], flat[4])]
 
     def meanwhile(stage, results=None):
@@ -1057,7 +1044,7 @@
         branch.append(branch_product(kept[2], mine, theirs))
         return grads + branch
 
-    return quad_sum(parts, meanwhile), grads, branch[0]
+    return quad_sum([part[i] for i in range(part.shape[0])], meanwhile), grads, branch[0]
 
 
 def rms_scale(x):
@@ -1144,13 +1131,12 @@
     )
     flat_cot, to_owners = cot.reshape(tokens, width), att.reshape(count, tokens, vw)
     if square():
-        attended, near, w_out_other = exchange(
-            to_owners, False, vw, 0, "gather", (flat_cot, w_out_piece), ((3, tokens, width), w_out_piece.shape)
+        attended, cots, w_out_other = exchange(
+            to_owners, False, vw, 0, "gather", (flat_cot, w_out_piece), ((4, tokens, width), w_out_piece.shape)
         )
-        cots = (flat_cot, near[0], near[1], near[2])
     else:
         (attended,) = exchange(to_owners, False, vw, 0)
-        cots = (lax.all_gather(flat_cot, QUAD, axis=0, tiled=True),)
+        cots = lax.all_gather(flat_cot, QUAD, axis=0, tiled=True)[None]
         w_out_other = swap(w_out_piece, "sc")
     w_out_halves = [w.reshape(count * vw, width // 2) for w in (w_out_piece, w_out_other)]
     attn_branch = by_halves(attended, *w_out_halves).reshape(rows_n, sub_len, width)
@@ -1181,7 +1167,8 @@
     ff_grads = lax.psum_scatter(ff_grads, "ha", scatter_dimension=0, tiled=True)
     grad_att = grad_att.reshape(count, rows_n, sub_len, vw)
     output = (middle + branch.astype(F32).reshape(rows_n, sub_len, width)).astype(BF)
-    grad_w_out = seq_sum(attended, flat_branch).reshape(count, vw, width // blocks)
+    part = core_sum(attended, flat_branch).reshape(-1, size_a, size_b, vw, width // blocks)
+    part = jnp.transpose(part, (0, 2, 1, 3, 4)).reshape(-1, size_a * vw, width // blocks)
     ff_grads = jnp.transpose(ff_grads.reshape(-1, 3, blocks, width // blocks), (2, 1, 0, 3))
     ff_grads = ff_grads.reshape(blocks, -1, width // blocks)
     gn, grad_states = row_call(
@@ -1209,7 +1196,21 @@
         [((count, rows_n, sub_len, xw), BF, 1)],
         nh * rows_n * length * 256 * 256 * 6,
     )
-    (grad_in,) = exchange(gqkv.reshape(count, tokens, xw), False, xw, 2, last_major=True)
+    to_owners = gqkv.reshape(count, tokens, xw)
+    if square():
+        y, b = lax.axis_index("sy"), lax.axis_index("hb")
+        turns = (y * 2 + b, y * 2 + 1 - b, (1 - y) * 2 + b, (1 - y) * 2 + 1 - b)
+        part = jnp.stack([lax.dynamic_index_in_dim(part, i, 0, False) for i in turns])
+        shape = part.shape[1:]
+        relay = (2, shape[0] // 2, shape[1])
+        grad_in, got, _ = exchange(
+            to_owners, False, xw, 2, "scatter", (part,), ((3,) + shape, relay), last_major=True
+        )
+        grad_w_out = sum((got[i].astype(F32) for i in range(3)), part[0].astype(F32)).astype(BF)
+    else:
+        (grad_in,) = exchange(to_owners, False, xw, 2, last_major=True)
+        grad_w_out = lax.psum_scatter(part, QUAD, scatter_dimension=0, tiled=True)
+    grad_w_out = grad_w_out.reshape(size_a, vw, width // blocks)
     w_in_all = w_in_all.reshape(blocks, count * xw, width // blocks)
     grad_one = jnp.concatenate([dot(grad_in, w_in_all[i]) for i in range(blocks)], axis=1)
     grad_one = grad_one.reshape(rows_n, sub_len, width)

time: 1160 us -> 1090 us (0.940)
  waiting for transfers between devices: 198 us -> 151 us
  local copies, waits for them, and re-layouts: 72.2 us -> 54.6 us
    ppermute x11 -> x10, waiting for transfers between devices: 78.6 us -> 28.2 us  [swap(): return lax.ppermute(x, axis, [(0, 1), (1, 0)])]
    pallas_call x3, Pallas kernels: 175 us -> 213 us  [exchange(): pl.pallas_call(functools.partial(exchange_kernel, to_blocks, width, last_...]
    pallas_call x4 -> x1, Pallas kernels: 99.4 us -> 68.3 us  [ff_pass(): pl.pallas_call(ff_kernel, out_shape=(keep, keep, keep, jax.ShapeDtypeStru...]
    pallas_call x1, Pallas kernels: 113 us -> 98.2 us  [send_home(): pl.pallas_call(home_kernel, out_shape=[jax.ShapeDtypeStruct(v.shape, v.dt...]
  transfers between devices with their start and end apart: 21 -> 20, of which waited for: 14 -> 12; matrix products, arithmetic and copies ran while one was open for 14% -> 15% of each run, Pallas kernels for 31% -> 34%
where the time goes in v4:
time: 1090 us; the launch traced here: 1080 us
  Pallas kernels  686 us (63%)
  waiting for transfers between devices  151 us (14%)
  matrix products  92.9 us (9%)
  other arithmetic  68.5 us (6%)
  local copies, waits for them, and re-layouts  54.6 us (5%)
  starting transfers between devices  15.6 us (1%)
  between operations  15 us (1%)
    pallas_call x3, Pallas kernels, exchange(): pl.pallas_call(functools.partial(exchange_kernel, to_blocks, width, last_...  213 us
    pallas_call x1, Pallas kernels, start(): pl.pallas_call(functools.partial(start_kernel, parts), out_shape=[jax.Sha...  168 us
    pallas_call x1, Pallas kernels, send_home(): pl.pallas_call(home_kernel, out_shape=[jax.ShapeDtypeStruct(v.shape, v.dt...  98.2 us
    dot_general x17, matrix products, dot(): return lax.dot_general(a, b, dims, preferred_element_type=F32)  81.7 us
    ppermute x6, waiting for transfers between devices, chain_pieces(): out.append(lax.ppermute(x, SEQ + ('ha',), perm))  79.9 us
    pallas_call x1, Pallas kernels, ff_pass(): pl.pallas_call(ff_kernel, out_shape=(keep, keep, keep, jax.ShapeDtypeStru...  68.3 us
    pallas_call x6, Pallas kernels, row_call(): pl.pallas_call(kernel, out_shape=tuple((jax.ShapeDtypeStruct(s, t) for s,...  67.9 us
    pallas_call x1, Pallas kernels, gather_near(): pl.pallas_call(functools.partial(near_kernel, rows), out_shape=[jax.Shape...  56.2 us
  transfers between devices with their start and end apart: 20, of which 12 were waited for; matrix products, arithmetic and copies ran while one was open for 15% of the time, Pallas kernels for 34%

profile of v4, /device:TPU:0, one launch (start us, length us, event | category | flops | bytes accessed | tf_op | source)
XLA Modules:
  0.0 1083.5 jit_solution(5020336577446395758)
XLA Ops:
  22.3 167.9 %shard_map.256 = (bf16[8,3,128,2048]{3,2,1,0:T(8,128)(2,1)}, bf16[384,2048]{1,0:T(8,128)(2,1)}, bf16[8,256,1024]{2,1,0:T(8,128)(2,1)}) custom-call(bf16[3,128,2048]{2,1,0:T(8,128)(2,1)} %fusion.5.src, bf16[384,2048]{1,0:T(8,128)(2,1)} %maximum_maximum_fusion.w_in, bf16[256,1024]{1,0:T(8,128)(2,1)} %constant_dynamic-slice_fusion.9.w_out), custom_call_target="tpu_custom_call" | custom-call | bytes 314572800 | tf_op jit(solution)/shard_map/pallas_call | solution.py:813
  190.3 11.2 %convolution_convert_fusion.4.x_ref = bf16[8,3,128,384]{3,2,1,0:T(8,128)(2,1)} fusion(bf16[8,3,128,2048]{3,2,1,0:T(8,128)(2,1)} %get-tuple-element.60, bf16[384,2048]{1,0:T(8,128)(2,1)} %get-tuple-element.61), kind=kOutput, calls=%fused_computation.43 | convolution fusion | flops 4833017856 | bytes 16515072 | tf_op jit(solution)/shard_map/grtd,cd->grtc/dot_general | solution.py:1100
  201.5 6.2 shard_map.258
  213.9 10.8 %shard_map.257 = (f32[3,1024,256]{2,1,0:T(8,128)}, f32[3,1024,128]{2,1,0:T(8,128)}) custom-call(s32[3,8]{1,0:T(4,128)} %lens.11, s32[1]{0:T(128)} %bitcast.1.meta, bf16[8,3,128,384]{3,2,1,0:T(8,128)(2,1)} %convolution_convert_fusion.4.x_ref, bf16[8,128,128]{2,1,0:T(8,128)(2,1)} %constant.89.clone.align), custom_call_target="tpu_custom_call" | custom-call | flops 6442450944 | bytes 7340032 | tf_op jit(solution)/shard_map/pallas_call | solution.py:304
  228.2 17.9 %collective-permute-done.1.rest_1_ = bf16[3,2,136,256]{3,2,1,0:T(8,128)(2,1)S(1)} collective-permute-done((bf16[3,2,136,256]{3,2,1,0:T(8,128)(2,1)}, bf16[3,2,136,256]{3,2,1,0:T(8,128)(2,1)S(1)}, u32[]{:S(2)}, u32[]{:S(2)}) %collective-permute-start.1) | collective-permute-done | bytes 417824 | tf_op jit(solution)/shard_map/ppermute | solution.py:851
  246.1 16.6 %collective-permute-done.2.rest_2_ = bf16[3,2,136,256]{3,2,1,0:T(8,128)(2,1)S(1)} collective-permute-done((bf16[3,2,136,256]{3,2,1,0:T(8,128)(2,1)}, bf16[3,2,136,256]{3,2,1,0:T(8,128)(2,1)S(1)}, u32[]{:S(2)}, u32[]{:S(2)}) %collective-permute-start.2) | collective-permute-done | bytes 417824 | tf_op jit(solution)/shard_map/ppermute | solution.py:851
  263.5 9.1 shard_map.259
  272.6 75.4 %shard_map.260 = (bf16[384,2048]{1,0:T(8,128)(2,1)}, bf16[4,384,2048]{2,1,0:T(8,128)(2,1)}, bf16[8,256,1024]{2,1,0:T(8,128)(2,1)}) custom-call(bf16[8,384,256]{2,1,0:T(8,128)(2,1)} %bitcast.222, bf16[384,2048]{1,0:T(8,128)(2,1)} %bitcast.221, bf16[8,256,1024]{2,1,0:T(8,128)(2,1)} %get-tuple-element.65.refs_1_), custom_call_target="tpu_custom_call" | custom-call | bytes 393216000 | tf_op jit(solution)/shard_map/pallas_call | solution.py:488
  359.2 30.0 %all-gather.5.cloned.1.call-done = bf16[2112,2048]{1,0:T(8,128)(2,1)} async-done(((bf16[528,2048]{1,0:T(8,128)(2,1)}), bf16[2112,2048]{1,0:T(8,128)(2,1)}) %all-gather.5.cloned.1.call-update) | async-done | bytes 8650768 | tf_op jit(solution)/shard_map/all_gather | solution.py:1097
  389.3 56.2 %shard_map.261 = (bf16[4,384,2048]{2,1,0:T(8,128)(2,1)}, bf16[4,528,2048]{2,1,0:T(8,128)(2,1)}) custom-call(bf16[384,2048]{1,0:T(8,128)(2,1)} %bitcast.224, bf16[4,528,2048]{2,1,0:T(8,128)(2,1)} %bitcast.215), custom_call_target="tpu_custom_call" | custom-call | bytes 157286400 | tf_op jit(solution)/shard_map/pallas_call | solution.py:644
  445.8 68.3 %shard_map.262 = (bf16[2,4,384,704]{3,2,1,0:T(8,128)(2,1)}, bf16[2,4,384,704]{3,2,1,0:T(8,128)(2,1)}, bf16[2,4,384,704]{3,2,1,0:T(8,128)(2,1)}, bf16[4,384,2048]{2,1,0:T(8,128)(2,1)}) custom-call(bf16[4,384,2048]{2,1,0:T(8,128)(2,1)} %get-tuple-element.70.n2, bf16[4,384,2048]{2,1,0:T(8,128)(2,1)} %get-tuple-element.71.cot, bf16[4,528,2048]{2,1,0:T(8,128)(2,1)} %bitcast.216, ...), custom_call_target="tpu_custom_call" | custom-call | flops 44291850240 | bytes 42467328 | tf_op jit(solution)/shard_map/pallas_call | solution.py:936
  518.4 9.6 convolution_convert_fusion.1
  528.1 6.1 convolution_convert_fusion.2
  535.0 6.1 convolution_convert_fusion.3
  544.5 6.6 fusion.47
  551.1 6.6 fusion.46
  557.7 6.9 fusion.45
  564.6 14.0 %shard_map.263 = bf16[1536,2048]{1,0:T(8,128)(2,1)S(1)} custom-call(s32[4]{0:T(128)S(1)} %pad_add_fusion.order, bf16[2,4,384,704]{3,2,1,0:T(8,128)(2,1)S(1)} %bitcast.204, bf16[4,528,2048]{2,1,0:T(8,128)(2,1)} %bitcast.217, bf16[4,528,2048]{2,1,0:T(8,128)(2,1)} %get-tuple-element.72.theirs), custom_call_target="tpu_custom_call" | custom-call | flops 8858370048 | bytes 17301504 | tf_op jit(solution)/shard_map/pallas_call | solution.py:965
  585.4 6.5 add_convert_fusion.1
  605.3 16.4 %collective-permute-done.10 = bf16[192,2048]{1,0:T(8,128)(2,1)} collective-permute-done((bf16[192,2048]{1,0:T(8,128)(2,1)S(1)}, bf16[192,2048]{1,0:T(8,128)(2,1)}, u32[]{:S(2)}, u32[]{:S(2)}) %collective-permute-start.10) | collective-permute-done | bytes 786464 | tf_op jit(solution)/shard_map/ppermute | solution.py:835
  639.8 58.3 %shard_map.264 = bf16[8,384,256]{2,1,0:T(8,128)(2,1)} custom-call(bf16[384,2048]{1,0:T(8,128)(2,1)} %add_convert_fusion.4.src), custom_call_target="tpu_custom_call" | custom-call | bytes 393216000 | tf_op jit(solution)/shard_map/pallas_call | solution.py:488
  698.0 7.4 pad_maximum_fusion
  705.4 12.8 %reduce-scatter.3.cloned.1.call-done = bf16[384,2048]{1,0:T(8,128)(2,1)} async-done(((bf16[1536,2048]{1,0:T(8,128)(2,1)}), bf16[384,2048]{1,0:T(8,128)(2,1)}) %reduce-scatter.3.cloned.1.call-update) | async-done | bytes 1572880 | tf_op jit(solution)/shard_map/reduce_scatter | solution.py:1164
  724.6 7.3 collective-permute-done.15
  748.5 9.5 shard_map.265
  762.1 22.6 %shard_map.266 = (f32[3,1024,128]{2,1,0:T(8,128)}, f32[3,1024,256]{2,1,0:T(8,128)}) custom-call(s32[3,8]{1,0:T(4,128)} %lens.11, s32[1]{0:T(128)} %bitcast.1.meta, bf16[8,3,128,384]{3,2,1,0:T(8,128)(2,1)} %convolution_convert_fusion.4.x_ref, bf16[3,1024,512]{2,1,0:T(8,128)(2,1)} %get-tuple-element.93.gn_ref, ...), custom_call_target="tpu_custom_call" | custom-call | flops 12884901888 | bytes 11436032 | tf_op jit(solution)/shard_map/pallas_call | solution.py:304
  786.4 18.7 %collective-permute-done.12.rest_0_ = bf16[3,2,136,256]{3,2,1,0:T(8,128)(2,1)S(1)} collective-permute-done((bf16[3,2,136,256]{3,2,1,0:T(8,128)(2,1)}, bf16[3,2,136,256]{3,2,1,0:T(8,128)(2,1)S(1)}, u32[]{:S(2)}, u32[]{:S(2)}) %collective-permute-start.12) | collective-permute-done | bytes 417824 | tf_op jit(solution)/shard_map/ppermute | solution.py:851
  805.1 23.2 %collective-permute-done.14.rest_2_ = bf16[3,2,136,256]{3,2,1,0:T(8,128)(2,1)S(1)} collective-permute-done((bf16[3,2,136,256]{3,2,1,0:T(8,128)(2,1)}, bf16[3,2,136,256]{3,2,1,0:T(8,128)(2,1)S(1)}, u32[]{:S(2)}, u32[]{:S(2)}) %collective-permute-start.14) | collective-permute-done | bytes 417824 | tf_op jit(solution)/shard_map/ppermute | solution.py:851
  829.1 9.6 shard_map.267
  838.7 79.7 %shard_map.268 = (bf16[384,3072]{1,0:T(8,128)(2,1)}, bf16[3,1024,512]{2,1,0:T(8,128)(2,1)}, bf16[2,512,512]{2,1,0:T(8,128)(2,1)}) custom-call(bf16[8,384,384]{2,1,0:T(8,128)(2,1)} %bitcast.214, bf16[4,1024,512]{2,1,0:T(8,128)(2,1)} %pad_maximum_fusion.2.refs_0_), custom_call_target="tpu_custom_call" | custom-call | bytes 589824000 | tf_op jit(solution)/shard_map/pallas_call | solution.py:488
  930.9 9.7 bitcast_convert_fusion
  960.7 98.2 %shard_map.269 = (f32[32,8,128]{2,1,0:T(8,128)}, bf16[4,384,512]{2,1,0:T(8,128)(2,1)}, bf16[4,528,512]{2,1,0:T(8,128)(2,1)}, bf16[4,256,512]{2,1,0:T(8,128)(2,1)}) custom-call(f32[32,8,128]{2,1,0:T(8,128)} %pad.4.refs_0_, bf16[4,384,512]{2,1,0:T(8,128)(2,1)} %bitcast.226, bf16[4,528,512]{2,1,0:T(8,128)(2,1)} %bitcast.218, bf16[4,256,512]{2,1,0:T(8,128)(2,1)} %bitcast.238), custom_call_target="tpu_custom_call" | custom-call | bytes 100000000 | tf_op jit(solution)/shard_map/pallas_call | solution.py:591
  (238 shorter events, 162.9 us)
Async XLA Ops:
  7.2 382.1 %all-gather.5.cloned.1.call-start = ((), (), s32[]{:S(2)}) async-start(), calls=%async_computation.4 | async-start | bytes 10813440 | tf_op jit(solution)/shard_map/all_gather | solution.py:1097
  190.2 412.9 %all-gather.7.cloned.1.call-start = ((), (), s32[]{:S(2)}) async-start(), calls=%async_computation.5 | async-start | bytes 12976128 | tf_op jit(solution)/shard_map/all_gather | solution.py:1150
  207.7 20.5 %collective-permute-start = (bf16[3,2,136,256]{3,2,1,0:T(8,128)(2,1)}, bf16[3,2,136,256]{3,2,1,0:T(8,128)(2,1)S(1)}, u32[]{:S(2)}, u32[]{:S(2)}) collective-permute-start(bf16[3,2,136,256]{3,2,1,0:T(8,128)(2,1)} %shard_map.258), channel_id=1, source_target_pairs={{0,4},{8,12},{16,20},{24,28},{4,18},{12,26},{20,2},{28,10},{18,22}... | collective-permute-start | bytes 1253384 | tf_op jit(solution)/shard_map/ppermute | solution.py:851
  209.0 37.1 %collective-permute-start.1 = (bf16[3,2,136,256]{3,2,1,0:T(8,128)(2,1)}, bf16[3,2,136,256]{3,2,1,0:T(8,128)(2,1)S(1)}, u32[]{:S(2)}, u32[]{:S(2)}) collective-permute-start(bf16[3,2,136,256]{3,2,1,0:T(8,128)(2,1)} %shard_map.258), channel_id=1, source_target_pairs={{0,18},{8,26},{16,2},{24,10},{4,22},{12,30},{20,6},{28,14},{1,19},... | collective-permute-start | bytes 1253384 | tf_op jit(solution)/shard_map/ppermute | solution.py:851
  210.3 52.4 %collective-permute-start.2 = (bf16[3,2,136,256]{3,2,1,0:T(8,128)(2,1)}, bf16[3,2,136,256]{3,2,1,0:T(8,128)(2,1)S(1)}, u32[]{:S(2)}, u32[]{:S(2)}) collective-permute-start(bf16[3,2,136,256]{3,2,1,0:T(8,128)(2,1)} %shard_map.258), channel_id=1, source_target_pairs={{0,22},{8,30},{16,6},{24,14},{1,23},{9,31},{17,7},{25,15}} | collective-permute-start | bytes 1253384 | tf_op jit(solution)/shard_map/ppermute | solution.py:851
  228.2 34.5 %copy-start.38 = (bf16[3,2,136,256]{3,2,1,0:T(8,128)(2,1)}, bf16[3,2,136,256]{3,2,1,0:T(8,128)(2,1)S(1)}, u32[]{:S(2)}) copy-start(bf16[3,2,136,256]{3,2,1,0:T(8,128)(2,1)S(1)} %collective-permute-done.rest_0_) | copy-start | bytes 1253380
  246.1 16.6 %copy-start.39 = (bf16[3,2,136,256]{3,2,1,0:T(8,128)(2,1)}, bf16[3,2,136,256]{3,2,1,0:T(8,128)(2,1)S(1)}, u32[]{:S(2)}) copy-start(bf16[3,2,136,256]{3,2,1,0:T(8,128)(2,1)S(1)} %collective-permute-done.1.rest_1_) | copy-start | bytes 1253380
  445.5 272.7 %reduce-scatter.3.cloned.1.call-start = ((), (), s32[]{:S(2)}) async-start(), calls=%async_computation.2 | async-start | bytes 7864320 | tf_op jit(solution)/shard_map/reduce_scatter | solution.py:1164
  514.1 14.0 %slice-start.15 = ((s8[6291456]{0:T(1024)(128)(4,1)}), s8[4194304]{0:T(1024)(128)(4,1)S(1)}, s32[]{:S(2)}) async-start(s8[6291456]{0:T(1024)(128)(4,1)} %bitcast.260), calls=%async_computation.21 | async-start | bytes 8388608
  518.4 9.7 slice-start.16
  528.0 53.2 %collective-permute-start.7 = (bf16[704,2048]{1,0:T(8,128)(2,1)}, bf16[704,2048]{1,0:T(8,128)(2,1)}, u32[]{:S(2)}, u32[]{:S(2)}) collective-permute-start(bf16[704,2048]{1,0:T(8,128)(2,1)} %convolution_convert_fusion.1), channel_id=1, source_target_pairs={{0,8},{8,0},{1,9},{9,1},{2,10},{10,2},{3,11},{11,3},{4,12},{12,4},... | collective-permute-start | bytes 8650760 | tf_op jit(solution)/shard_map/ppermute | solution.py:835
  534.2 47.1 %collective-permute-start.6 = (bf16[704,2048]{1,0:T(8,128)(2,1)}, bf16[704,2048]{1,0:T(8,128)(2,1)}, u32[]{:S(2)}, u32[]{:S(2)}) collective-permute-start(bf16[704,2048]{1,0:T(8,128)(2,1)} %convolution_convert_fusion.2), channel_id=1, source_target_pairs={{0,8},{8,0},{1,9},{9,1},{2,10},{10,2},{3,11},{11,3},{4,12},{12,4},... | collective-permute-start | bytes 8650760 | tf_op jit(solution)/shard_map/ppermute | solution.py:835
  534.7 9.8 slice-start.13
  541.1 40.2 %collective-permute-start.5 = (bf16[704,2048]{1,0:T(8,128)(2,1)}, bf16[704,2048]{1,0:T(8,128)(2,1)}, u32[]{:S(2)}, u32[]{:S(2)}) collective-permute-start(bf16[704,2048]{1,0:T(8,128)(2,1)} %convolution_convert_fusion.3), channel_id=1, source_target_pairs={{0,8},{8,0},{1,9},{9,1},{2,10},{10,2},{3,11},{11,3},{4,12},{12,4},... | collective-permute-start | bytes 8650760 | tf_op jit(solution)/shard_map/ppermute | solution.py:835
  542.5 38.7 %collective-permute-start.3 = (bf16[192,2048]{1,0:T(8,128)(2,1)}, bf16[192,2048]{1,0:T(8,128)(2,1)S(1)}, u32[]{:S(2)}, u32[]{:S(2)}) collective-permute-start(bf16[192,2048]{1,0:T(8,128)(2,1)} %get-tuple-element.159), channel_id=1, source_target_pairs={{0,1},{1,0},{2,3},{3,2},{4,5},{5,4},{6,7},{7,6},{8,9},{9,8},{10,11... | collective-permute-start | bytes 2359304 | tf_op jit(solution)/shard_map/ppermute | solution.py:835
  543.2 38.1 %collective-permute-start.4 = (bf16[192,2048]{1,0:T(8,128)(2,1)}, bf16[192,2048]{1,0:T(8,128)(2,1)S(1)}, u32[]{:S(2)}, u32[]{:S(2)}) collective-permute-start(bf16[192,2048]{1,0:T(8,128)(2,1)} %get-tuple-element.158), channel_id=1, source_target_pairs={{0,16},{16,0},{1,17},{17,1},{2,18},{18,2},{3,19},{19,3},{4,20},{20... | collective-permute-start | bytes 2359304 | tf_op jit(solution)/shard_map/ppermute | solution.py:835
  551.1 13.5 %slice-start = ((s8[4718592]{0:T(1024)(128)(4,1)}), s8[4194304]{0:T(1024)(128)(4,1)S(1)}, s32[]{:S(2)}) async-start(s8[4718592]{0:T(1024)(128)(4,1)} %bitcast.203), calls=%async_computation.6 | async-start | bytes 8388608
  583.2 19.4 %collective-permute-start.8 = (bf16[192,2048]{1,0:T(8,128)(2,1)S(1)}, bf16[192,2048]{1,0:T(8,128)(2,1)S(1)}, u32[]{:S(2)}, u32[]{:S(2)}) collective-permute-start(bf16[192,2048]{1,0:T(8,128)(2,1)S(1)} %get-tuple-element.161), channel_id=1, source_target_pairs={{0,16},{16,0},{1,17},{17,1},{2,18},{18,2},{3,19},{19,3},{4,20},{20... | collective-permute-start | bytes 2359304 | tf_op jit(solution)/shard_map/ppermute | solution.py:835
  584.0 19.1 %collective-permute-start.9 = (bf16[192,2048]{1,0:T(8,128)(2,1)S(1)}, bf16[192,2048]{1,0:T(8,128)(2,1)S(1)}, u32[]{:S(2)}, u32[]{:S(2)}) collective-permute-start(bf16[192,2048]{1,0:T(8,128)(2,1)S(1)} %get-tuple-element.160), channel_id=1, source_target_pairs={{0,1},{1,0},{2,3},{3,2},{4,5},{5,4},{6,7},{7,6},{8,9},{9,8},{10,11... | collective-permute-start | bytes 2359304 | tf_op jit(solution)/shard_map/ppermute | solution.py:835
  585.4 11.1 %slice-start.9 = ((s8[5767168]{0:T(1024)(128)(4,1)}), s8[4194304]{0:T(1024)(128)(4,1)S(1)}, s32[]{:S(2)}) async-start(s8[5767168]{0:T(1024)(128)(4,1)} %bitcast.234), calls=%async_computation.15 | async-start | bytes 8388608
  603.1 351.1 %reduce-scatter.5.cloned.1.call-start = ((), (), s32[]{:S(2)}) async-start(), calls=%async_computation.3 | async-start | bytes 10813440 | tf_op jit(solution)/shard_map/reduce_scatter | solution.py:1167
  603.2 18.5 %collective-permute-start.10 = (bf16[192,2048]{1,0:T(8,128)(2,1)S(1)}, bf16[192,2048]{1,0:T(8,128)(2,1)}, u32[]{:S(2)}, u32[]{:S(2)}) collective-permute-start(bf16[192,2048]{1,0:T(8,128)(2,1)S(1)} %get-tuple-element.156), channel_id=1, source_target_pairs={{0,1},{1,0},{2,3},{3,2},{4,5},{5,4},{6,7},{7,6},{8,9},{9,8},{10,11... | collective-permute-start | bytes 2359304 | tf_op jit(solution)/shard_map/ppermute | solution.py:835
  604.6 19.4 %collective-permute-start.11 = (bf16[192,2048]{1,0:T(8,128)(2,1)S(1)}, bf16[192,2048]{1,0:T(8,128)(2,1)}, u32[]{:S(2)}, u32[]{:S(2)}) collective-permute-start(bf16[192,2048]{1,0:T(8,128)(2,1)S(1)} %get-tuple-element.157), channel_id=1, source_target_pairs={{0,16},{16,0},{1,17},{17,1},{2,18},{18,2},{3,19},{19,3},{4,20},{20... | collective-permute-start | bytes 2359304 | tf_op jit(solution)/shard_map/ppermute | solution.py:835
  718.4 13.5 %copy-start.37 = (bf16[384,2048]{1,0:T(8,128)(2,1)S(1)}, bf16[384,2048]{1,0:T(8,128)(2,1)}, u32[]{:S(2)}) copy-start(bf16[384,2048]{1,0:T(8,128)(2,1)} %get-tuple-element.66) | copy-start | bytes 4718596
  724.4 7.5 collective-permute-start.15
  758.0 47.1 %collective-permute-start.12 = (bf16[3,2,136,256]{3,2,1,0:T(8,128)(2,1)}, bf16[3,2,136,256]{3,2,1,0:T(8,128)(2,1)S(1)}, u32[]{:S(2)}, u32[]{:S(2)}) collective-permute-start(bf16[3,2,136,256]{3,2,1,0:T(8,128)(2,1)} %get-tuple-element.97), channel_id=1, source_target_pairs={{4,0},{12,8},{20,16},{28,24},{18,4},{26,12},{2,20},{10,28},{22,18}... | collective-permute-start | bytes 1253384 | tf_op jit(solution)/shard_map/ppermute | solution.py:851
  759.3 45.9 %collective-permute-start.13 = (bf16[3,2,136,256]{3,2,1,0:T(8,128)(2,1)}, bf16[3,2,136,256]{3,2,1,0:T(8,128)(2,1)S(1)}, u32[]{:S(2)}, u32[]{:S(2)}) collective-permute-start(bf16[3,2,136,256]{3,2,1,0:T(8,128)(2,1)} %get-tuple-element.97), channel_id=1, source_target_pairs={{18,0},{26,8},{2,16},{10,24},{22,4},{30,12},{6,20},{14,28},{19,1},... | collective-permute-start | bytes 1253384 | tf_op jit(solution)/shard_map/ppermute | solution.py:851
  760.6 67.8 %collective-permute-start.14 = (bf16[3,2,136,256]{3,2,1,0:T(8,128)(2,1)}, bf16[3,2,136,256]{3,2,1,0:T(8,128)(2,1)S(1)}, u32[]{:S(2)}, u32[]{:S(2)}) collective-permute-start(bf16[3,2,136,256]{3,2,1,0:T(8,128)(2,1)} %get-tuple-element.97), channel_id=1, source_target_pairs={{22,0},{30,8},{6,16},{14,24},{23,1},{31,9},{7,17},{15,25}} | collective-permute-start | bytes 1253384 | tf_op jit(solution)/shard_map/ppermute | solution.py:851
  762.1 22.6 %copy-start.5 = (f32[3,128,2048]{2,1,0:T(8,128)S(1)}, f32[3,128,2048]{2,1,0:T(8,128)}, u32[]{:S(2)}) copy-start(f32[3,128,2048]{2,1,0:T(8,128)} %copy-done.3) | copy-start | bytes 9437188
  762.1 22.6 %copy-start.21 = (bf16[384,2048]{1,0:T(8,128)(2,1)S(1)}, bf16[384,2048]{1,0:T(8,128)(2,1)}, u32[]{:S(2)}) copy-start(bf16[384,2048]{1,0:T(8,128)(2,1)} %reduce-scatter.3.cloned.1.call-done) | copy-start | bytes 4718596
  805.1 23.2 %copy-start.23 = (bf16[3,2,136,256]{3,2,1,0:T(8,128)(2,1)}, bf16[3,2,136,256]{3,2,1,0:T(8,128)(2,1)S(1)}, u32[]{:S(2)}) copy-start(bf16[3,2,136,256]{3,2,1,0:T(8,128)(2,1)S(1)} %collective-permute-done.12.rest_0_) | copy-start | bytes 1253380
  805.1 23.2 %copy-start.24 = (bf16[3,2,136,256]{3,2,1,0:T(8,128)(2,1)}, bf16[3,2,136,256]{3,2,1,0:T(8,128)(2,1)S(1)}, u32[]{:S(2)}) copy-start(bf16[3,2,136,256]{3,2,1,0:T(8,128)(2,1)S(1)} %collective-permute-done.13.rest_1_) | copy-start | bytes 1253380
  (46 other events, 192.0 us)
Sparse Core Ops, SparseCore 0:
  190.4 198.8 all-gather.4
  445.6 105.5 all-gather.6
  603.3 114.9 reduce-scatter.2
  720.4 225.5 reduce-scatter.4

commit v5 on v4

--- a/solution.py
+++ b/solution.py
@@ -656,7 +656,7 @@
     return near, theirs
 
 
-def start_kernel(parts, src, w_in, w_out, dst, w_in_home, w_out_all, ssem, rsem, lsem, wsem, vsem):
+def start_kernel(parts, live, src, w_in, w_out, dst, w_in_home, w_out_all, ssem, rsem, lsem, wsem, vsem):
     sy, sc, a, b = here()
     block, head = own_place()
     size = lax.axis_size("ha")
@@ -679,6 +679,9 @@
     pl.when(has_down)(lambda: signal(to_down))
     own_w = pltpu.make_async_copy(w_out, w_out_all.at[a * 2 + b], lsem.at[parts])
     own_w.start()
+    pad = pl.ds(live, w_in.shape[0] - live)
+    own_pad = pltpu.make_async_copy(w_in.at[pad], w_in_home.at[pad], lsem.at[parts + 2])
+    own_pad.start()
     pl.semaphore_wait(
         bar, 3 + apart.astype(jnp.int32) + has_up.astype(jnp.int32) + has_down.astype(jnp.int32)
     )
@@ -701,8 +704,8 @@
 
     def w_home():
         return pltpu.make_async_remote_copy(
-            src_ref=w_in,
-            dst_ref=w_in_home,
+            src_ref=w_in.at[pl.ds(0, live)],
+            dst_ref=w_in_home.at[pl.ds(0, live)],
             send_sem=wsem.at[0],
             recv_sem=wsem.at[1],
             device_id=target,
@@ -710,7 +713,7 @@
         )
 
     def w_stay():
-        return pltpu.make_async_copy(w_in, w_in_home, lsem.at[parts + 1])
+        return pltpu.make_async_copy(w_in.at[pl.ds(0, live)], w_in_home.at[pl.ds(0, live)], lsem.at[parts + 1])
 
     for r in range(parts):
         pl.when(apart)(lambda: home(r).start())
@@ -790,6 +793,7 @@
         w_step(k)
     pl.when(apart)(lambda: w_home().wait_recv())
     pl.when(same)(lambda: w_stay().wait())
+    own_pad.wait()
     for k in range(size):
         ref = w_out_all.at[k * 2 + 1 - b]
         remote(ref, ref, vsem.at[0], vsem.at[1], 2 * size + k, to_x).wait_recv()
@@ -803,7 +807,7 @@
     pl.when(apart)(lambda: w_home().wait_send())
 
 
-def start(x, w_in, w_out, collective):
+def start(x, w_in, live, w_out, collective):
     if not square():
         size = lax.axis_size("ha")
         perm = [(s * size + z, z * size + s) for s in range(size) for z in range(size)]
@@ -811,7 +815,7 @@
         return lax.all_gather(x, ("sy", "sc", "hb"), axis=0), w_in, lax.all_gather(w_out, HEAD, axis=0)
     parts = x.shape[0]
     return pl.pallas_call(
-        functools.partial(start_kernel, parts),
+        functools.partial(start_kernel, parts, live),
         out_shape=[
             jax.ShapeDtypeStruct((8,) + x.shape, x.dtype),
             jax.ShapeDtypeStruct(w_in.shape, w_in.dtype),
@@ -822,7 +826,7 @@
         scratch_shapes=[
             pltpu.SemaphoreType.DMA((9 * parts,)),
             pltpu.SemaphoreType.DMA((9 * parts,)),
-            pltpu.SemaphoreType.DMA((parts + 2,)),
+            pltpu.SemaphoreType.DMA((parts + 3,)),
             pltpu.SemaphoreType.DMA((2,)),
             pltpu.SemaphoreType.DMA((2, 12)),
         ],
@@ -1092,7 +1096,7 @@
     windows = [unit_window(w, blocks) for w in (gate_weight.T, up_weight.T, down_weight)]
     w_in_piece = my_columns(w_in, False)
     to_fetch = jnp.concatenate(windows, axis=0)
-    normed_full, w_in_home, w_out_piece = start((normed_one * attn_gain).astype(BF), w_in, my_columns(w_out, True), 3)
+    normed_full, w_in_home, w_out_piece = start((normed_one * attn_gain).astype(BF), w_in, vw + 2 * nh * FEAT, my_columns(w_out, True), 3)
     to_fetch, normed_full = tie(to_fetch, normed_full)
     fetched = lax.all_gather(to_fetch, "ha", axis=0)
     window = windows[0].shape[0]
@@ -1162,8 +1166,9 @@
     grad_att = by_halves_back(flat_branch, *w_out_halves).astype(BF)
     branch, w_in_all = tie(branch, w_in_all)
     branch = lax.psum_scatter(branch, QUAD, scatter_dimension=0, tiled=True)
+    grad_att, ff_grads = tie(grad_att, jnp.concatenate(ff_grads, axis=1))
     (grad_att,) = exchange(grad_att, True, vw, 1)
-    ff_grads, branch, grad_att = tie(jnp.concatenate(ff_grads, axis=1), branch, grad_att)
+    ff_grads, branch, grad_att = tie(ff_grads, branch, grad_att)
     ff_grads = lax.psum_scatter(ff_grads, "ha", scatter_dimension=0, tiled=True)
     grad_att = grad_att.reshape(count, rows_n, sub_len, vw)
     output = (middle + branch.astype(F32).reshape(rows_n, sub_len, width)).astype(BF)
@@ -1223,7 +1228,9 @@
 
     flat_tokens = count * tokens
     grad_w_in = dot(gqkv.reshape(flat_tokens, xw), normed_full.reshape(flat_tokens, width), TN)
-    grad_w_in = jnp.transpose(grad_w_in.astype(BF).reshape(xw, blocks, width // blocks), (1, 0, 2))
+    live = vw + 2 * nh * FEAT
+    grad_w_in = grad_w_in.astype(BF)[:live].reshape(live, blocks, width // blocks)
+    grad_w_in = jnp.transpose(grad_w_in, (1, 0, 2))
     vectors = jnp.stack([gain_one_part, bias_part, gain_two_part])
     vectors, grad_w_in, ff_grads, grad_w_out = send_home(vectors, grad_w_in, ff_grads, grad_w_out, 5)
     ff_grads = ff_grads.astype(F32).reshape(blocks, 3, -1, width // blocks)

time: 1090 us -> 1070 us (0.982)
  Pallas kernels: 686 us -> 672 us
    unnamed x118 -> x128, local copies, waits for them, and re-layouts: 22 us -> 24.1 us
  transfers between devices with their start and end apart: 20 -> 20, of which waited for: 12 -> 13; matrix products, arithmetic and copies ran while one was open for 15% -> 14% of each run, Pallas kernels for 34% -> 34%
where the time goes in v5:
time: 1070 us; the launch traced here: 1060 us
  Pallas kernels  672 us (63%)
  waiting for transfers between devices  155 us (14%)
  matrix products  91.7 us (9%)
  other arithmetic  61 us (6%)
  local copies, waits for them, and re-layouts  52.6 us (5%)
  starting transfers between devices  15.7 us (1%)
  between operations  14.8 us (1%)
    pallas_call x3, Pallas kernels, exchange(): pl.pallas_call(functools.partial(exchange_kernel, to_blocks, width, last_...  212 us
    pallas_call x1, Pallas kernels, start(): pl.pallas_call(functools.partial(start_kernel, parts, live), out_shape=[j...  159 us
    pallas_call x1, Pallas kernels, send_home(): pl.pallas_call(home_kernel, out_shape=[jax.ShapeDtypeStruct(v.shape, v.dt...  93.8 us
    dot_general x17, matrix products, dot(): return lax.dot_general(a, b, dims, preferred_element_type=F32)  80.5 us
    ppermute x6, waiting for transfers between devices, chain_pieces(): out.append(lax.ppermute(x, SEQ + ('ha',), perm))  80.3 us
    pallas_call x1, Pallas kernels, ff_pass(): pl.pallas_call(ff_kernel, out_shape=(keep, keep, keep, jax.ShapeDtypeStru...  68.3 us
    pallas_call x6, Pallas kernels, row_call(): pl.pallas_call(kernel, out_shape=tuple((jax.ShapeDtypeStruct(s, t) for s,...  68 us
    pallas_call x1, Pallas kernels, gather_near(): pl.pallas_call(functools.partial(near_kernel, rows), out_shape=[jax.Shape...  56.2 us
  transfers between devices with their start and end apart: 20, of which 13 were waited for; matrix products, arithmetic and copies ran while one was open for 14% of the time, Pallas kernels for 34%

profile of v5, /device:TPU:0, one launch (start us, length us, event | category | flops | bytes accessed | tf_op | source)
XLA Modules:
  0.0 1063.2 jit_solution(12618385553023473176)
XLA Ops:
  22.3 159.5 %shard_map.256 = (bf16[8,3,128,2048]{3,2,1,0:T(8,128)(2,1)}, bf16[384,2048]{1,0:T(8,128)(2,1)}, bf16[8,256,1024]{2,1,0:T(8,128)(2,1)}) custom-call(bf16[3,128,2048]{2,1,0:T(8,128)(2,1)} %fusion.5.src, bf16[384,2048]{1,0:T(8,128)(2,1)} %maximum_maximum_fusion.w_in, bf16[256,1024]{1,0:T(8,128)(2,1)} %constant_dynamic-slice_fusion.9.w_out), custom_call_target="tpu_custom_call" | custom-call | bytes 314572800 | tf_op jit(solution)/shard_map/pallas_call | solution.py:817
  181.9 11.2 %convolution_convert_fusion.4.x_ref = bf16[8,3,128,384]{3,2,1,0:T(8,128)(2,1)} fusion(bf16[8,3,128,2048]{3,2,1,0:T(8,128)(2,1)} %get-tuple-element.62, bf16[384,2048]{1,0:T(8,128)(2,1)} %get-tuple-element.63), kind=kOutput, calls=%fused_computation.44 | convolution fusion | flops 4833017856 | bytes 16515072 | tf_op jit(solution)/shard_map/grtd,cd->grtc/dot_general | solution.py:1104
  193.1 6.2 shard_map.258
  205.5 10.8 %shard_map.257 = (f32[3,1024,256]{2,1,0:T(8,128)}, f32[3,1024,128]{2,1,0:T(8,128)}) custom-call(s32[3,8]{1,0:T(4,128)} %lens.11, s32[1]{0:T(128)} %bitcast.1.meta, bf16[8,3,128,384]{3,2,1,0:T(8,128)(2,1)} %convolution_convert_fusion.4.x_ref, bf16[8,128,128]{2,1,0:T(8,128)(2,1)} %constant.89.clone.align), custom_call_target="tpu_custom_call" | custom-call | flops 6442450944 | bytes 7340032 | tf_op jit(solution)/shard_map/pallas_call | solution.py:304
  219.8 17.9 %collective-permute-done.1.rest_1_ = bf16[3,2,136,256]{3,2,1,0:T(8,128)(2,1)S(1)} collective-permute-done((bf16[3,2,136,256]{3,2,1,0:T(8,128)(2,1)}, bf16[3,2,136,256]{3,2,1,0:T(8,128)(2,1)S(1)}, u32[]{:S(2)}, u32[]{:S(2)}) %collective-permute-start.1) | collective-permute-done | bytes 417824 | tf_op jit(solution)/shard_map/ppermute | solution.py:855
  237.7 16.6 %collective-permute-done.2.rest_2_ = bf16[3,2,136,256]{3,2,1,0:T(8,128)(2,1)S(1)} collective-permute-done((bf16[3,2,136,256]{3,2,1,0:T(8,128)(2,1)}, bf16[3,2,136,256]{3,2,1,0:T(8,128)(2,1)S(1)}, u32[]{:S(2)}, u32[]{:S(2)}) %collective-permute-start.2) | collective-permute-done | bytes 417824 | tf_op jit(solution)/shard_map/ppermute | solution.py:855
  255.1 9.2 shard_map.259
  264.2 75.4 %shard_map.260 = (bf16[384,2048]{1,0:T(8,128)(2,1)}, bf16[4,384,2048]{2,1,0:T(8,128)(2,1)}, bf16[8,256,1024]{2,1,0:T(8,128)(2,1)}) custom-call(bf16[8,384,256]{2,1,0:T(8,128)(2,1)} %bitcast.227, bf16[384,2048]{1,0:T(8,128)(2,1)} %bitcast.226, bf16[8,256,1024]{2,1,0:T(8,128)(2,1)} %get-tuple-element.67.refs_1_), custom_call_target="tpu_custom_call" | custom-call | bytes 393216000 | tf_op jit(solution)/shard_map/pallas_call | solution.py:488
  350.8 30.3 %all-gather.5.cloned.1.call-done = bf16[2112,2048]{1,0:T(8,128)(2,1)} async-done(((bf16[528,2048]{1,0:T(8,128)(2,1)}), bf16[2112,2048]{1,0:T(8,128)(2,1)}) %all-gather.5.cloned.1.call-update) | async-done | bytes 8650768 | tf_op jit(solution)/shard_map/all_gather | solution.py:1101
  381.1 56.2 %shard_map.261 = (bf16[4,384,2048]{2,1,0:T(8,128)(2,1)}, bf16[4,528,2048]{2,1,0:T(8,128)(2,1)}) custom-call(bf16[384,2048]{1,0:T(8,128)(2,1)} %bitcast.229, bf16[4,528,2048]{2,1,0:T(8,128)(2,1)} %bitcast.220), custom_call_target="tpu_custom_call" | custom-call | bytes 157286400 | tf_op jit(solution)/shard_map/pallas_call | solution.py:644
  437.6 68.3 %shard_map.262 = (bf16[2,4,384,704]{3,2,1,0:T(8,128)(2,1)}, bf16[2,4,384,704]{3,2,1,0:T(8,128)(2,1)}, bf16[2,4,384,704]{3,2,1,0:T(8,128)(2,1)}, bf16[4,384,2048]{2,1,0:T(8,128)(2,1)}) custom-call(bf16[4,384,2048]{2,1,0:T(8,128)(2,1)} %get-tuple-element.72.n2, bf16[4,384,2048]{2,1,0:T(8,128)(2,1)} %get-tuple-element.73.cot, bf16[4,528,2048]{2,1,0:T(8,128)(2,1)} %bitcast.221, ...), custom_call_target="tpu_custom_call" | custom-call | flops 44291850240 | bytes 42467328 | tf_op jit(solution)/shard_map/pallas_call | solution.py:940
  510.3 9.9 convolution_convert_fusion.1
  520.2 6.1 convolution_convert_fusion.2
  527.2 6.1 convolution_convert_fusion.3
  536.7 6.5 fusion.47
  543.2 6.4 fusion.46
  549.6 6.6 fusion.45
  556.2 14.0 %shard_map.263 = bf16[1536,2048]{1,0:T(8,128)(2,1)S(1)} custom-call(s32[4]{0:T(128)S(1)} %pad_add_fusion.order, bf16[2,4,384,704]{3,2,1,0:T(8,128)(2,1)S(1)} %bitcast.209, bf16[4,528,2048]{2,1,0:T(8,128)(2,1)} %bitcast.222, bf16[4,528,2048]{2,1,0:T(8,128)(2,1)} %get-tuple-element.74.theirs), custom_call_target="tpu_custom_call" | custom-call | flops 8858370048 | bytes 17301504 | tf_op jit(solution)/shard_map/pallas_call | solution.py:969
  577.0 6.5 add_convert_fusion.1
  596.9 16.3 %collective-permute-done.11 = bf16[192,2048]{1,0:T(8,128)(2,1)} collective-permute-done((bf16[192,2048]{1,0:T(8,128)(2,1)S(1)}, bf16[192,2048]{1,0:T(8,128)(2,1)}, u32[]{:S(2)}, u32[]{:S(2)}) %collective-permute-start.11) | collective-permute-done | bytes 786464 | tf_op jit(solution)/shard_map/ppermute | solution.py:839
  636.3 59.1 %shard_map.264 = bf16[8,384,256]{2,1,0:T(8,128)(2,1)} custom-call(bf16[384,2048]{1,0:T(8,128)(2,1)} %add_convert_fusion.4.src), custom_call_target="tpu_custom_call" | custom-call | bytes 393216000 | tf_op jit(solution)/shard_map/pallas_call | solution.py:488
  695.5 16.4 %reduce-scatter.3.cloned.1.call-done = bf16[384,2048]{1,0:T(8,128)(2,1)} async-done(((bf16[1536,2048]{1,0:T(8,128)(2,1)}), bf16[384,2048]{1,0:T(8,128)(2,1)}) %reduce-scatter.3.cloned.1.call-update) | async-done | bytes 1572880 | tf_op jit(solution)/shard_map/reduce_scatter | solution.py:1168
  712.1 5.9 convolution_convert_fusion
  718.1 7.3 collective-permute-done.15
  741.8 9.5 shard_map.265
  755.6 22.6 %shard_map.266 = (f32[3,1024,128]{2,1,0:T(8,128)}, f32[3,1024,256]{2,1,0:T(8,128)}) custom-call(s32[3,8]{1,0:T(4,128)} %lens.11, s32[1]{0:T(128)} %bitcast.1.meta, bf16[8,3,128,384]{3,2,1,0:T(8,128)(2,1)} %convolution_convert_fusion.4.x_ref, bf16[3,1024,512]{2,1,0:T(8,128)(2,1)} %get-tuple-element.97.gn_ref, ...), custom_call_target="tpu_custom_call" | custom-call | flops 12884901888 | bytes 11436032 | tf_op jit(solution)/shard_map/pallas_call | solution.py:304
  779.9 16.5 %collective-permute-done.12.rest_0_ = bf16[3,2,136,256]{3,2,1,0:T(8,128)(2,1)S(1)} collective-permute-done((bf16[3,2,136,256]{3,2,1,0:T(8,128)(2,1)}, bf16[3,2,136,256]{3,2,1,0:T(8,128)(2,1)S(1)}, u32[]{:S(2)}, u32[]{:S(2)}) %collective-permute-start.12) | collective-permute-done | bytes 417824 | tf_op jit(solution)/shard_map/ppermute | solution.py:855
  799.2 23.0 %collective-permute-done.14.rest_2_ = bf16[3,2,136,256]{3,2,1,0:T(8,128)(2,1)S(1)} collective-permute-done((bf16[3,2,136,256]{3,2,1,0:T(8,128)(2,1)}, bf16[3,2,136,256]{3,2,1,0:T(8,128)(2,1)S(1)}, u32[]{:S(2)}, u32[]{:S(2)}) %collective-permute-start.14) | collective-permute-done | bytes 417824 | tf_op jit(solution)/shard_map/ppermute | solution.py:855
  823.0 9.7 shard_map.267
  832.7 77.8 %shard_map.268 = (bf16[384,3072]{1,0:T(8,128)(2,1)}, bf16[3,1024,512]{2,1,0:T(8,128)(2,1)}, bf16[2,512,512]{2,1,0:T(8,128)(2,1)}) custom-call(bf16[8,384,384]{2,1,0:T(8,128)(2,1)} %bitcast.219, bf16[4,1024,512]{2,1,0:T(8,128)(2,1)} %pad_maximum_fusion.2.refs_0_), custom_call_target="tpu_custom_call" | custom-call | bytes 589824000 | tf_op jit(solution)/shard_map/pallas_call | solution.py:488
  923.1 8.9 convolution_bitcast_fusion
  945.4 93.8 %shard_map.269 = (f32[32,8,128]{2,1,0:T(8,128)}, bf16[4,320,512]{2,1,0:T(8,128)(2,1)}, bf16[4,528,512]{2,1,0:T(8,128)(2,1)}, bf16[4,256,512]{2,1,0:T(8,128)(2,1)}) custom-call(f32[32,8,128]{2,1,0:T(8,128)} %pad.4.refs_0_, bf16[4,320,512]{2,1,0:T(8,128)(2,1)} %bitcast.240, bf16[4,528,512]{2,1,0:T(8,128)(2,1)} %bitcast.223, bf16[4,256,512]{2,1,0:T(8,128)(2,1)} %bitcast.246), custom_call_target="tpu_custom_call" | custom-call | bytes 100000000 | tf_op jit(solution)/shard_map/pallas_call | solution.py:591
  (248 shorter events, 157.8 us)
Async XLA Ops:
  7.2 373.9 %all-gather.5.cloned.1.call-start = ((), (), s32[]{:S(2)}) async-start(), calls=%async_computation.4 | async-start | bytes 10813440 | tf_op jit(solution)/shard_map/all_gather | solution.py:1101
  181.8 413.0 %all-gather.7.cloned.1.call-start = ((), (), s32[]{:S(2)}) async-start(), calls=%async_computation.5 | async-start | bytes 12976128 | tf_op jit(solution)/shard_map/all_gather | solution.py:1154
  199.3 20.5 %collective-permute-start = (bf16[3,2,136,256]{3,2,1,0:T(8,128)(2,1)}, bf16[3,2,136,256]{3,2,1,0:T(8,128)(2,1)S(1)}, u32[]{:S(2)}, u32[]{:S(2)}) collective-permute-start(bf16[3,2,136,256]{3,2,1,0:T(8,128)(2,1)} %shard_map.258), channel_id=1, source_target_pairs={{0,4},{8,12},{16,20},{24,28},{4,18},{12,26},{20,2},{28,10},{18,22}... | collective-permute-start | bytes 1253384 | tf_op jit(solution)/shard_map/ppermute | solution.py:855
  200.6 37.1 %collective-permute-start.1 = (bf16[3,2,136,256]{3,2,1,0:T(8,128)(2,1)}, bf16[3,2,136,256]{3,2,1,0:T(8,128)(2,1)S(1)}, u32[]{:S(2)}, u32[]{:S(2)}) collective-permute-start(bf16[3,2,136,256]{3,2,1,0:T(8,128)(2,1)} %shard_map.258), channel_id=1, source_target_pairs={{0,18},{8,26},{16,2},{24,10},{4,22},{12,30},{20,6},{28,14},{1,19},... | collective-permute-start | bytes 1253384 | tf_op jit(solution)/shard_map/ppermute | solution.py:855
  201.9 52.4 %collective-permute-start.2 = (bf16[3,2,136,256]{3,2,1,0:T(8,128)(2,1)}, bf16[3,2,136,256]{3,2,1,0:T(8,128)(2,1)S(1)}, u32[]{:S(2)}, u32[]{:S(2)}) collective-permute-start(bf16[3,2,136,256]{3,2,1,0:T(8,128)(2,1)} %shard_map.258), channel_id=1, source_target_pairs={{0,22},{8,30},{16,6},{24,14},{1,23},{9,31},{17,7},{25,15}} | collective-permute-start | bytes 1253384 | tf_op jit(solution)/shard_map/ppermute | solution.py:855
  219.8 34.5 %copy-start.43 = (bf16[3,2,136,256]{3,2,1,0:T(8,128)(2,1)}, bf16[3,2,136,256]{3,2,1,0:T(8,128)(2,1)S(1)}, u32[]{:S(2)}) copy-start(bf16[3,2,136,256]{3,2,1,0:T(8,128)(2,1)S(1)} %collective-permute-done.rest_0_) | copy-start | bytes 1253380
  237.7 16.6 %copy-start.44 = (bf16[3,2,136,256]{3,2,1,0:T(8,128)(2,1)}, bf16[3,2,136,256]{3,2,1,0:T(8,128)(2,1)S(1)}, u32[]{:S(2)}) copy-start(bf16[3,2,136,256]{3,2,1,0:T(8,128)(2,1)S(1)} %collective-permute-done.1.rest_1_) | copy-start | bytes 1253380
  437.3 274.5 %reduce-scatter.3.cloned.1.call-start = ((), (), s32[]{:S(2)}) async-start(), calls=%async_computation.2 | async-start | bytes 7864320 | tf_op jit(solution)/shard_map/reduce_scatter | solution.py:1168
  505.9 14.2 %slice-start.15 = ((s8[6291456]{0:T(1024)(128)(4,1)}), s8[4194304]{0:T(1024)(128)(4,1)S(1)}, s32[]{:S(2)}) async-start(s8[6291456]{0:T(1024)(128)(4,1)} %bitcast.265), calls=%async_computation.21 | async-start | bytes 8388608
  510.3 9.9 slice-start.16
  520.2 52.7 %collective-permute-start.8 = (bf16[704,2048]{1,0:T(8,128)(2,1)}, bf16[704,2048]{1,0:T(8,128)(2,1)}, u32[]{:S(2)}, u32[]{:S(2)}) collective-permute-start(bf16[704,2048]{1,0:T(8,128)(2,1)} %convolution_convert_fusion.1), channel_id=1, source_target_pairs={{0,8},{8,0},{1,9},{9,1},{2,10},{10,2},{3,11},{11,3},{4,12},{12,4},... | collective-permute-start | bytes 8650760 | tf_op jit(solution)/shard_map/ppermute | solution.py:839
  526.3 46.5 %collective-permute-start.7 = (bf16[704,2048]{1,0:T(8,128)(2,1)}, bf16[704,2048]{1,0:T(8,128)(2,1)}, u32[]{:S(2)}, u32[]{:S(2)}) collective-permute-start(bf16[704,2048]{1,0:T(8,128)(2,1)} %convolution_convert_fusion.2), channel_id=1, source_target_pairs={{0,8},{8,0},{1,9},{9,1},{2,10},{10,2},{3,11},{11,3},{4,12},{12,4},... | collective-permute-start | bytes 8650760 | tf_op jit(solution)/shard_map/ppermute | solution.py:839
  526.8 9.8 slice-start.13
  533.3 39.6 %collective-permute-start.6 = (bf16[704,2048]{1,0:T(8,128)(2,1)}, bf16[704,2048]{1,0:T(8,128)(2,1)}, u32[]{:S(2)}, u32[]{:S(2)}) collective-permute-start(bf16[704,2048]{1,0:T(8,128)(2,1)} %convolution_convert_fusion.3), channel_id=1, source_target_pairs={{0,8},{8,0},{1,9},{9,1},{2,10},{10,2},{3,11},{11,3},{4,12},{12,4},... | collective-permute-start | bytes 8650760 | tf_op jit(solution)/shard_map/ppermute | solution.py:839
  534.7 38.2 %collective-permute-start.4 = (bf16[192,2048]{1,0:T(8,128)(2,1)}, bf16[192,2048]{1,0:T(8,128)(2,1)S(1)}, u32[]{:S(2)}, u32[]{:S(2)}) collective-permute-start(bf16[192,2048]{1,0:T(8,128)(2,1)} %get-tuple-element.163), channel_id=1, source_target_pairs={{0,1},{1,0},{2,3},{3,2},{4,5},{5,4},{6,7},{7,6},{8,9},{9,8},{10,11... | collective-permute-start | bytes 2359304 | tf_op jit(solution)/shard_map/ppermute | solution.py:839
  535.4 37.5 %collective-permute-start.5 = (bf16[192,2048]{1,0:T(8,128)(2,1)}, bf16[192,2048]{1,0:T(8,128)(2,1)S(1)}, u32[]{:S(2)}, u32[]{:S(2)}) collective-permute-start(bf16[192,2048]{1,0:T(8,128)(2,1)} %get-tuple-element.162), channel_id=1, source_target_pairs={{0,16},{16,0},{1,17},{17,1},{2,18},{18,2},{3,19},{19,3},{4,20},{20... | collective-permute-start | bytes 2359304 | tf_op jit(solution)/shard_map/ppermute | solution.py:839
  543.2 13.0 %slice-start = ((s8[4718592]{0:T(1024)(128)(4,1)}), s8[4194304]{0:T(1024)(128)(4,1)S(1)}, s32[]{:S(2)}) async-start(s8[4718592]{0:T(1024)(128)(4,1)} %bitcast.208), calls=%async_computation.6 | async-start | bytes 8388608
  574.9 19.4 %collective-permute-start.10 = (bf16[192,2048]{1,0:T(8,128)(2,1)S(1)}, bf16[192,2048]{1,0:T(8,128)(2,1)S(1)}, u32[]{:S(2)}, u32[]{:S(2)}) collective-permute-start(bf16[192,2048]{1,0:T(8,128)(2,1)S(1)} %get-tuple-element.164), channel_id=1, source_target_pairs={{0,1},{1,0},{2,3},{3,2},{4,5},{5,4},{6,7},{7,6},{8,9},{9,8},{10,11... | collective-permute-start | bytes 2359304 | tf_op jit(solution)/shard_map/ppermute | solution.py:839
  575.7 19.1 %collective-permute-start.9 = (bf16[192,2048]{1,0:T(8,128)(2,1)S(1)}, bf16[192,2048]{1,0:T(8,128)(2,1)S(1)}, u32[]{:S(2)}, u32[]{:S(2)}) collective-permute-start(bf16[192,2048]{1,0:T(8,128)(2,1)S(1)} %get-tuple-element.165), channel_id=1, source_target_pairs={{0,16},{16,0},{1,17},{17,1},{2,18},{18,2},{3,19},{19,3},{4,20},{20... | collective-permute-start | bytes 2359304 | tf_op jit(solution)/shard_map/ppermute | solution.py:839
  577.0 11.1 %slice-start.9 = ((s8[5767168]{0:T(1024)(128)(4,1)}), s8[4194304]{0:T(1024)(128)(4,1)S(1)}, s32[]{:S(2)}) async-start(s8[5767168]{0:T(1024)(128)(4,1)} %bitcast.237), calls=%async_computation.15 | async-start | bytes 8388608
  594.8 344.2 %reduce-scatter.5.cloned.1.call-start = ((), (), s32[]{:S(2)}) async-start(), calls=%async_computation.3 | async-start | bytes 10813440 | tf_op jit(solution)/shard_map/reduce_scatter | solution.py:1172
  594.8 18.4 %collective-permute-start.11 = (bf16[192,2048]{1,0:T(8,128)(2,1)S(1)}, bf16[192,2048]{1,0:T(8,128)(2,1)}, u32[]{:S(2)}, u32[]{:S(2)}) collective-permute-start(bf16[192,2048]{1,0:T(8,128)(2,1)S(1)} %get-tuple-element.161), channel_id=1, source_target_pairs={{0,16},{16,0},{1,17},{17,1},{2,18},{18,2},{3,19},{19,3},{4,20},{20... | collective-permute-start | bytes 2359304 | tf_op jit(solution)/shard_map/ppermute | solution.py:839
  596.3 19.4 %collective-permute-start.3 = (bf16[192,2048]{1,0:T(8,128)(2,1)S(1)}, bf16[192,2048]{1,0:T(8,128)(2,1)}, u32[]{:S(2)}, u32[]{:S(2)}) collective-permute-start(bf16[192,2048]{1,0:T(8,128)(2,1)S(1)} %get-tuple-element.160), channel_id=1, source_target_pairs={{0,1},{1,0},{2,3},{3,2},{4,5},{5,4},{6,7},{7,6},{8,9},{9,8},{10,11... | collective-permute-start | bytes 2359304 | tf_op jit(solution)/shard_map/ppermute | solution.py:839
  712.1 13.4 %copy-start.42 = (bf16[384,2048]{1,0:T(8,128)(2,1)S(1)}, bf16[384,2048]{1,0:T(8,128)(2,1)}, u32[]{:S(2)}) copy-start(bf16[384,2048]{1,0:T(8,128)(2,1)} %get-tuple-element.68) | copy-start | bytes 4718596
  718.0 7.5 collective-permute-start.15
  751.3 45.1 %collective-permute-start.12 = (bf16[3,2,136,256]{3,2,1,0:T(8,128)(2,1)}, bf16[3,2,136,256]{3,2,1,0:T(8,128)(2,1)S(1)}, u32[]{:S(2)}, u32[]{:S(2)}) collective-permute-start(bf16[3,2,136,256]{3,2,1,0:T(8,128)(2,1)} %get-tuple-element.101), channel_id=1, source_target_pairs={{4,0},{12,8},{20,16},{28,24},{18,4},{26,12},{2,20},{10,28},{22,18}... | collective-permute-start | bytes 1253384 | tf_op jit(solution)/shard_map/ppermute | solution.py:855
  752.6 46.6 %collective-permute-start.13 = (bf16[3,2,136,256]{3,2,1,0:T(8,128)(2,1)}, bf16[3,2,136,256]{3,2,1,0:T(8,128)(2,1)S(1)}, u32[]{:S(2)}, u32[]{:S(2)}) collective-permute-start(bf16[3,2,136,256]{3,2,1,0:T(8,128)(2,1)} %get-tuple-element.101), channel_id=1, source_target_pairs={{18,0},{26,8},{2,16},{10,24},{22,4},{30,12},{6,20},{14,28},{19,1},... | collective-permute-start | bytes 1253384 | tf_op jit(solution)/shard_map/ppermute | solution.py:855
  753.9 68.3 %collective-permute-start.14 = (bf16[3,2,136,256]{3,2,1,0:T(8,128)(2,1)}, bf16[3,2,136,256]{3,2,1,0:T(8,128)(2,1)S(1)}, u32[]{:S(2)}, u32[]{:S(2)}) collective-permute-start(bf16[3,2,136,256]{3,2,1,0:T(8,128)(2,1)} %get-tuple-element.101), channel_id=1, source_target_pairs={{22,0},{30,8},{6,16},{14,24},{23,1},{31,9},{7,17},{15,25}} | collective-permute-start | bytes 1253384 | tf_op jit(solution)/shard_map/ppermute | solution.py:855
  755.6 22.6 %copy-start.5 = (f32[3,128,2048]{2,1,0:T(8,128)S(1)}, f32[3,128,2048]{2,1,0:T(8,128)}, u32[]{:S(2)}) copy-start(f32[3,128,2048]{2,1,0:T(8,128)} %copy-done.3) | copy-start | bytes 9437188
  755.6 22.6 %copy-start.25 = (bf16[384,2048]{1,0:T(8,128)(2,1)S(1)}, bf16[384,2048]{1,0:T(8,128)(2,1)}, u32[]{:S(2)}) copy-start(bf16[384,2048]{1,0:T(8,128)(2,1)} %reduce-scatter.3.cloned.1.call-done) | copy-start | bytes 4718596
  796.4 25.8 %copy-start.28 = (bf16[3,2,136,256]{3,2,1,0:T(8,128)(2,1)}, bf16[3,2,136,256]{3,2,1,0:T(8,128)(2,1)S(1)}, u32[]{:S(2)}) copy-start(bf16[3,2,136,256]{3,2,1,0:T(8,128)(2,1)S(1)} %collective-permute-done.12.rest_0_) | copy-start | bytes 1253380
  799.2 23.0 %copy-start.29 = (bf16[3,2,136,256]{3,2,1,0:T(8,128)(2,1)}, bf16[3,2,136,256]{3,2,1,0:T(8,128)(2,1)S(1)}, u32[]{:S(2)}) copy-start(bf16[3,2,136,256]{3,2,1,0:T(8,128)(2,1)S(1)} %collective-permute-done.13.rest_1_) | copy-start | bytes 1253380
  (51 other events, 206.4 us)
Sparse Core Ops, SparseCore 0:
  181.9 199.1 all-gather.4
  437.4 105.5 all-gather.6
  594.9 116.8 reduce-scatter.2
  714.1 223.5 reduce-scatter.4

commit v6 on v5

--- a/solution.py
+++ b/solution.py
@@ -14,6 +14,7 @@
 ROOT_HALF = 0.7071067811865476
 TILE = 256
 AUX = 136
+MOST = 1536
 BF = jnp.bfloat16
 F32 = jnp.float32
 MESH_ID = pl.DeviceIdType.MESH
@@ -64,9 +65,13 @@
     return found
 
 
+def chain_reach(blocks, length):
+    return min(blocks - 1, (MOST - 2) // length + 1)
+
+
 def chain_weights(lens, row, docs, block, blocks, length, backward):
     out, alive = [], None
-    for k in range(1, blocks):
+    for k in range(1, chain_reach(blocks, length) + 1):
         source = block + k if backward else block - k
         inside = (source < blocks) if backward else (source >= 0)
         here = inside if alive is None else jnp.logical_and(alive, inside)
@@ -168,7 +173,7 @@
 
 
 def attend_kernel(nh, vd, docs, blocks, lens, meta, x_ref, num, den, pa, pb, rows, *rest):
-    sts, (att_out, den_out, st_out) = rest[: blocks - 1], rest[blocks - 1 :]
+    sts, (att_out, den_out, st_out) = rest[:-3], rest[-3:]
     row = pl.program_id(0)
     x = flat(x_ref)
     length = x.shape[0]
@@ -267,7 +272,7 @@
 
 
 def back_key_kernel(nh, vd, docs, blocks, lens, meta, x_ref, gqk_ref, gv_ref, pa, pb, rows, *rest):
-    sts, (out,) = rest[: blocks - 1], rest[blocks - 1 :]
+    sts, out = rest[:-1], rest[-1]
     row = pl.program_id(0)
     x = flat(x_ref)
     length = x.shape[0]
@@ -844,10 +849,10 @@
     return (sy * 2 + sc) * size + ha
 
 
-def chain_pieces(x, backward):
+def chain_pieces(x, reach, backward):
     size, special = lax.axis_size("ha"), square()
     out = []
-    for k in range(1, size):
+    for k in range(1, reach + 1):
         perm = []
         for i in range(size - k):
             ends = (i + k, i) if backward else (i, i + k)
@@ -1111,7 +1116,7 @@
         [((rows_n, nh, AUX, TILE), BF, 0)],
         nh * rows_n * length * 256 * 256 * 4,
     )
-    earlier = chain_pieces(states, False)
+    earlier = chain_pieces(states, chain_reach(blocks, length), False)
     num, den = row_call(
         functools.partial(intra_kernel, nh, vd, docs),
         rows_n,
@@ -1184,7 +1189,7 @@
         [((rows_n, length, nh * 256), BF, 0), ((rows_n, nh, AUX, TILE), BF, 0)],
         nh * rows_n * length * 256 * 256 * 4,
     )
-    later = chain_pieces(grad_states, True)
+    later = chain_pieces(grad_states, chain_reach(blocks, length), True)
     gqk, gv = row_call(
         functools.partial(back_intra_kernel, nh, vd, docs),
         rows_n,

time: 1070 us -> 1040 us (0.972)
  waiting for transfers between devices: 155 us -> 132 us
    ppermute x6 -> x4, waiting for transfers between devices: 80.3 us -> 38.4 us  [chain_pieces(): out.append(lax.ppermute(x, SEQ + ('ha',), perm))]
    reduce_scatter x1, waiting for transfers between devices: 0.01 us -> 13.3 us  [on_device(): ff_grads = lax.psum_scatter(ff_grads, 'ha', scatter_dimension=0, tiled=True)]
    unnamed x128 -> x124, local copies, waits for them, and re-layouts: 24.1 us -> 24.7 us
  transfers between devices with their start and end apart: 20 -> 18, of which waited for: 13 -> 12; matrix products, arithmetic and copies ran while one was open for 14% -> 14% of each run, Pallas kernels for 34% -> 35%
where the time goes in v6:
time: 1040 us
  Pallas kernels  671 us (65%)
  waiting for transfers between devices  132 us (13%)
  matrix products  91.6 us (9%)
  other arithmetic  61.2 us (6%)
  local copies, waits for them, and re-layouts  53.1 us (5%)
  between operations  14.8 us (1%)
  starting transfers between devices  13.1 us (1%)
    pallas_call x3, Pallas kernels, exchange(): pl.pallas_call(functools.partial(exchange_kernel, to_blocks, width, last_...  217 us
    pallas_call x1, Pallas kernels, start(): pl.pallas_call(functools.partial(start_kernel, parts, live), out_shape=[j...  159 us
    pallas_call x1, Pallas kernels, send_home(): pl.pallas_call(home_kernel, out_shape=[jax.ShapeDtypeStruct(v.shape, v.dt...  84.9 us
    dot_general x17, matrix products, dot(): return lax.dot_general(a, b, dims, preferred_element_type=F32)  80.4 us
    pallas_call x1, Pallas kernels, ff_pass(): pl.pallas_call(ff_kernel, out_shape=(keep, keep, keep, jax.ShapeDtypeStru...  68.3 us
    pallas_call x6, Pallas kernels, row_call(): pl.pallas_call(kernel, out_shape=tuple((jax.ShapeDtypeStruct(s, t) for s,...  67.7 us
    pallas_call x1, Pallas kernels, gather_near(): pl.pallas_call(functools.partial(near_kernel, rows), out_shape=[jax.Shape...  58.9 us
    all_gather x1, waiting for transfers between devices, on_device(): fetched = lax.all_gather(to_fetch, 'ha', axis=0)  39.4 us
  transfers between devices with their start and end apart: 18, of which 12 were waited for; matrix products, arithmetic and copies ran while one was open for 14% of the time, Pallas kernels for 35%

profile of v6, /device:TPU:0, one launch (start us, length us, event | category | flops | bytes accessed | tf_op | source)
XLA Modules:
  0.0 1036.6 jit_solution(8698081425041688609)
XLA Ops:
  22.3 159.5 %shard_map.256 = (bf16[8,3,128,2048]{3,2,1,0:T(8,128)(2,1)}, bf16[384,2048]{1,0:T(8,128)(2,1)}, bf16[8,256,1024]{2,1,0:T(8,128)(2,1)}) custom-call(bf16[3,128,2048]{2,1,0:T(8,128)(2,1)} %fusion.5.src, bf16[384,2048]{1,0:T(8,128)(2,1)} %maximum_maximum_fusion.w_in, bf16[256,1024]{1,0:T(8,128)(2,1)} %constant_dynamic-slice_fusion.9.w_out), custom_call_target="tpu_custom_call" | custom-call | bytes 314572800 | tf_op jit(solution)/shard_map/pallas_call | solution.py:822
  181.9 11.2 %convolution_convert_fusion.4.x_ref = bf16[8,3,128,384]{3,2,1,0:T(8,128)(2,1)} fusion(bf16[8,3,128,2048]{3,2,1,0:T(8,128)(2,1)} %get-tuple-element.62, bf16[384,2048]{1,0:T(8,128)(2,1)} %get-tuple-element.63), kind=kOutput, calls=%fused_computation.44 | convolution fusion | flops 4833017856 | bytes 16515072 | tf_op jit(solution)/shard_map/grtd,cd->grtc/dot_general | solution.py:1109
  193.1 6.2 shard_map.258
  204.2 10.8 %shard_map.257 = (f32[3,1024,256]{2,1,0:T(8,128)}, f32[3,1024,128]{2,1,0:T(8,128)}) custom-call(s32[3,8]{1,0:T(4,128)} %lens.11, s32[1]{0:T(128)} %bitcast.1.meta, bf16[8,3,128,384]{3,2,1,0:T(8,128)(2,1)} %convolution_convert_fusion.4.x_ref, bf16[8,128,128]{2,1,0:T(8,128)(2,1)} %constant.89.clone.align), custom_call_target="tpu_custom_call" | custom-call | flops 6442450944 | bytes 7340032 | tf_op jit(solution)/shard_map/pallas_call | solution.py:309
  215.0 4.8 collective-permute-done.rest_0_
  219.8 16.6 %collective-permute-done.1.rest_1_ = bf16[3,2,136,256]{3,2,1,0:T(8,128)(2,1)S(1)} collective-permute-done((bf16[3,2,136,256]{3,2,1,0:T(8,128)(2,1)}, bf16[3,2,136,256]{3,2,1,0:T(8,128)(2,1)S(1)}, u32[]{:S(2)}, u32[]{:S(2)}) %collective-permute-start.1) | collective-permute-done | bytes 417824 | tf_op jit(solution)/shard_map/ppermute | solution.py:860
  237.2 9.0 shard_map.259
  246.2 75.3 %shard_map.260 = (bf16[384,2048]{1,0:T(8,128)(2,1)}, bf16[4,384,2048]{2,1,0:T(8,128)(2,1)}, bf16[8,256,1024]{2,1,0:T(8,128)(2,1)}) custom-call(bf16[8,384,256]{2,1,0:T(8,128)(2,1)} %bitcast.227, bf16[384,2048]{1,0:T(8,128)(2,1)} %bitcast.226, bf16[8,256,1024]{2,1,0:T(8,128)(2,1)} %get-tuple-element.67.refs_1_), custom_call_target="tpu_custom_call" | custom-call | bytes 393216000 | tf_op jit(solution)/shard_map/pallas_call | solution.py:493
  332.8 39.4 %all-gather.5.cloned.1.call-done = bf16[2112,2048]{1,0:T(8,128)(2,1)} async-done(((bf16[528,2048]{1,0:T(8,128)(2,1)}), bf16[2112,2048]{1,0:T(8,128)(2,1)}) %all-gather.5.cloned.1.call-update) | async-done | bytes 8650768 | tf_op jit(solution)/shard_map/all_gather | solution.py:1106
  372.2 58.9 %shard_map.261 = (bf16[4,384,2048]{2,1,0:T(8,128)(2,1)}, bf16[4,528,2048]{2,1,0:T(8,128)(2,1)}) custom-call(bf16[384,2048]{1,0:T(8,128)(2,1)} %bitcast.229, bf16[4,528,2048]{2,1,0:T(8,128)(2,1)} %bitcast.220), custom_call_target="tpu_custom_call" | custom-call | bytes 157286400 | tf_op jit(solution)/shard_map/pallas_call | solution.py:649
  431.5 68.3 %shard_map.262 = (bf16[2,4,384,704]{3,2,1,0:T(8,128)(2,1)}, bf16[2,4,384,704]{3,2,1,0:T(8,128)(2,1)}, bf16[2,4,384,704]{3,2,1,0:T(8,128)(2,1)}, bf16[4,384,2048]{2,1,0:T(8,128)(2,1)}) custom-call(bf16[4,384,2048]{2,1,0:T(8,128)(2,1)} %get-tuple-element.72.n2, bf16[4,384,2048]{2,1,0:T(8,128)(2,1)} %get-tuple-element.73.cot, bf16[4,528,2048]{2,1,0:T(8,128)(2,1)} %bitcast.221, ...), custom_call_target="tpu_custom_call" | custom-call | flops 44291850240 | bytes 42467328 | tf_op jit(solution)/shard_map/pallas_call | solution.py:945
  504.2 9.9 convolution_convert_fusion.1
  514.1 6.1 convolution_convert_fusion.2
  521.1 6.1 convolution_convert_fusion.3
  530.6 6.5 fusion.47
  537.1 6.4 fusion.46
  543.6 6.6 fusion.45
  550.2 14.0 %shard_map.263 = bf16[1536,2048]{1,0:T(8,128)(2,1)S(1)} custom-call(s32[4]{0:T(128)S(1)} %pad_add_fusion.order, bf16[2,4,384,704]{3,2,1,0:T(8,128)(2,1)S(1)} %bitcast.209, bf16[4,528,2048]{2,1,0:T(8,128)(2,1)} %bitcast.222, bf16[4,528,2048]{2,1,0:T(8,128)(2,1)} %get-tuple-element.74.theirs), custom_call_target="tpu_custom_call" | custom-call | flops 8858370048 | bytes 17301504 | tf_op jit(solution)/shard_map/pallas_call | solution.py:974
  570.9 6.7 add_convert_fusion.1
  590.9 21.1 %collective-permute-done.10 = bf16[192,2048]{1,0:T(8,128)(2,1)} collective-permute-done((bf16[192,2048]{1,0:T(8,128)(2,1)S(1)}, bf16[192,2048]{1,0:T(8,128)(2,1)}, u32[]{:S(2)}, u32[]{:S(2)}) %collective-permute-start.10) | collective-permute-done | bytes 786464 | tf_op jit(solution)/shard_map/ppermute | solution.py:844
  635.4 58.1 %shard_map.264 = bf16[8,384,256]{2,1,0:T(8,128)(2,1)} custom-call(bf16[384,2048]{1,0:T(8,128)(2,1)} %add_convert_fusion.4.src), custom_call_target="tpu_custom_call" | custom-call | bytes 393216000 | tf_op jit(solution)/shard_map/pallas_call | solution.py:493
  693.5 8.0 reduce-scatter.3.cloned.1.call-done
  701.8 5.9 convolution_convert_fusion
  707.8 7.3 collective-permute-done.13
  731.4 9.5 shard_map.265
  744.0 22.6 %shard_map.266 = (f32[3,1024,128]{2,1,0:T(8,128)}, f32[3,1024,256]{2,1,0:T(8,128)}) custom-call(s32[3,8]{1,0:T(4,128)} %lens.11, s32[1]{0:T(128)} %bitcast.1.meta, bf16[8,3,128,384]{3,2,1,0:T(8,128)(2,1)} %convolution_convert_fusion.4.x_ref, bf16[3,1024,512]{2,1,0:T(8,128)(2,1)} %get-tuple-element.97.gn_ref, ...), custom_call_target="tpu_custom_call" | custom-call | flops 12884901888 | bytes 11436032 | tf_op jit(solution)/shard_map/pallas_call | solution.py:309
  768.3 15.1 %collective-permute-done.11.rest_0_ = bf16[3,2,136,256]{3,2,1,0:T(8,128)(2,1)S(1)} collective-permute-done((bf16[3,2,136,256]{3,2,1,0:T(8,128)(2,1)}, bf16[3,2,136,256]{3,2,1,0:T(8,128)(2,1)S(1)}, u32[]{:S(2)}, u32[]{:S(2)}) %collective-permute-start.11) | collective-permute-done | bytes 417824 | tf_op jit(solution)/shard_map/ppermute | solution.py:860
  786.0 9.5 shard_map.267
  795.5 84.0 %shard_map.268 = (bf16[384,3072]{1,0:T(8,128)(2,1)}, bf16[3,1024,512]{2,1,0:T(8,128)(2,1)}, bf16[2,512,512]{2,1,0:T(8,128)(2,1)}) custom-call(bf16[8,384,384]{2,1,0:T(8,128)(2,1)} %bitcast.219, bf16[4,1024,512]{2,1,0:T(8,128)(2,1)} %pad_maximum_fusion.2.refs_0_), custom_call_target="tpu_custom_call" | custom-call | bytes 589824000 | tf_op jit(solution)/shard_map/pallas_call | solution.py:493
  892.2 8.8 convolution_bitcast_fusion
  908.0 13.3 %reduce-scatter.5.cloned.1.call-done = bf16[176,6144]{1,0:T(8,128)(2,1)} async-done(((bf16[704,6144]{1,0:T(8,128)(2,1)}), bf16[176,6144]{1,0:T(8,128)(2,1)}) %reduce-scatter.5.cloned.1.call-update) | async-done | bytes 2162704 | tf_op jit(solution)/shard_map/reduce_scatter | solution.py:1177
  927.7 84.9 %shard_map.269 = (f32[32,8,128]{2,1,0:T(8,128)}, bf16[4,320,512]{2,1,0:T(8,128)(2,1)}, bf16[4,528,512]{2,1,0:T(8,128)(2,1)}, bf16[4,256,512]{2,1,0:T(8,128)(2,1)}) custom-call(f32[32,8,128]{2,1,0:T(8,128)} %pad.4.refs_0_, bf16[4,320,512]{2,1,0:T(8,128)(2,1)} %bitcast.240, bf16[4,528,512]{2,1,0:T(8,128)(2,1)} %bitcast.223, bf16[4,256,512]{2,1,0:T(8,128)(2,1)} %bitcast.246), custom_call_target="tpu_custom_call" | custom-call | bytes 100000000 | tf_op jit(solution)/shard_map/pallas_call | solution.py:596
  (240 shorter events, 151.1 us)
Async XLA Ops:
  7.2 8.8 copy-start
  7.2 365.0 %all-gather.5.cloned.1.call-start = ((), (), s32[]{:S(2)}) async-start(), calls=%async_computation.4 | async-start | bytes 10813440 | tf_op jit(solution)/shard_map/all_gather | solution.py:1106
  9.1 7.7 copy-start.35
  181.8 407.0 %all-gather.7.cloned.1.call-start = ((), (), s32[]{:S(2)}) async-start(), calls=%async_computation.5 | async-start | bytes 12976128 | tf_op jit(solution)/shard_map/all_gather | solution.py:1159
  199.3 20.5 %collective-permute-start = (bf16[3,2,136,256]{3,2,1,0:T(8,128)(2,1)}, bf16[3,2,136,256]{3,2,1,0:T(8,128)(2,1)S(1)}, u32[]{:S(2)}, u32[]{:S(2)}) collective-permute-start(bf16[3,2,136,256]{3,2,1,0:T(8,128)(2,1)} %shard_map.258), channel_id=1, source_target_pairs={{0,4},{8,12},{16,20},{24,28},{4,18},{12,26},{20,2},{28,10},{18,22}... | collective-permute-start | bytes 1253384 | tf_op jit(solution)/shard_map/ppermute | solution.py:860
  200.6 35.8 %collective-permute-start.1 = (bf16[3,2,136,256]{3,2,1,0:T(8,128)(2,1)}, bf16[3,2,136,256]{3,2,1,0:T(8,128)(2,1)S(1)}, u32[]{:S(2)}, u32[]{:S(2)}) collective-permute-start(bf16[3,2,136,256]{3,2,1,0:T(8,128)(2,1)} %shard_map.258), channel_id=1, source_target_pairs={{0,18},{8,26},{16,2},{24,10},{4,22},{12,30},{20,6},{28,14},{1,19},... | collective-permute-start | bytes 1253384 | tf_op jit(solution)/shard_map/ppermute | solution.py:860
  219.8 16.6 %copy-start.42 = (bf16[3,2,136,256]{3,2,1,0:T(8,128)(2,1)}, bf16[3,2,136,256]{3,2,1,0:T(8,128)(2,1)S(1)}, u32[]{:S(2)}) copy-start(bf16[3,2,136,256]{3,2,1,0:T(8,128)(2,1)S(1)} %collective-permute-done.rest_0_) | copy-start | bytes 1253380
  431.2 270.4 %reduce-scatter.3.cloned.1.call-start = ((), (), s32[]{:S(2)}) async-start(), calls=%async_computation.2 | async-start | bytes 7864320 | tf_op jit(solution)/shard_map/reduce_scatter | solution.py:1173
  499.8 14.2 %slice-start.15 = ((s8[6291456]{0:T(1024)(128)(4,1)}), s8[4194304]{0:T(1024)(128)(4,1)S(1)}, s32[]{:S(2)}) async-start(s8[6291456]{0:T(1024)(128)(4,1)} %bitcast.265), calls=%async_computation.21 | async-start | bytes 8388608
  504.1 9.9 slice-start.16
  514.1 52.7 %collective-permute-start.7 = (bf16[704,2048]{1,0:T(8,128)(2,1)}, bf16[704,2048]{1,0:T(8,128)(2,1)}, u32[]{:S(2)}, u32[]{:S(2)}) collective-permute-start(bf16[704,2048]{1,0:T(8,128)(2,1)} %convolution_convert_fusion.1), channel_id=1, source_target_pairs={{0,8},{8,0},{1,9},{9,1},{2,10},{10,2},{3,11},{11,3},{4,12},{12,4},... | collective-permute-start | bytes 8650760 | tf_op jit(solution)/shard_map/ppermute | solution.py:844
  520.2 46.6 %collective-permute-start.6 = (bf16[704,2048]{1,0:T(8,128)(2,1)}, bf16[704,2048]{1,0:T(8,128)(2,1)}, u32[]{:S(2)}, u32[]{:S(2)}) collective-permute-start(bf16[704,2048]{1,0:T(8,128)(2,1)} %convolution_convert_fusion.2), channel_id=1, source_target_pairs={{0,8},{8,0},{1,9},{9,1},{2,10},{10,2},{3,11},{11,3},{4,12},{12,4},... | collective-permute-start | bytes 8650760 | tf_op jit(solution)/shard_map/ppermute | solution.py:844
  520.7 9.9 slice-start.13
  521.1 9.5 slice-start.14
  527.1 39.7 %collective-permute-start.5 = (bf16[704,2048]{1,0:T(8,128)(2,1)}, bf16[704,2048]{1,0:T(8,128)(2,1)}, u32[]{:S(2)}, u32[]{:S(2)}) collective-permute-start(bf16[704,2048]{1,0:T(8,128)(2,1)} %convolution_convert_fusion.3), channel_id=1, source_target_pairs={{0,8},{8,0},{1,9},{9,1},{2,10},{10,2},{3,11},{11,3},{4,12},{12,4},... | collective-permute-start | bytes 8650760 | tf_op jit(solution)/shard_map/ppermute | solution.py:844
  528.6 38.2 %collective-permute-start.3 = (bf16[192,2048]{1,0:T(8,128)(2,1)}, bf16[192,2048]{1,0:T(8,128)(2,1)S(1)}, u32[]{:S(2)}, u32[]{:S(2)}) collective-permute-start(bf16[192,2048]{1,0:T(8,128)(2,1)} %get-tuple-element.163), channel_id=1, source_target_pairs={{0,1},{1,0},{2,3},{3,2},{4,5},{5,4},{6,7},{7,6},{8,9},{9,8},{10,11... | collective-permute-start | bytes 2359304 | tf_op jit(solution)/shard_map/ppermute | solution.py:844
  529.4 37.4 %collective-permute-start.4 = (bf16[192,2048]{1,0:T(8,128)(2,1)}, bf16[192,2048]{1,0:T(8,128)(2,1)S(1)}, u32[]{:S(2)}, u32[]{:S(2)}) collective-permute-start(bf16[192,2048]{1,0:T(8,128)(2,1)} %get-tuple-element.162), channel_id=1, source_target_pairs={{0,16},{16,0},{1,17},{17,1},{2,18},{18,2},{3,19},{19,3},{4,20},{20... | collective-permute-start | bytes 2359304 | tf_op jit(solution)/shard_map/ppermute | solution.py:844
  537.1 13.1 %slice-start = ((s8[4718592]{0:T(1024)(128)(4,1)}), s8[4194304]{0:T(1024)(128)(4,1)S(1)}, s32[]{:S(2)}) async-start(s8[4718592]{0:T(1024)(128)(4,1)} %bitcast.208), calls=%async_computation.6 | async-start | bytes 8388608
  568.8 19.5 %collective-permute-start.8 = (bf16[192,2048]{1,0:T(8,128)(2,1)S(1)}, bf16[192,2048]{1,0:T(8,128)(2,1)S(1)}, u32[]{:S(2)}, u32[]{:S(2)}) collective-permute-start(bf16[192,2048]{1,0:T(8,128)(2,1)S(1)} %get-tuple-element.165), channel_id=1, source_target_pairs={{0,16},{16,0},{1,17},{17,1},{2,18},{18,2},{3,19},{19,3},{4,20},{20... | collective-permute-start | bytes 2359304 | tf_op jit(solution)/shard_map/ppermute | solution.py:844
  569.7 7.9 slice-start.7
  569.7 7.9 slice-start.8
  569.7 19.1 %collective-permute-start.9 = (bf16[192,2048]{1,0:T(8,128)(2,1)S(1)}, bf16[192,2048]{1,0:T(8,128)(2,1)S(1)}, u32[]{:S(2)}, u32[]{:S(2)}) collective-permute-start(bf16[192,2048]{1,0:T(8,128)(2,1)S(1)} %get-tuple-element.164), channel_id=1, source_target_pairs={{0,1},{1,0},{2,3},{3,2},{4,5},{5,4},{6,7},{7,6},{8,9},{9,8},{10,11... | collective-permute-start | bytes 2359304 | tf_op jit(solution)/shard_map/ppermute | solution.py:844
  570.9 11.2 %slice-start.9 = ((s8[5767168]{0:T(1024)(128)(4,1)}), s8[4194304]{0:T(1024)(128)(4,1)S(1)}, s32[]{:S(2)}) async-start(s8[5767168]{0:T(1024)(128)(4,1)} %bitcast.237), calls=%async_computation.15 | async-start | bytes 8388608
  588.8 332.4 %reduce-scatter.5.cloned.1.call-start = ((), (), s32[]{:S(2)}) async-start(), calls=%async_computation.3 | async-start | bytes 10813440 | tf_op jit(solution)/shard_map/reduce_scatter | solution.py:1177
  588.9 23.2 %collective-permute-start.10 = (bf16[192,2048]{1,0:T(8,128)(2,1)S(1)}, bf16[192,2048]{1,0:T(8,128)(2,1)}, u32[]{:S(2)}, u32[]{:S(2)}) collective-permute-start(bf16[192,2048]{1,0:T(8,128)(2,1)S(1)} %get-tuple-element.161), channel_id=1, source_target_pairs={{0,16},{16,0},{1,17},{17,1},{2,18},{18,2},{3,19},{19,3},{4,20},{20... | collective-permute-start | bytes 2359304 | tf_op jit(solution)/shard_map/ppermute | solution.py:844
  590.2 24.1 %collective-permute-start.2 = (bf16[192,2048]{1,0:T(8,128)(2,1)S(1)}, bf16[192,2048]{1,0:T(8,128)(2,1)}, u32[]{:S(2)}, u32[]{:S(2)}) collective-permute-start(bf16[192,2048]{1,0:T(8,128)(2,1)S(1)} %get-tuple-element.160), channel_id=1, source_target_pairs={{0,1},{1,0},{2,3},{3,2},{4,5},{5,4},{6,7},{7,6},{8,9},{9,8},{10,11... | collective-permute-start | bytes 2359304 | tf_op jit(solution)/shard_map/ppermute | solution.py:844
  701.8 13.4 %copy-start.41 = (bf16[384,2048]{1,0:T(8,128)(2,1)S(1)}, bf16[384,2048]{1,0:T(8,128)(2,1)}, u32[]{:S(2)}) copy-start(bf16[384,2048]{1,0:T(8,128)(2,1)} %get-tuple-element.68) | copy-start | bytes 4718596
  707.7 7.5 collective-permute-start.13
  741.0 42.4 %collective-permute-start.11 = (bf16[3,2,136,256]{3,2,1,0:T(8,128)(2,1)}, bf16[3,2,136,256]{3,2,1,0:T(8,128)(2,1)S(1)}, u32[]{:S(2)}, u32[]{:S(2)}) collective-permute-start(bf16[3,2,136,256]{3,2,1,0:T(8,128)(2,1)} %get-tuple-element.101), channel_id=1, source_target_pairs={{4,0},{12,8},{20,16},{28,24},{18,4},{26,12},{2,20},{10,28},{22,18}... | collective-permute-start | bytes 1253384 | tf_op jit(solution)/shard_map/ppermute | solution.py:860
  742.3 43.0 %collective-permute-start.12 = (bf16[3,2,136,256]{3,2,1,0:T(8,128)(2,1)}, bf16[3,2,136,256]{3,2,1,0:T(8,128)(2,1)S(1)}, u32[]{:S(2)}, u32[]{:S(2)}) collective-permute-start(bf16[3,2,136,256]{3,2,1,0:T(8,128)(2,1)} %get-tuple-element.101), channel_id=1, source_target_pairs={{18,0},{26,8},{2,16},{10,24},{22,4},{30,12},{6,20},{14,28},{19,1},... | collective-permute-start | bytes 1253384 | tf_op jit(solution)/shard_map/ppermute | solution.py:860
  744.0 22.6 %copy-start.5 = (f32[3,128,2048]{2,1,0:T(8,128)S(1)}, f32[3,128,2048]{2,1,0:T(8,128)}, u32[]{:S(2)}) copy-start(f32[3,128,2048]{2,1,0:T(8,128)} %copy-done.3) | copy-start | bytes 9437188
  744.0 22.6 %copy-start.25 = (bf16[384,2048]{1,0:T(8,128)(2,1)S(1)}, bf16[384,2048]{1,0:T(8,128)(2,1)}, u32[]{:S(2)}) copy-start(bf16[384,2048]{1,0:T(8,128)(2,1)} %reduce-scatter.3.cloned.1.call-done) | copy-start | bytes 4718596
  (47 other events, 167.2 us)
Sparse Core Ops, SparseCore 0:
  181.9 190.2 all-gather.4
  431.3 103.7 all-gather.6
  589.0 112.5 reduce-scatter.2
  703.8 217.4 reduce-scatter.4
